TPU v7x, 32 devices: a whole 2x2x4 slice. The times are simulated.
32 devices in a mesh: groups: 2 (over y), depth: 16 (over z, x, core).
Axes of the slice: x: 2, y: 2, z: 4, core: 2. Of those that a mesh axis runs over, the one named last changes fastest.
Arguments:
- sources: float32 [2, 8, 8, 128], P(None, 'groups'), parts along dimension 1, may hold values from -6 to 6
- plan: int32 [8], P('groups'), parts along dimension 0, may hold values from 0 to 1023
- absorb: float32 [16, 16, 128], P('depth', 'groups'), parts along dimension 1, as said below
- labels: int32 [16, 16, 128], P('depth', 'groups'), parts along dimension 1, may hold values from 0 to 7
- region_kk: float32 [8], replicated, may hold values from 0.1 to 1
- damp_cells: int32 [256], P('groups'), parts along dimension 0, may hold values from 0 to 1023
- initial_guess: float32 [2, 8, 1024, 8, 128], P(None, 'groups', 'depth'), parts along dimension 1, may hold values from -3 to 3
Outputs:
- solution: float32 [2, 8, 1024, 8, 128], P(None, 'groups', 'depth'), parts along dimension 1
There are 2 independent parts, one for each index of `groups`. A program takes and returns all parts, laid end to end along the dimension named above; an argument that names none is the same for every part. Nothing has to cross between parts.
Inputs may be any that keep to these rules, and one draw needn't show every extreme that they name: `plan`: each source sits on one plane, counted over the whole depth. `damp_cells`: entries may repeat. `absorb`: every entry is positive.
All inputs are finite; a program needn't handle non-finite values.
Results may differ from a plain program's by a relative error of at most 0.0003.
Values sent between devices are 32-bit elements; how exact they have to be, the bound alone decides.
No kernel may reach another device: no remote copies, remote signals or barrier semaphores. Data moves between devices by JAX's collectives and lax.ppermute only.
A program may use at most 64 MiB of HBM per device.

v0:
```python
import jax
import jax.numpy as jnp
from jax import lax
from jax.sharding import PartitionSpec as P

SLAB = 64
STEPS = 2


relax_weight = 0.8
shift_ratio = 0.5
damping = 3.0
coupling = 0.25


def with_halo(block, sides, width):
    for axis, dim in sides:
        count = lax.axis_size(axis)
        forward = [(i, i + 1) for i in range(count - 1)]
        backward = [(target, source) for source, target in forward]
        low = lax.ppermute(
            lax.slice_in_dim(block, block.shape[dim] - width, None, axis=dim), axis, forward
        )
        high = lax.ppermute(lax.slice_in_dim(block, 0, width, axis=dim), axis, backward)
        block = jnp.concatenate([low, block, high], axis=dim)
    return block


def carried_in(part, axis, combine, identity, reverse):
    count = lax.axis_size(axis)
    place = lax.axis_index(axis)
    ahead = count - 1 - place if reverse else place
    gathered = jax.tree.map(lambda a: lax.all_gather(a, axis), part)
    state = jax.tree.map(lambda a, e: jnp.zeros_like(a) + jnp.asarray(e, a.dtype), part, identity)

    def one(turn, state):
        source = count - 1 - turn if reverse else turn
        return combine(
            state, jax.tree.map(lambda a: lax.dynamic_index_in_dim(a, source, 0, False), gathered)
        )

    return lax.fori_loop(0, ahead, one, state)


def complex_mul(left, right):
    return jnp.stack(
        [left[0] * right[0] - left[1] * right[1], left[0] * right[1] + left[1] * right[0]]
    )


def lateral_sum(field):
    widths = [(0, 0)] * (field.ndim - 2) + [(1, 1), (0, 0)]
    padded = jnp.pad(field, widths)
    total = padded[..., 2:, :] + padded[..., :-2, :]
    widths = [(0, 0)] * (field.ndim - 1) + [(1, 1)]
    padded = jnp.pad(field, widths)
    return total + padded[..., 2:] + padded[..., :-2]


def neighbours(extended):
    middle = extended[:, :, 1:-1]
    return extended[:, :, 2:] + extended[:, :, :-2] + lateral_sum(middle)


def link(earlier, later):
    return (complex_mul(later[0], earlier[0]), complex_mul(later[0], earlier[1]) + later[1])


def local(sources, plan, absorb, labels, region_kk, damp_cells, initial_guess):
    position = lax.axis_index("depth")
    height = labels.shape[1]
    breadth = labels.shape[2]
    regions = jnp.arange(region_kk.shape[0])
    squared = jnp.sum(jnp.where(labels[..., None] == regions, region_kk, 0.0), axis=-1)
    cells = jnp.arange(height * breadth)
    layer = (
        jnp.any(damp_cells[:, None] == cells[None, :], axis=0)
        .astype(jnp.float32)
        .reshape(height, breadth)
    )
    diagonal_real_part = 6.0 - squared
    imag_diag = shift_ratio * squared + damping * layer
    complex_magnitude = diagonal_real_part * diagonal_real_part + imag_diag * imag_diag
    inverse = jnp.stack([diagonal_real_part / complex_magnitude, -imag_diag / complex_magnitude])
    orders = jnp.arange(SLAB + 1).astype(jnp.float32)[:, None, None]
    magnitude = jnp.exp(-orders * absorb / SLAB)
    phase_angle_sum = orders * jnp.sqrt(squared)
    powers = jnp.stack([magnitude * jnp.cos(phase_angle_sum), magnitude * jnp.sin(phase_angle_sum)])
    passage = powers[:, SLAB]
    toward_next = powers[:, :SLAB][:, ::-1][:, None]
    toward_prev = powers[:, :SLAB][:, None]
    entry_next = powers[:, 1:][:, None]
    entry_prev = powers[:, 1:][:, ::-1][:, None]
    local_plane = plan - position * SLAB
    hits = (jnp.arange(SLAB)[None, :] == local_plane[:, None]).astype(jnp.float32)
    forcing = sources[:, :, None] * hits[None, :, :, None, None]
    solution = initial_guess
    around_inverse = with_halo(inverse, (("depth", 1),), 1)
    inverse_wide = jnp.concatenate(
        [
            jnp.broadcast_to(around_inverse[:, 0:1], (2, 2, height, breadth)),
            jnp.broadcast_to(inverse, (2, SLAB, height, breadth)),
            jnp.broadcast_to(around_inverse[:, 2:3], (2, 2, height, breadth)),
        ],
        axis=1,
    )[:, None]
    for turn in range(STEPS):
        extended = with_halo(solution, (("depth", 2),), 1)
        beside_all = neighbours(extended)
        applied = jnp.stack(
            [
                diagonal_real_part * solution[0] - beside_all[0] - damping * layer * solution[1],
                diagonal_real_part * solution[1] - beside_all[1] + damping * layer * solution[0],
            ]
        )
        residual = forcing - applied
        emit_next = jnp.sum(complex_mul(toward_next, residual), axis=2)
        emit_prev = jnp.sum(complex_mul(toward_prev, residual), axis=2)
        identity = (
            jnp.stack([jnp.ones_like(passage[0]), jnp.zeros_like(passage[0])]),
            jnp.zeros_like(emit_next),
        )
        incoming_next = carried_in((passage, emit_next), "depth", link, identity, False)[1]
        incoming_prev = carried_in((passage, emit_prev), "depth", link, identity, True)[1]
        corrected_field = residual + coupling * (
            complex_mul(entry_next, incoming_next[:, :, None])
            + complex_mul(entry_prev, incoming_prev[:, :, None])
        )
        wide = with_halo(corrected_field, (("depth", 2),), 2)
        update = relax_weight * complex_mul(inverse_wide, wide)
        for inner in range(2):
            padded = jnp.pad(update, ((0, 0), (0, 0), (1, 1), (0, 0), (0, 0)))
            update = (1.0 - relax_weight) * update + relax_weight * complex_mul(
                inverse_wide, wide + neighbours(padded)
            )
        update = update[:, :, 2:-2]
        solution = solution + update
    return solution


def solution(mesh):
    return jax.shard_map(
        local,
        mesh=mesh,
        in_specs=(
            P(None, "groups", None, None),
            P("groups"),
            P("depth", "groups", None),
            P("depth", "groups", None),
            P(),
            P("groups"),
            P(None, "groups", "depth", None, None),
        ),
        out_specs=P(None, "groups", "depth", None, None),
        check_vma=False,
    )
```

profile of v0, /device:TPU:25, one launch (start us, length us, event | category | flops | bytes accessed | tf_op | source)
XLA Modules:
  0.0 239.0 jit_solution(2938973607917760691)
XLA Ops:
  1.6 3.7 %collective-permute-start = (f32[2,1,8,128]{3,2,1,0:T(8,128)S(1)}, f32[2,1,8,128]{3,2,1,0:T(8,128)S(1)}, u32[]{:S(2)}, u32[]{:S(2)}) collective-permute-start(f32[2,1,8,128]{3,2,1,0:T(8,128)S(1)} %get-tuple-element.386), channel_id=1, source_target_pairs={{0,1},{1,2},{2,3},{3,4},{4,5},{5,6},{6,7},{7,8},{8,9},{9,10},{10,1... | collective-permute-start | bytes 24584 | tf_op jit(solution)/shard_map/ppermute | solution.py:21
  5.3 1.9 collective-permute-start.1
  7.2 1.4 fusion.59
  8.6 3.4 %collective-permute-start.2 = (f32[2,4,1,8,128]{4,3,2,1,0:T(8,128)}, f32[2,4,1,8,128]{4,3,2,1,0:T(8,128)S(1)}, u32[]{:S(2)}, u32[]{:S(2)}) collective-permute-start(f32[2,4,1,8,128]{4,3,2,1,0:T(8,128)} %get-tuple-element.355), channel_id=1, source_target_pairs={{1,0},{2,1},{3,2},{4,3},{5,4},{6,5},{7,6},{8,7},{9,8},{10,9},{11,1... | collective-permute-start | bytes 98312 | tf_op jit(solution)/shard_map/ppermute | solution.py:24
  12.1 2.1 collective-permute-start.3
  14.3 1.7 fusion.49
  20.0 17.8 %all-gather = f32[32,1,8,128]{3,2,1,0:T(8,128)} all-gather(f32[2,1,8,128]{3,2,1,0:T(8,128)S(1)} %pad_maximum_fusion.11), channel_id=2, replica_groups=mesh['groups'=2,'depth'=16] {'depth'}, dimensions={0}, use_global_device_ids=true | all-gather | bytes 139264 | tf_op jit(solution)/shard_map/all_gather | solution.py:33
  43.0 20.9 %all-gather.2 = f32[32,4,8,128]{3,2,1,0:T(8,128)} all-gather(f32[2,4,8,128]{3,2,1,0:T(8,128)S(1)} %maximum_reduce_fusion.1), channel_id=4, replica_groups=mesh['groups'=2,'depth'=16] {'depth'}, dimensions={0}, use_global_device_ids=true | all-gather | bytes 557056 | tf_op jit(solution)/shard_map/all_gather | solution.py:33
  63.9 2.9 %while.53 = (s32[]{:T(128)}, f32[2,4,8,128]{3,2,1,0:T(8,128)S(1)}, s32[]{:T(128)}, f32[16,2,8,128]{3,2,1,0:T(8,128)}, f32[16,2,4,8,128]{4,3,2,1,0:T(8,128)}, /*i...) while((s32[]{:T(128)}, f32[2,4,8,128]{3,2,1,0:T(8,128)S(1)}, s32[]{:T(128)}, ...), condition=%wide.region_7.8_spmd, body=%wide.region_6.7_spmd.sunk | while | flops 40967 | bytes 188587 | solution.py:42
  66.9 38.1 %all-gather.1 = f32[32,4,8,128]{3,2,1,0:T(8,128)S(1)} all-gather(f32[2,4,8,128]{3,2,1,0:T(8,128)S(1)} %maximum_reduce_fusion), channel_id=3, replica_groups=mesh['groups'=2,'depth'=16] {'depth'}, dimensions={0}, use_global_device_ids=true | all-gather | bytes 557056 | tf_op jit(solution)/shard_map/all_gather | solution.py:33
  105.0 9.7 %while.52 = (s32[]{:T(128)}, f32[2,4,8,128]{3,2,1,0:T(8,128)S(1)}, s32[]{:T(128)}, f32[16,2,8,128]{3,2,1,0:T(8,128)}, f32[16,2,4,8,128]{4,3,2,1,0:T(8,128)S(1)}, /*index=5*/s32[]{:T(128)}, s32[]{:T(128)}, s32[]{:T(128)}, s32[]{}) while((s32[]{:T(128)}, f32[2,4,8,128]{3,2,1,0:T(8,128)S(1)}, s32[]{:T(128)}, f32[16,2,8,128]{3,2,1,0:T(8,128)}, ...), condition=%wide.region_4.5_spmd, body=%wide.region_3.4_spmd.sunk | while | flops 40966 | bytes 188567 | solution.py:42
  114.7 1.3 multiply_subtract_fusion.16
  117.0 5.4 %collective-permute-start.4 = (f32[2,4,2,8,128]{4,3,2,1,0:T(8,128)S(1)}, f32[2,4,2,8,128]{4,3,2,1,0:T(8,128)S(1)}, u32[]{:S(2)}, u32[]{:S(2)}) collective-permute-start(f32[2,4,2,8,128]{4,3,2,1,0:T(8,128)S(1)} %get-tuple-element.351), channel_id=1, source_target_pairs={{0,1},{1,2},{2,3},{3,4},{4,5},{5,6},{6,7},{7,8},{8,9},{9,10},{10,1... | collective-permute-start | bytes 196616 | tf_op jit(solution)/shard_map/ppermute | solution.py:21
  122.4 1.9 collective-permute-start.5
  124.4 3.6 %collective-permute-done.5 = f32[2,4,2,8,128]{4,3,2,1,0:T(8,128)S(1)} collective-permute-done((f32[2,4,2,8,128]{4,3,2,1,0:T(8,128)S(1)}, f32[2,4,2,8,128]{4,3,2,1,0:T(8,128)S(1)}, u32[]{:S(2)}, u32[]{:S(2)}) %collective-permute-start.5) | collective-permute-done | bytes 65568 | tf_op jit(solution)/shard_map/ppermute | solution.py:24
  128.7 1.5 fusion.4
  130.8 1.5 fusion.9
  132.5 1.3 copy-done.1
  134.3 1.9 collective-permute-start.6
  136.2 3.8 %collective-permute-start.7 = (f32[2,4,1,8,128]{4,3,2,1,0:T(8,128)S(1)}, f32[2,4,1,8,128]{4,3,2,1,0:T(8,128)S(1)}, u32[]{:S(2)}, u32[]{:S(2)}) collective-permute-start(f32[2,4,1,8,128]{4,3,2,1,0:T(8,128)S(1)} %get-tuple-element.350), channel_id=1, source_target_pairs={{0,1},{1,2},{2,3},{3,4},{4,5},{5,6},{6,7},{7,8},{8,9},{9,10},{10,1... | collective-permute-start | bytes 98312 | tf_op jit(solution)/shard_map/ppermute | solution.py:21
  144.7 1.7 multiply_subtract_fusion.13
  146.6 19.3 %all-gather.4 = f32[32,4,8,128]{3,2,1,0:T(8,128)S(1)} all-gather(f32[2,4,8,128]{3,2,1,0:T(8,128)S(1)} %maximum_reduce_fusion.3), channel_id=6, replica_groups=mesh['groups'=2,'depth'=16] {'depth'}, dimensions={0}, use_global_device_ids=true | all-gather | bytes 557056 | tf_op jit(solution)/shard_map/all_gather | solution.py:33
  165.8 1.5 while.55
  167.3 1.7 maximum_reduce_fusion.2
  169.0 30.6 %all-gather.3 = f32[32,4,8,128]{3,2,1,0:T(8,128)} all-gather(f32[2,4,8,128]{3,2,1,0:T(8,128)S(1)} %maximum_reduce_fusion.2), channel_id=5, replica_groups=mesh['groups'=2,'depth'=16] {'depth'}, dimensions={0}, use_global_device_ids=true | all-gather | bytes 557056 | tf_op jit(solution)/shard_map/all_gather | solution.py:33
  199.6 19.1 %while.54 = (s32[]{:T(128)}, f32[2,4,8,128]{3,2,1,0:T(8,128)S(1)}, s32[]{:T(128)}, f32[16,2,8,128]{3,2,1,0:T(8,128)}, f32[16,2,4,8,128]{4,3,2,1,0:T(8,128)}, /*index=5*/s32[]{:T(128)}, s32[]{:T(128)}, s32[]{:T(128)}, s32[]{}) while((s32[]{:T(128)}, f32[2,4,8,128]{3,2,1,0:T(8,128)S(1)}, s32[]{:T(128)}, f32[16,2,8,128]{3,2,1,0:T(8,128)}, ...), condition=%wide.region_10.11_spmd, body=%wide.region_9.10_spmd.sunk | while | flops 40966 | bytes 188567 | solution.py:42
  220.9 6.1 %collective-permute-start.8 = (f32[2,4,2,8,128]{4,3,2,1,0:T(8,128)S(1)}, f32[2,4,2,8,128]{4,3,2,1,0:T(8,128)S(1)}, u32[]{:S(2)}, u32[]{:S(2)}) collective-permute-start(f32[2,4,2,8,128]{4,3,2,1,0:T(8,128)S(1)} %get-tuple-element.345), channel_id=1, source_target_pairs={{0,1},{1,2},{2,3},{3,4},{4,5},{5,6},{6,7},{7,8},{8,9},{9,10},{10,1... | collective-permute-start | bytes 196616 | tf_op jit(solution)/shard_map/ppermute | solution.py:21
  227.1 1.9 collective-permute-start.9
  229.0 3.7 %collective-permute-done.9 = f32[2,4,2,8,128]{4,3,2,1,0:T(8,128)S(1)} collective-permute-done((f32[2,4,2,8,128]{4,3,2,1,0:T(8,128)S(1)}, f32[2,4,2,8,128]{4,3,2,1,0:T(8,128)S(1)}, u32[]{:S(2)}, u32[]{:S(2)}) %collective-permute-start.9) | collective-permute-done | bytes 65568 | tf_op jit(solution)/shard_map/ppermute | solution.py:24
  233.4 1.5 fusion.14
  235.5 1.5 fusion.19
  237.2 1.8 fusion.31
  (201 shorter events, 54.7 us)
Async XLA Ops:
  1.6 36.1 %collective-permute-start = (f32[2,1,8,128]{3,2,1,0:T(8,128)S(1)}, f32[2,1,8,128]{3,2,1,0:T(8,128)S(1)}, u32[]{:S(2)}, u32[]{:S(2)}) collective-permute-start(f32[2,1,8,128]{3,2,1,0:T(8,128)S(1)} %get-tuple-element.386), channel_id=1, source_target_pairs={{0,1},{1,2},{2,3},{3,4},{4,5},{5,6},{6,7},{7,8},{8,9},{9,10},{10,1... | collective-permute-start | bytes 24584 | tf_op jit(solution)/shard_map/ppermute | solution.py:21
  5.3 32.5 %collective-permute-start.1 = (f32[2,1,8,128]{3,2,1,0:T(8,128)S(1)}, f32[2,1,8,128]{3,2,1,0:T(8,128)}, u32[]{:S(2)}, u32[]{:S(2)}) collective-permute-start(f32[2,1,8,128]{3,2,1,0:T(8,128)S(1)} %get-tuple-element.386), channel_id=1, source_target_pairs={{1,0},{2,1},{3,2},{4,3},{5,4},{6,5},{7,6},{8,7},{9,8},{10,9},{11,1... | collective-permute-start | bytes 24584 | tf_op jit(solution)/shard_map/ppermute | solution.py:24
  8.6 30.7 %collective-permute-start.2 = (f32[2,4,1,8,128]{4,3,2,1,0:T(8,128)}, f32[2,4,1,8,128]{4,3,2,1,0:T(8,128)S(1)}, u32[]{:S(2)}, u32[]{:S(2)}) collective-permute-start(f32[2,4,1,8,128]{4,3,2,1,0:T(8,128)} %get-tuple-element.355), channel_id=1, source_target_pairs={{1,0},{2,1},{3,2},{4,3},{5,4},{6,5},{7,6},{8,7},{9,8},{10,9},{11,1... | collective-permute-start | bytes 98312 | tf_op jit(solution)/shard_map/ppermute | solution.py:24
  12.1 27.3 %collective-permute-start.3 = (f32[2,4,1,8,128]{4,3,2,1,0:T(8,128)S(1)}, f32[2,4,1,8,128]{4,3,2,1,0:T(8,128)S(1)}, u32[]{:S(2)}, u32[]{:S(2)}) collective-permute-start(f32[2,4,1,8,128]{4,3,2,1,0:T(8,128)S(1)} %get-tuple-element.356), channel_id=1, source_target_pairs={{0,1},{1,2},{2,3},{3,4},{4,5},{5,6},{6,7},{7,8},{8,9},{9,10},{10,1... | collective-permute-start | bytes 98312 | tf_op jit(solution)/shard_map/ppermute | solution.py:21
  14.3 2.7 %copy-start.21 = (s32[4]{0:T(128)S(1)}, s32[4]{0:T(128)}, u32[]{:S(2)}) copy-start(s32[4]{0:T(128)} %param.16) | copy-start | bytes 52
  17.0 22.4 %copy-start = (f32[2,4,64,8,128]{4,3,2,1,0:T(8,128)S(1)}, f32[2,4,64,8,128]{4,3,2,1,0:T(8,128)}, u32[]{:S(2)}) copy-start(f32[2,4,64,8,128]{4,3,2,1,0:T(8,128)} %param.21) | copy-start | bytes 6291460
  40.5 0.8 copy-start.20
  40.8 1.0 copy-start.6
  41.3 0.9 copy-start.8
  41.3 1.0 copy-start.10
  41.3 1.1 copy-start.12
  105.0 11.1 %copy-start.14 = (f32[64,8,128]{2,1,0:T(8,128)S(1)}, f32[64,8,128]{2,1,0:T(8,128)}, u32[]{:S(2)}) copy-start(f32[64,8,128]{2,1,0:T(8,128)} %get-tuple-element.368) | copy-start | bytes 786436
  105.0 11.1 %copy-start.16 = (f32[64,8,128]{2,1,0:T(8,128)S(1)}, f32[64,8,128]{2,1,0:T(8,128)}, u32[]{:S(2)}) copy-start(f32[64,8,128]{2,1,0:T(8,128)} %get-tuple-element.392) | copy-start | bytes 786436
  114.7 1.6 copy-start.7
  116.4 8.0 %copy-start.19 = (f32[2,68,8,128]{3,2,1,0:T(8,128)S(1)}, f32[2,68,8,128]{3,2,1,0:T(8,128)}, u32[]{:S(2)}) copy-start(f32[2,68,8,128]{3,2,1,0:T(8,128)} %pad_maximum_fusion.10) | copy-start | bytes 1671172
  117.0 7.4 %collective-permute-start.4 = (f32[2,4,2,8,128]{4,3,2,1,0:T(8,128)S(1)}, f32[2,4,2,8,128]{4,3,2,1,0:T(8,128)S(1)}, u32[]{:S(2)}, u32[]{:S(2)}) collective-permute-start(f32[2,4,2,8,128]{4,3,2,1,0:T(8,128)S(1)} %get-tuple-element.351), channel_id=1, source_target_pairs={{0,1},{1,2},{2,3},{3,4},{4,5},{5,6},{6,7},{7,8},{8,9},{9,10},{10,1... | collective-permute-start | bytes 196616 | tf_op jit(solution)/shard_map/ppermute | solution.py:21
  122.4 5.6 %collective-permute-start.5 = (f32[2,4,2,8,128]{4,3,2,1,0:T(8,128)S(1)}, f32[2,4,2,8,128]{4,3,2,1,0:T(8,128)S(1)}, u32[]{:S(2)}, u32[]{:S(2)}) collective-permute-start(f32[2,4,2,8,128]{4,3,2,1,0:T(8,128)S(1)} %get-tuple-element.352), channel_id=1, source_target_pairs={{1,0},{2,1},{3,2},{4,3},{5,4},{6,5},{7,6},{8,7},{9,8},{10,9},{11,1... | collective-permute-start | bytes 196616 | tf_op jit(solution)/shard_map/ppermute | solution.py:24
  132.2 1.6 copy-start.1
  134.3 5.8 %collective-permute-start.6 = (f32[2,4,1,8,128]{4,3,2,1,0:T(8,128)S(1)}, f32[2,4,1,8,128]{4,3,2,1,0:T(8,128)S(1)}, u32[]{:S(2)}, u32[]{:S(2)}) collective-permute-start(f32[2,4,1,8,128]{4,3,2,1,0:T(8,128)S(1)} %get-tuple-element.349), channel_id=1, source_target_pairs={{1,0},{2,1},{3,2},{4,3},{5,4},{6,5},{7,6},{8,7},{9,8},{10,9},{11,1... | collective-permute-start | bytes 98312 | tf_op jit(solution)/shard_map/ppermute | solution.py:24
  136.2 4.7 %collective-permute-start.7 = (f32[2,4,1,8,128]{4,3,2,1,0:T(8,128)S(1)}, f32[2,4,1,8,128]{4,3,2,1,0:T(8,128)S(1)}, u32[]{:S(2)}, u32[]{:S(2)}) collective-permute-start(f32[2,4,1,8,128]{4,3,2,1,0:T(8,128)S(1)} %get-tuple-element.350), channel_id=1, source_target_pairs={{0,1},{1,2},{2,3},{3,4},{4,5},{5,6},{6,7},{7,8},{8,9},{9,10},{10,1... | collective-permute-start | bytes 98312 | tf_op jit(solution)/shard_map/ppermute | solution.py:21
  142.3 1.0 copy-start.2
  142.3 1.3 copy-start.4
  143.6 0.9 copy-start.9
  143.6 1.0 copy-start.11
  143.6 1.1 copy-start.13
  167.3 51.4 %copy-start.18 = (f32[64,8,128]{2,1,0:T(8,128)S(1)}, f32[64,8,128]{2,1,0:T(8,128)}, u32[]{:S(2)}) copy-start(f32[64,8,128]{2,1,0:T(8,128)} %reverse_bitcast_fusion) | copy-start | bytes 786436
  199.6 20.5 %copy-start.15 = (f32[64,8,128]{2,1,0:T(8,128)S(1)}, f32[64,8,128]{2,1,0:T(8,128)}, u32[]{:S(2)}) copy-start(f32[64,8,128]{2,1,0:T(8,128)} %get-tuple-element.368) | copy-start | bytes 786436
  199.6 20.5 %copy-start.17 = (f32[64,8,128]{2,1,0:T(8,128)S(1)}, f32[64,8,128]{2,1,0:T(8,128)}, u32[]{:S(2)}) copy-start(f32[64,8,128]{2,1,0:T(8,128)} %get-tuple-element.392) | copy-start | bytes 786436
  218.7 1.6 copy-start.3
  218.7 1.6 copy-start.5
  220.9 8.1 %collective-permute-start.8 = (f32[2,4,2,8,128]{4,3,2,1,0:T(8,128)S(1)}, f32[2,4,2,8,128]{4,3,2,1,0:T(8,128)S(1)}, u32[]{:S(2)}, u32[]{:S(2)}) collective-permute-start(f32[2,4,2,8,128]{4,3,2,1,0:T(8,128)S(1)} %get-tuple-element.345), channel_id=1, source_target_pairs={{0,1},{1,2},{2,3},{3,4},{4,5},{5,6},{6,7},{7,8},{8,9},{9,10},{10,1... | collective-permute-start | bytes 196616 | tf_op jit(solution)/shard_map/ppermute | solution.py:21
  227.1 5.7 %collective-permute-start.9 = (f32[2,4,2,8,128]{4,3,2,1,0:T(8,128)S(1)}, f32[2,4,2,8,128]{4,3,2,1,0:T(8,128)S(1)}, u32[]{:S(2)}, u32[]{:S(2)}) collective-permute-start(f32[2,4,2,8,128]{4,3,2,1,0:T(8,128)S(1)} %get-tuple-element.346), channel_id=1, source_target_pairs={{1,0},{2,1},{3,2},{4,3},{5,4},{6,5},{7,6},{8,7},{9,8},{10,9},{11,1... | collective-permute-start | bytes 196616 | tf_op jit(solution)/shard_map/ppermute | solution.py:24
where the time goes:
time: 242 us; the launch traced here: 239 us
  blocking collectives  127 us (52%)
  other arithmetic  39.2 us (16%)
  starting transfers between devices  32.3 us (13%)
  local copies, waits for them, and re-layouts  31.5 us (13%)
  waiting for transfers between devices  8.14 us (3%)
    all_gather x5, blocking collectives, carried_in(): gathered = jax.tree.map(lambda a: lax.all_gather(a, axis), part)  127 us
    mul x37, local copies, waits for them, and re-layouts, complex_mul(): left[0] * right[0] - left[1] * right[1]  22.3 us
    ppermute x5, starting transfers between devices, with_halo(): lax.ppermute(lax.slice_in_dim(block, block.shape[dim] - width, None, axis...  21.2 us
    add x30, other arithmetic, link(): complex_mul(later[0], earlier[1]) + later[1]  11.7 us
    ppermute x5, starting transfers between devices, with_halo(): lax.ppermute(lax.slice_in_dim(block, 0, width, axis=dim), axis, backward)  11.1 us
    ppermute x5, waiting for transfers between devices, with_halo(): lax.ppermute(lax.slice_in_dim(block, 0, width, axis=dim), axis, backward)  7.32 us
    sub x42, other arithmetic, complex_mul(): left[0] * right[0] - left[1] * right[1]  7.17 us
    add x4, other arithmetic, local(): wide + neighbours(padded)  5.84 us
  transfers between devices with their start and end apart: 10, of which 3 were waited for; matrix products, arithmetic and copies ran while one was open for 4% of the time, Pallas kernels for 0%

commit v1 on v0

v1 whole, which is shorter than its diff:
```python
import functools

import jax
import jax.numpy as jnp
from jax import lax
from jax.experimental import pallas as pl
from jax.experimental.pallas import tpu as pltpu
from jax.sharding import PartitionSpec as P

relax_weight = 0.8
shift_ratio = 0.5
damping = 3.0
coupling = 0.25

DEEP = 6
keep = 1.0 - relax_weight

VMEM = pltpu.VMEM
SMEM = pltpu.SMEM
ANY = pl.ANY


def cmul(a, b):
    return a[0] * b[0] - a[1] * b[1], a[0] * b[1] + a[1] * b[0]


def add(a, b):
    return a[0] + b[0], a[1] + b[1]


def scale(c, a):
    return c * a[0], c * a[1]


def pick(cond, a, b):
    return jnp.where(cond, a[0], b[0]), jnp.where(cond, a[1], b[1])


def edge_masks(height, breadth):
    row = lax.broadcasted_iota(jnp.int32, (height, breadth), 0)
    lane = lax.broadcasted_iota(jnp.int32, (height, breadth), 1)
    return row > 0, row < height - 1, lane > 0, lane < breadth - 1


def lateral(field, masks):
    height, breadth = field.shape[-2:]
    rows, lanes = field.ndim - 2, field.ndim - 1
    total = jnp.where(masks[0], pltpu.roll(field, 1, rows), 0.0)
    total += jnp.where(masks[1], pltpu.roll(field, height - 1, rows), 0.0)
    total += jnp.where(masks[2], pltpu.roll(field, 1, lanes), 0.0)
    total += jnp.where(masks[3], pltpu.roll(field, breadth - 1, lanes), 0.0)
    return total


def around(before, here, after, masks):
    out = []
    for part in range(2):
        total = lateral(here[part], masks)
        if before is not None:
            total += before[part]
        if after is not None:
            total += after[part]
        out.append(total)
    return tuple(out)


def minus_a(before, here, after, diagonal, layer3, masks):
    beside = around(before, here, after, masks)
    return (
        beside[0] - diagonal * here[0] + layer3 * here[1],
        beside[1] - diagonal * here[1] - layer3 * here[0],
    )


def coefficients(squared, layer):
    diagonal = 6.0 - squared
    imag = shift_ratio * squared + damping * layer
    size = diagonal * diagonal + imag * imag
    return diagonal, (relax_weight * diagonal / size, -relax_weight * imag / size)


def wave(absorb, squared, slab):
    size = jnp.exp(-absorb / slab)
    angle = jnp.sqrt(squared)
    return size * jnp.cos(angle), size * jnp.sin(angle)


def region_values(labels, kk_ref):
    squared = jnp.zeros(labels.shape, jnp.float32)
    for region in range(kk_ref.shape[0]):
        squared = jnp.where(labels == region, kk_ref[region], squared)
    return squared


def loop(start, stop, body, carry, unroll):
    trips = (stop - start) // unroll

    def several(trip, carry):
        for i in range(unroll):
            carry = body(start + trip * unroll + i, carry)
        return carry

    carry = lax.fori_loop(0, trips, several, carry)
    for plane in range(start + trips * unroll, stop):
        carry = body(plane, carry)
    return carry


def start_kernel(
    plan, kk, damp, sources, absorb, labels, guess,
    residual, emits, media, power, ends,
):
    slab = guess.shape[2]
    count = guess.shape[1]
    height, breadth = guess.shape[-2:]
    masks = edge_masks(height, breadth)
    row = lax.broadcasted_iota(jnp.int32, (height, breadth), 0)
    lane = lax.broadcasted_iota(jnp.int32, (height, breadth), 1)
    cell = row * breadth + lane

    def mark(i, hit):
        return jnp.where(cell == damp[i], 1.0, hit)

    layer = loop(0, damp.shape[0], mark, jnp.zeros((height, breadth), jnp.float32), 8)
    squared = region_values(labels[0], kk)
    diagonal, inverse = coefficients(squared, layer)
    layer3 = damping * layer
    factor = wave(absorb[0], squared, slab)
    media[0], media[1], media[2], media[3] = inverse[0], inverse[1], diagonal, layer3
    media[4], media[5] = factor

    power[0, 0] = jnp.ones((height, breadth), jnp.float32)
    power[0, 1] = jnp.zeros((height, breadth), jnp.float32)
    for first, last in halves(count):
        pick_s = slice(first, last)

        def get(k):
            return guess[0, pick_s, k], guess[1, pick_s, k]

        def plane(k, carry, before=True, after=True):
            toward_next, toward_prev, w = carry
            r = minus_a(
                get(k - 1) if before else None, get(k), get(k + 1) if after else None,
                diagonal, layer3, masks,
            )
            residual[0, pick_s, k], residual[1, pick_s, k] = r
            toward_next = add(cmul(factor, toward_next), r)
            toward_prev = add(toward_prev, cmul(w, r))
            w = cmul(factor, w)
            power[k + 1, 0], power[k + 1, 1] = w
            return toward_next, toward_prev, w

        zero = jnp.zeros((last - first, height, breadth), jnp.float32)
        carry = ((zero, zero), (zero, zero), (power[0, 0], power[0, 1]))
        carry = plane(0, carry, before=False)
        carry = loop(1, slab - 1, plane, carry, 2)
        carry = plane(slab - 1, carry, after=False)
        for part in range(2):
            emits[0, part, pick_s] = carry[0][part]
            emits[1, part, pick_s] = carry[1][part]
    first_plane = lax.axis_index("depth") * slab
    for s in range(count):
        k = plan[s] - first_plane

        @pl.when((k >= 0) & (k < slab))
        def _():
            src = sources[0, s], sources[1, s]
            for part in range(2):
                residual[part, s, k] += src[part]
            one = cmul((power[slab - 1 - k, 0], power[slab - 1 - k, 1]), src)
            two = cmul((power[k, 0], power[k, 1]), src)
            for part in range(2):
                emits[0, part, s] += one[part]
                emits[1, part, s] += two[part]

    for end, k in enumerate((0, slab - 1)):
        for part in range(2):
            ends[0, end, part] = guess[part, :, k]
            ends[1, end, part] = residual[part, :, k]


def halves(count):
    if count == 1:
        return [(0, 1)]
    return [(0, count // 2), (count // 2, count)]


def arrange_kernel(
    got_even, got_odd, ends, emits, media, power, full, *sends,
):
    count = emits.shape[2]
    slab = power.shape[0] - 1
    place = lax.axis_index("depth")
    even = lax.rem(place, 2) == 0
    weight = power[slab - 1, 0], power[slab - 1, 1]
    tile = lambda part, s, k: (part * count + s) * DEEP + k
    for s in range(count):
        low = tuple(
            jnp.where(even, got_odd[tile(c, s, DEEP - 1)], got_even[tile(c, s, DEEP - 1)])
            for c in range(2)
        )
        high = tuple(
            jnp.where(even, got_even[tile(c, s, 0)], got_odd[tile(c, s, 0)])
            for c in range(2)
        )
        toward_next = add(add(cmul(weight, low), high), (emits[0, 0, s], emits[0, 1, s]))
        toward_prev = add(add(cmul(weight, high), low), (emits[1, 0, s], emits[1, 1, s]))
        for part in range(2):
            full[0, part, s] = toward_next[part]
            full[1, part, s] = toward_prev[part]
    fill_sends(place, full, sends, halves(count), (power[slab, 0], power[slab, 1]))


def fill_sends(place, full, sends, spans, passage=None):
    for send, (first, last) in zip(sends, spans):
        width = last - first

        def one(j, unused):
            later = j > place
            for part in range(2):
                send[j, pl.ds(part * width, width)] = jnp.where(
                    later, full[0, part, first:last], full[1, part, first:last]
                )
            if passage is not None and first == 0:
                send[j, 2 * width] = passage[0]
                send[j, 2 * width + 1] = passage[1]
            return unused

        lax.fori_loop(0, send.shape[0], one, 0)


def prepare_kernel(
    plan, kk, got_even, got_odd, sources, ends, media,
    near, near_residual, near_media, near_power,
):
    count = sources.shape[1]
    slab = near_power.shape[1] - 1
    height, breadth = sources.shape[-2:]
    masks = edge_masks(height, breadth)
    place = lax.axis_index("depth")
    last_place = lax.axis_size("depth") - 1
    even = lax.rem(place, 2) == 0
    tiles = 2 * count * DEEP
    layer3 = media[3]
    layer = layer3 / damping
    for side in range(2):
        first, second = (got_odd, got_even) if side == 0 else (got_even, got_odd)

        def copy(i, unused):
            part = i // count
            s = lax.rem(i, count)
            near[side, part, s] = jnp.where(
                even, first[pl.ds(i * DEEP, DEEP)], second[pl.ds(i * DEEP, DEEP)]
            )
            return unused

        lax.fori_loop(0, 2 * count, copy, 0)
        absorb = jnp.where(even, first[tiles], second[tiles])
        labels = jnp.where(even, first[tiles + 1], second[tiles + 1]).astype(jnp.int32)
        squared = region_values(labels, kk)
        diagonal, inverse = coefficients(squared, layer)
        inside = (place > 0) if side == 0 else (place < last_place)
        for part in range(2):
            near_media[side, part] = jnp.where(inside, inverse[part], 0.0)
        near_media[side, 2] = diagonal
        near_media[side, 3] = layer3
        factor = wave(absorb, squared, slab)
        near_media[side, 4], near_media[side, 5] = factor
        near_power[side, 0, 0] = jnp.ones((height, breadth), jnp.float32)
        near_power[side, 0, 1] = jnp.zeros((height, breadth), jnp.float32)

    def raise_power(k, w):
        out = []
        for side in range(2):
            next_w = cmul((near_media[side, 4], near_media[side, 5]), w[side])
            near_power[side, k + 1, 0], near_power[side, k + 1, 1] = next_w
            out.append(next_w)
        return tuple(out)

    start = tuple((near_power[side, 0, 0], near_power[side, 0, 1]) for side in range(2))
    loop(0, slab, raise_power, start, 4)

    for first, last in halves(count):
        pick_s = slice(first, last)
        for side in range(2):

            def get(i):
                if side == 0 and i == DEEP:
                    return ends[0, 0, 0, pick_s], ends[0, 0, 1, pick_s]
                if side == 1 and i == -1:
                    return ends[0, 1, 0, pick_s], ends[0, 1, 1, pick_s]
                return near[side, 0, pick_s, i], near[side, 1, pick_s, i]

            for i in range(1 - side, DEEP - side):
                r = minus_a(
                    get(i - 1), get(i), get(i + 1),
                    near_media[side, 2], layer3, masks,
                )
                for part in range(2):
                    near_residual[side, part, pick_s, i if side else i - 1] = r[part]

    for s in range(count):
        k = plan[s] - place * slab
        for side, low in ((0, 1 - DEEP), (1, slab)):
            i = k - low

            @pl.when((i >= 0) & (i < DEEP - 1))
            def _():
                for part in range(2):
                    near_residual[side, part, s, i] += sources[part, s]


def own_incoming(place, last_place, got, passages, at, width, full, span, power, slab):
    shape = got.shape[-2:]
    zero = jnp.zeros((width,) + shape, jnp.float32)

    def wave_of(j):
        return got[j, pl.ds(0, width)], got[j, pl.ds(width, width)]

    def step(j, state):
        return add(cmul((passages[j, at], passages[j, at + 1]), state), wave_of(j))

    below = jnp.maximum(place - 1, 0)
    above = jnp.minimum(place + 1, last_place)
    next_low = lax.fori_loop(0, below, step, (zero, zero))
    next_own = pick(place > 0, step(below, next_low), (zero, zero))
    prev_high = lax.fori_loop(
        0, last_place - above, lambda t, state: step(last_place - t, state), (zero, zero)
    )
    prev_own = pick(place < last_place, step(above, prev_high), (zero, zero))
    passage = power[slab, 0], power[slab, 1]
    first, last = span
    emit = lambda way: (full[way, 0, first:last], full[way, 1, first:last])
    next_high = add(cmul(passage, next_own), emit(0))
    prev_low = add(cmul(passage, prev_own), emit(1))
    return [
        (scale(coupling, a), scale(coupling, b))
        for a, b in ((next_low, prev_low), (next_own, prev_own), (next_high, prev_high))
    ]


def update_passes(
    reach, slab, incoming, residual_of, media, near_media, power, near_power,
    first_update, second_update, emit, masks,
):
    sides = (
        (-reach, 0, near_media.at[0], near_power.at[0], incoming[0], slab),
        (0, slab, media, power, incoming[1], 0),
        (slab, slab + reach, near_media.at[1], near_power.at[1], incoming[2], -slab),
    )
    for which, (start, stop, m, w, (onward, back), shift) in enumerate(sides):
        inverse = m[0], m[1]

        def begin(p, unused):
            k = p + shift
            c = residual_of(which, p)
            c = add(c, cmul((w[k + 1, 0], w[k + 1, 1]), onward))
            c = add(c, cmul((w[slab - k, 0], w[slab - k, 1]), back))
            u = cmul(inverse, c)
            first_update[0, :, p + reach], first_update[1, :, p + reach] = u
            return unused

        if which == 1:
            begin(0, 0)
            loop(1, slab - 1, begin, 0, 2)
            begin(slab - 1, 0)
        else:
            loop(start, stop, begin, 0, 1)
    for which, (start, stop, m, *rest) in enumerate(sides):
        inverse = m[0], m[1]

        def second(p, unused):
            get = lambda q: (first_update[0, :, q + reach], first_update[1, :, q + reach])
            here = get(p)
            beside = around(get(p - 1), here, get(p + 1), masks)
            u = add(scale(1.0 + keep, here), cmul(inverse, beside))
            second_update[0, :, p + reach - 1], second_update[1, :, p + reach - 1] = u
            return unused

        loop(max(start, 1 - reach), min(stop, slab + reach - 1), second, 0, 2)
    for which, (start, stop, m, *rest) in enumerate(sides):
        inverse = m[0], m[1]

        def third(p, unused):
            get = lambda q: (
                second_update[0, :, q + reach - 1],
                second_update[1, :, q + reach - 1],
            )
            here = get(p)
            beside = around(get(p - 1), here, get(p + 1), masks)
            u = add(scale(keep, here), cmul(inverse, beside))
            u = add(u, (first_update[0, :, p + reach], first_update[1, :, p + reach]))
            emit(which, p, u)
            return unused

        loop(max(start, 2 - reach), min(stop, slab + reach - 2), third, 0, 2)


def middle_kernel(
    span, at, plan, sources, guess, residual, near, near_residual, ends, media, power,
    near_media, near_power, got, passages, full,
    solution, next_residual, next_full, send, first_update, second_update,
):
    first, last = span
    width = last - first
    slab = guess.shape[2]
    height, breadth = guess.shape[-2:]
    masks = edge_masks(height, breadth)
    place = lax.axis_index("depth")
    last_place = lax.axis_size("depth") - 1
    reach = DEEP - 1
    even = lax.rem(place, 2) == 0
    incoming = own_incoming(
        place, last_place, got, passages, at, width, full, span, power, slab
    )

    def residual_of(which, p):
        if which == 0:
            i = p + reach
            return near_residual[0, 0, first:last, i], near_residual[0, 1, first:last, i]
        if which == 2:
            i = p - slab
            return near_residual[1, 0, first:last, i], near_residual[1, 1, first:last, i]
        r = residual[0, first:last, p], residual[1, first:last, p]
        if isinstance(p, int) and p == 0:
            r = add(r, (near[0, 0, first:last, DEEP - 1], near[0, 1, first:last, DEEP - 1]))
        if isinstance(p, int) and p == slab - 1:
            r = add(r, (near[1, 0, first:last, 0], near[1, 1, first:last, 0]))
        return r

    ext = reach - 2

    def emit(which, p, u):
        for part in range(2):
            if which == 0:
                old = near[0, part, first:last, p + DEEP]
            elif which == 1:
                old = guess[part, first:last, p]
            else:
                old = near[1, part, first:last, p - slab]
            solution[part, :, p + ext] = old + u[part]

    update_passes(
        reach, slab, incoming, residual_of, media, near_media, power, near_power,
        first_update, second_update, emit, masks,
    )

    get = lambda p: (solution[0, :, p + ext], solution[1, :, p + ext])
    layer3 = media[3]
    more = ext - 1
    factor = media[4], media[5]

    def outside(diagonal):
        def one(p, unused):
            r = minus_a(get(p - 1), get(p), get(p + 1), diagonal, layer3, masks)
            next_residual[0, :, p + more], next_residual[1, :, p + more] = r
            return unused

        return one

    loop(-more, 0, outside(near_media[0, 2]), 0, 1)
    loop(slab, slab + more, outside(near_media[1, 2]), 0, 1)
    diagonal = media[2]

    def inside(p, carry):
        toward_next, toward_prev = carry
        r = minus_a(get(p - 1), get(p), get(p + 1), diagonal, layer3, masks)
        next_residual[0, :, p + more], next_residual[1, :, p + more] = r
        toward_next = add(cmul(factor, toward_next), r)
        toward_prev = add(toward_prev, cmul((power[p, 0], power[p, 1]), r))
        return toward_next, toward_prev

    zero = jnp.zeros((width, height, breadth), jnp.float32)
    carry = loop(0, slab, inside, ((zero, zero), (zero, zero)), 2)
    for way in range(2):
        for part in range(2):
            next_full[way, part] = carry[way][part]
    for s in range(width):
        k = plan[first + s] - place * slab
        src = sources[0, first + s], sources[1, first + s]

        @pl.when((k >= -more) & (k < slab + more))
        def _():
            for part in range(2):
                next_residual[part, s, k + more] += src[part]

        @pl.when((k >= 0) & (k < slab))
        def _():
            one = cmul((power[slab - 1 - k, 0], power[slab - 1 - k, 1]), src)
            two = cmul((power[k, 0], power[k, 1]), src)
            for part in range(2):
                next_full[0, part, s] += one[part]
                next_full[1, part, s] += two[part]

    fill_sends(place, next_full, (send,), [(0, width)])


def final_kernel(
    span, at, aliased, residual, solution, media, power, near_media, near_power,
    got, passages, full, *rest,
):
    if aliased:
        rest = rest[1:]
    out, first_update, second_update, stage, sems = rest
    first, last = span
    width = last - first
    slab = out.shape[2]
    height, breadth = out.shape[-2:]
    masks = edge_masks(height, breadth)
    place = lax.axis_index("depth")
    last_place = lax.axis_size("depth") - 1
    reach = 2
    ext = DEEP - 3
    incoming = own_incoming(
        place, last_place, got, passages, at, width, full, (0, width), power, slab
    )

    def residual_of(which, p):
        return residual[0, :, p + reach], residual[1, :, p + reach]

    def emit(which, p, u):
        for part in range(2):
            stage[part, :, p] = solution[part, :, p + ext] + u[part]

    update_passes(
        reach, slab, incoming, residual_of, media, near_media, power, near_power,
        first_update, second_update, emit, masks,
    )
    copies = []
    for part in range(2):
        copies.append(
            pltpu.make_async_copy(
                stage.at[part], out.at[part, pl.ds(first, width)], sems.at[part]
            )
        )
        copies[-1].start()
    for copy in copies:
        copy.wait()


def call(kernel, operands, out_shape, spaces, out_spaces=None, scratch=(), cost=0, alias=None, name=None):
    space = lambda s: pl.BlockSpec(memory_space=s)
    single = not isinstance(out_shape, (tuple, list))
    outs = (out_shape,) if single else tuple(out_shape)
    out_spaces = out_spaces or (VMEM,) * len(outs)
    result = pl.pallas_call(
        kernel,
        out_shape=tuple(jax.ShapeDtypeStruct(s, jnp.float32) for s in outs),
        in_specs=[space(s) for s in spaces],
        out_specs=tuple(space(s) for s in out_spaces),
        scratch_shapes=scratch,
        input_output_aliases=alias or {},
        compiler_params=pltpu.CompilerParams(vmem_limit_bytes=24 << 20),
        cost_estimate=pl.CostEstimate(flops=cost, bytes_accessed=4 << 20, transcendentals=0),
        name=name,
    )(*operands)
    return result


def local(sources, plan, absorb, labels, region_kk, damp_cells, guess):
    size = lax.axis_size("depth")
    place = lax.axis_index("depth")
    _, count, slab, height, breadth = guess.shape
    tile = (height, breadth)
    spans = halves(count)

    even = place % 2 == 0
    top = slab - DEEP

    def payload(start):
        planes = lax.dynamic_slice_in_dim(guess, start, DEEP, axis=2)
        return jnp.concatenate(
            [planes.reshape((-1,) + tile), absorb, labels.astype(jnp.float32)], axis=0
        )

    even_pairs = [(i, i ^ 1) for i in range(size) if i ^ 1 < size]
    odd_pairs = [(i, i + 1) for i in range(1, size - 1, 2)]
    odd_pairs += [(b, a) for a, b in odd_pairs]
    got_odd = lax.ppermute(payload(jnp.where(even, 0, top)), "depth", odd_pairs)
    got_even = lax.ppermute(payload(jnp.where(even, top, 0)), "depth", even_pairs)

    field = (2, count, slab) + tile
    residual, emits, media, power, ends = call(
        start_kernel,
        (plan, region_kk, damp_cells, sources, absorb, labels, guess),
        (
            field,
            (2, 2, count) + tile,
            (6,) + tile,
            (slab + 1, 2) + tile,
            (2, 2, 2, count) + tile,
        ),
        (SMEM, SMEM, SMEM, VMEM, VMEM, VMEM, VMEM),
        cost=40_000_000,
        name="start",
    )
    sends = tuple(
        (size, 2 * (b - a) + (2 if a == 0 else 0)) + tile for a, b in spans
    )
    full, *sends = call(
        arrange_kernel,
        (got_even, got_odd, ends, emits, media, power),
        ((2, 2, count) + tile,) + sends,
        (VMEM,) * 6,
        cost=1_000_000,
        name="arrange",
    )
    got = [lax.all_to_all(send, "depth", 0, 0) for send in sends]
    near, near_residual, near_media, near_power = call(
        prepare_kernel,
        (plan, region_kk, got_even, got_odd, sources, ends, media),
        (
            (2, 2, count, DEEP) + tile,
            (2, 2, count, DEEP - 1) + tile,
            (2, 6) + tile,
            (2, slab + 1, 2) + tile,
        ),
        (SMEM, SMEM, VMEM, VMEM, VMEM, VMEM, VMEM),
        cost=2_000_000,
        name="prepare",
    )
    passages = got[0]
    at = 2 * (spans[0][1] - spans[0][0])
    middles = []
    for span, piece in zip(spans, got):
        width = span[1] - span[0]
        middles.append(
            call(
                functools.partial(middle_kernel, span, at),
                (
                    plan, sources, guess, residual, near, near_residual, ends, media,
                    power, near_media, near_power, piece, passages, full,
                ),
                (
                    (2, width, slab + 2 * (DEEP - 3)) + tile,
                    (2, width, slab + 2 * (DEEP - 4)) + tile,
                    (2, 2, width) + tile,
                    (size, 2 * width) + tile,
                ),
                (SMEM,) + (VMEM,) * 13,
                scratch=[
                    pltpu.VMEM((2, width, slab + 2 * DEEP - 2) + tile, jnp.float32),
                    pltpu.VMEM((2, width, slab + 2 * DEEP - 4) + tile, jnp.float32),
                ],
                cost=40_000_000,
                name="middle",
            )
        )
    got = [lax.all_to_all(m[3], "depth", 0, 0) for m in middles]
    out = None
    for span, piece, (solution, next_residual, next_full, _) in zip(spans, got, middles):
        width = span[1] - span[0]
        operands = (
            next_residual, solution, media, power, near_media, near_power,
            piece, passages, next_full,
        )
        spaces = (VMEM,) * 9
        alias = {}
        if out is not None:
            operands += (out,)
            spaces += (ANY,)
            alias = {9: 0}
        (out,) = call(
            functools.partial(final_kernel, span, at, out is not None),
            operands,
            (field,),
            spaces,
            (ANY,),
            scratch=[
                pltpu.VMEM((2, width, slab + 4) + tile, jnp.float32),
                pltpu.VMEM((2, width, slab + 2) + tile, jnp.float32),
                pltpu.VMEM((2, width, slab) + tile, jnp.float32),
                pltpu.SemaphoreType.DMA((2,)),
            ],
            cost=30_000_000,
            alias=alias,
            name="final",
        )
    return out


def solution(mesh):
    return jax.shard_map(
        local,
        mesh=mesh,
        in_specs=(
            P(None, "groups", None, None),
            P("groups"),
            P("depth", "groups", None),
            P("depth", "groups", None),
            P(),
            P("groups"),
            P(None, "groups", "depth", None, None),
        ),
        out_specs=P(None, "groups", "depth", None, None),
        check_vma=False,
    )
```

time: 242 us -> 137 us (0.57)
  the two profiles are of different devices: /device:TPU:25 before, /device:TPU:0 now
where the time goes in v1:
time: 137 us; the launch traced here: 135 us
  Pallas kernels  48.9 us (36%)
  local copies, waits for them, and re-layouts  46.1 us (34%)
  blocking collectives  20.7 us (15%)
  starting transfers between devices  17.3 us (13%)
  other arithmetic  1.41 us (1%)
    pallas_call x7, Pallas kernels, call(): pl.pallas_call(kernel, out_shape=tuple((jax.ShapeDtypeStruct(s, jnp.float...  48.9 us
    unnamed x124, local copies, waits for them, and re-layouts  45 us
    all_to_all x1, blocking collectives, local(): got = [lax.all_to_all(send, 'depth', 0, 0) for send in sends]  20.7 us
    all_to_all x2, starting transfers between devices, local(): got = [lax.all_to_all(m[3], 'depth', 0, 0) for m in middles]  11.9 us
    all_to_all x1, starting transfers between devices, local(): got = [lax.all_to_all(send, 'depth', 0, 0) for send in sends]  4.2 us
  transfers between devices with their start and end apart: 5, of which 0 were waited for; matrix products, arithmetic and copies ran while one was open for 0% of the time, Pallas kernels for 30%

profile of v1, /device:TPU:0, one launch (start us, length us, event | category | flops | bytes accessed | tf_op | source)
XLA Modules:
  0.0 134.8 jit_solution(3328050247807525951)
XLA Ops:
  0.7 1.0 constant_dynamic-slice_fusion
  3.7 1.6 %copy-done = f32[2,4,64,8,128]{4,3,2,1,0:T(8,128)S(1)} copy-done((f32[2,4,64,8,128]{4,3,2,1,0:T(8,128)S(1)}, f32[2,4,64,8,128]{4,3,2,1,0:T(8,128)}, u32[]{:S(2)}) %copy-start) | copy-done | bytes 2097176
  9.4 6.9 %start.1 = (f32[2,4,64,8,128]{4,3,2,1,0:T(8,128)S(1)}, f32[2,2,4,8,128]{4,3,2,1,0:T(8,128)S(1)}, f32[6,8,128]{2,1,0:T(8,128)S(1)}, f32[65,2,8,128]{3,2,1,0:T(8,128)S(1)}, f32[2,2,2,4,8,128]{5,4,3,2,1,0:T(8,128)S(1)}) custom-call(s32[4]{0:T(128)S(1)} %copy-done.55, f32[8]{0:T(128)S(1)} %copy-done.59, s32[128]{0:T(128)S(1)} %copy-done.61, ...), custom_call_target="tpu_custom_call" | custom-call | flops 40000000 | bytes 4194304 | tf_op jit(solution)/shard_map/start/pallas_call | solution.py:546
  16.3 1.3 copy-done.7
  17.7 1.0 arrange.1
  18.7 20.7 %all_to_all.20.passages.got = f32[16,6,8,128]{3,2,1,0:T(8,128)S(1)} all-to-all(f32[16,6,8,128]{3,2,1,0:T(8,128)S(1)} %get-tuple-element.35), channel_id=1, replica_groups=mesh['groups'=2,'depth'=16] {'depth'}, dimensions={0} | all-to-all | bytes 786432 | tf_op jit(solution)/shard_map/all_to_all | solution.py:608
  39.5 4.2 %all-to-all-start = ((f32[16,4,8,128]{3,2,1,0:T(8,128)}), f32[16,4,8,128]{3,2,1,0:T(8,128)}, u32[]{:S(2)}, u32[]{:S(2)}) async-start(f32[16,4,8,128]{3,2,1,0:T(8,128)} %get-tuple-element.34), calls=%async_computation | async-start | bytes 524288 | tf_op jit(solution)/shard_map/all_to_all | solution.py:608
  45.3 0.9 copy-done.33
  46.2 0.9 copy-done.35
  49.2 1.3 prepare.1
  50.6 1.0 copy-done.3
  51.6 1.6 %copy-done.8 = f32[2,4,64,8,128]{4,3,2,1,0:T(8,128)S(1)} copy-done((f32[2,4,64,8,128]{4,3,2,1,0:T(8,128)S(1)}, f32[2,4,64,8,128]{4,3,2,1,0:T(8,128)}, u32[]{:S(2)}) %copy-start.8) | copy-done | bytes 2097176
  53.2 0.9 copy-done.12
  57.1 11.3 %middle.3 = (f32[2,2,70,8,128]{4,3,2,1,0:T(8,128)S(1)}, f32[2,2,68,8,128]{4,3,2,1,0:T(8,128)S(1)}, f32[2,2,2,8,128]{4,3,2,1,0:T(8,128)S(1)}, f32[16,4,8,128]{3,2,1,0:T(8,128)S(1)}) custom-call(s32[4]{0:T(128)S(1)} %copy-done.57, f32[2,4,8,128]{3,2,1,0:T(8,128)S(1)} %copy-done.42, f32[2,4,64,8,128]{4,3,2,1,0:T(8,128)S(1)} %copy-done.1, ...), custom_call_target="tpu_custom_call" | custom-call | flops 40000000 | bytes 4194304 | tf_op jit(solution)/shard_map/middle/pallas_call | solution.py:546
  69.9 1.0 copy-done.20
  70.9 1.0 copy-done.24
  73.9 5.9 %all-to-all-start.3 = ((f32[16,4,8,128]{3,2,1,0:T(8,128)}), f32[16,4,8,128]{3,2,1,0:T(8,128)}, u32[]{:S(2)}, u32[]{:S(2)}) async-start(f32[16,4,8,128]{3,2,1,0:T(8,128)} %copy-done.48), calls=%async_computation.3 | async-start | bytes 524288 | tf_op jit(solution)/shard_map/all_to_all | solution.py:649
  79.8 1.0 copy-done.4
  80.9 1.6 %copy-done.9 = f32[2,4,64,8,128]{4,3,2,1,0:T(8,128)S(1)} copy-done((f32[2,4,64,8,128]{4,3,2,1,0:T(8,128)S(1)}, f32[2,4,64,8,128]{4,3,2,1,0:T(8,128)}, u32[]{:S(2)}) %copy-start.9) | copy-done | bytes 2097176
  82.5 0.9 copy-done.13
  83.4 1.0 copy-done.15
  84.4 1.0 copy-done.17
  89.1 11.7 %middle.2 = (f32[2,2,70,8,128]{4,3,2,1,0:T(8,128)S(1)}, f32[2,2,68,8,128]{4,3,2,1,0:T(8,128)S(1)}, f32[2,2,2,8,128]{4,3,2,1,0:T(8,128)S(1)}, f32[16,4,8,128]{3,2,1,0:T(8,128)S(1)}) custom-call(s32[4]{0:T(128)S(1)} %copy-done.58, f32[2,4,8,128]{3,2,1,0:T(8,128)S(1)} %copy-done.43, f32[2,4,64,8,128]{4,3,2,1,0:T(8,128)S(1)} %copy-done.1, ...), custom_call_target="tpu_custom_call" | custom-call | flops 40000000 | bytes 4194304 | tf_op jit(solution)/shard_map/middle/pallas_call | solution.py:546
  100.9 1.0 copy-done.18
  101.9 1.0 copy-done.22
  104.2 5.9 %all-to-all-start.2 = ((f32[16,4,8,128]{3,2,1,0:T(8,128)}), f32[16,4,8,128]{3,2,1,0:T(8,128)S(1)}, u32[]{:S(2)}, u32[]{:S(2)}) async-start(f32[16,4,8,128]{3,2,1,0:T(8,128)} %copy-done.47), calls=%async_computation.2 | async-start | bytes 524288 | tf_op jit(solution)/shard_map/all_to_all | solution.py:649
  110.2 1.0 copy-done.5
  111.2 1.3 copy-done.21
  112.5 1.2 copy-done.25
  116.0 8.9 %final.2.rest_0_ = f32[2,4,64,8,128]{4,3,2,1,0:T(8,128)} custom-call(f32[2,2,68,8,128]{4,3,2,1,0:T(8,128)S(1)} %copy-done.25, f32[2,2,70,8,128]{4,3,2,1,0:T(8,128)S(1)} %copy-done.21, f32[6,8,128]{2,1,0:T(8,128)S(1)} %copy-done.30, f32[65,2,8,128]{3,2,1,0:T(8,128)S(1)} %copy-done.5, f32[2,6,8,128]{3,2,1,0:T(8,128)S(1)} %copy-done.38, ...), custom_call_target="tpu_custom_call" | custom-call | flops 30000000 | bytes 4194304 | tf_op jit(solution)/shard_map/final/pallas_call | solution.py:546
  125.0 1.2 copy-done.23
  127.0 7.8 %final.3 = f32[2,4,64,8,128]{4,3,2,1,0:T(8,128)} custom-call(f32[2,2,68,8,128]{4,3,2,1,0:T(8,128)S(1)} %copy-done.23, f32[2,2,70,8,128]{4,3,2,1,0:T(8,128)S(1)} %copy-done.19, f32[6,8,128]{2,1,0:T(8,128)S(1)} %copy-done.31, f32[65,2,8,128]{3,2,1,0:T(8,128)S(1)} %copy-done.6, f32[2,6,8,128]{3,2,1,0:T(8,128)S(1)} %copy-done.39, ...), custom_call_target="tpu_custom_call", output_to_operand_aliasing={{}: (9, {})} | custom-call | flops 30000000 | bytes 4194304 | tf_op jit(solution)/shard_map/final/pallas_call | solution.py:546
  (113 shorter events, 25.1 us)
Async XLA Ops:
  2.5 15.2 %collective-permute-start = (f32[50,8,128]{2,1,0:T(8,128)S(1)}, f32[50,8,128]{2,1,0:T(8,128)S(1)}, u32[]{:S(2)}, u32[]{:S(2)}) collective-permute-start(f32[50,8,128]{2,1,0:T(8,128)S(1)} %get-tuple-element.48), channel_id=1, source_target_pairs={{0,1},{1,0},{2,3},{3,2},{4,5},{5,4},{6,7},{7,6},{8,9},{9,8},{10,11... | collective-permute-start | bytes 614408 | tf_op jit(solution)/shard_map/ppermute | solution.py:580
  3.0 14.6 %collective-permute-start.1 = (f32[50,8,128]{2,1,0:T(8,128)S(1)}, f32[50,8,128]{2,1,0:T(8,128)S(1)}, u32[]{:S(2)}, u32[]{:S(2)}) collective-permute-start(f32[50,8,128]{2,1,0:T(8,128)S(1)} %get-tuple-element.47), channel_id=1, source_target_pairs={{1,2},{3,4},{5,6},{7,8},{9,10},{11,12},{13,14},{2,1},{4,3},{6,5},{... | collective-permute-start | bytes 614408 | tf_op jit(solution)/shard_map/ppermute | solution.py:579
  3.7 1.6 %copy-start = (f32[2,4,64,8,128]{4,3,2,1,0:T(8,128)S(1)}, f32[2,4,64,8,128]{4,3,2,1,0:T(8,128)}, u32[]{:S(2)}) copy-start(f32[2,4,64,8,128]{4,3,2,1,0:T(8,128)} %guess.5) | copy-start | bytes 6291460
  9.4 41.2 %copy-start.1 = (f32[2,4,64,8,128]{4,3,2,1,0:T(8,128)S(1)}, f32[2,4,64,8,128]{4,3,2,1,0:T(8,128)}, u32[]{:S(2)}) copy-start(f32[2,4,64,8,128]{4,3,2,1,0:T(8,128)} %guess.5) | copy-start | bytes 6291460
  16.3 1.3 copy-start.7
  17.6 1.1 copy-start.2
  17.6 1.1 copy-start.10
  17.6 21.8 %copy-start.26 = (f32[6,8,128]{2,1,0:T(8,128)}, f32[6,8,128]{2,1,0:T(8,128)S(1)}, u32[]{:S(2)}) copy-start(f32[6,8,128]{2,1,0:T(8,128)S(1)} %get-tuple-element.27.media) | copy-start | bytes 73732
  17.7 21.8 %copy-start.32 = (f32[50,8,128]{2,1,0:T(8,128)}, f32[50,8,128]{2,1,0:T(8,128)S(1)}, u32[]{:S(2)}) copy-start(f32[50,8,128]{2,1,0:T(8,128)S(1)} %collective-permute-done.got_even) | copy-start | bytes 614404
  17.7 21.8 %copy-start.34 = (f32[50,8,128]{2,1,0:T(8,128)}, f32[50,8,128]{2,1,0:T(8,128)S(1)}, u32[]{:S(2)}) copy-start(f32[50,8,128]{2,1,0:T(8,128)S(1)} %collective-permute-done.1.got_odd) | copy-start | bytes 614404
  18.7 20.7 %copy-start.44 = (f32[2,2,4,8,128]{4,3,2,1,0:T(8,128)}, f32[2,2,4,8,128]{4,3,2,1,0:T(8,128)S(1)}, u32[]{:S(2)}) copy-start(f32[2,2,4,8,128]{4,3,2,1,0:T(8,128)S(1)} %get-tuple-element.36.full) | copy-start | bytes 196612
  39.5 34.4 %all-to-all-start = ((f32[16,4,8,128]{3,2,1,0:T(8,128)}), f32[16,4,8,128]{3,2,1,0:T(8,128)}, u32[]{:S(2)}, u32[]{:S(2)}) async-start(f32[16,4,8,128]{3,2,1,0:T(8,128)} %get-tuple-element.34), calls=%async_computation | async-start | bytes 524288 | tf_op jit(solution)/shard_map/all_to_all | solution.py:608
  50.6 1.0 copy-start.3
  51.6 1.6 %copy-start.8 = (f32[2,4,64,8,128]{4,3,2,1,0:T(8,128)S(1)}, f32[2,4,64,8,128]{4,3,2,1,0:T(8,128)}, u32[]{:S(2)}) copy-start(f32[2,4,64,8,128]{4,3,2,1,0:T(8,128)} %copy-done.7) | copy-start | bytes 6291460
  69.9 1.0 copy-start.20
  70.9 1.0 copy-start.24
  73.9 30.4 %all-to-all-start.3 = ((f32[16,4,8,128]{3,2,1,0:T(8,128)}), f32[16,4,8,128]{3,2,1,0:T(8,128)}, u32[]{:S(2)}, u32[]{:S(2)}) async-start(f32[16,4,8,128]{3,2,1,0:T(8,128)} %copy-done.48), calls=%async_computation.3 | async-start | bytes 524288 | tf_op jit(solution)/shard_map/all_to_all | solution.py:649
  79.8 1.0 copy-start.4
  80.9 1.6 %copy-start.9 = (f32[2,4,64,8,128]{4,3,2,1,0:T(8,128)S(1)}, f32[2,4,64,8,128]{4,3,2,1,0:T(8,128)}, u32[]{:S(2)}) copy-start(f32[2,4,64,8,128]{4,3,2,1,0:T(8,128)} %copy-done.7) | copy-start | bytes 6291460
  83.4 1.0 copy-start.15
  84.4 1.0 copy-start.17
  100.8 1.0 copy-start.18
  101.9 1.0 copy-start.22
  104.2 20.7 %all-to-all-start.2 = ((f32[16,4,8,128]{3,2,1,0:T(8,128)}), f32[16,4,8,128]{3,2,1,0:T(8,128)S(1)}, u32[]{:S(2)}, u32[]{:S(2)}) async-start(f32[16,4,8,128]{3,2,1,0:T(8,128)} %copy-done.47), calls=%async_computation.2 | async-start | bytes 524288 | tf_op jit(solution)/shard_map/all_to_all | solution.py:649
  110.2 1.0 copy-start.5
  111.2 1.3 copy-start.21
  112.5 1.2 copy-start.25
  116.0 8.9 %copy-start.6 = (f32[65,2,8,128]{3,2,1,0:T(8,128)S(1)}, f32[65,2,8,128]{3,2,1,0:T(8,128)}, u32[]{:S(2)}) copy-start(f32[65,2,8,128]{3,2,1,0:T(8,128)} %copy-done.2) | copy-start | bytes 1597444
  116.0 8.9 %copy-start.19 = (f32[2,2,70,8,128]{4,3,2,1,0:T(8,128)S(1)}, f32[2,2,70,8,128]{4,3,2,1,0:T(8,128)}, u32[]{:S(2)}) copy-start(f32[2,2,70,8,128]{4,3,2,1,0:T(8,128)} %copy-done.18) | copy-start | bytes 3440644
  116.0 8.9 %copy-start.31 = (f32[6,8,128]{2,1,0:T(8,128)S(1)}, f32[6,8,128]{2,1,0:T(8,128)}, u32[]{:S(2)}) copy-start(f32[6,8,128]{2,1,0:T(8,128)} %copy-done.26) | copy-start | bytes 73732
  116.0 8.9 %copy-start.39 = (f32[2,6,8,128]{3,2,1,0:T(8,128)S(1)}, f32[2,6,8,128]{3,2,1,0:T(8,128)}, u32[]{:S(2)}) copy-start(f32[2,6,8,128]{3,2,1,0:T(8,128)} %copy-done.36) | copy-start | bytes 147460
  125.0 1.2 copy-start.23
  (35 other events, 26.1 us)

commit v2 on v0

v2 whole, which is shorter than its diff:
```python
import functools

import jax
import jax.numpy as jnp
from jax import lax
from jax.experimental import pallas as pl
from jax.experimental.pallas import tpu as pltpu
from jax.sharding import PartitionSpec as P

relax_weight = 0.8
shift_ratio = 0.5
damping = 3.0
coupling = 0.25
keep = 1.0 - relax_weight

DEEP = 6
UNROLL = 4
PIECES = 4


def cmul(a, b):
    return a[0] * b[0] - a[1] * b[1], a[0] * b[1] + a[1] * b[0]


def add(a, b):
    return a[0] + b[0], a[1] + b[1]


def scale(c, a):
    return c * a[0], c * a[1]


def pick(cond, a, b):
    return jnp.where(cond, a[0], b[0]), jnp.where(cond, a[1], b[1])


def tile_of(ref, *at):
    return ref[at + (0,)], ref[at + (1,)]


class Inward:
    def __init__(self, source, target, sem):
        self.ref = target
        self.copy = pltpu.make_async_copy(source, target, sem)
        self.copy.start()

    def wait(self):
        self.copy.wait()
        return self.ref


def kernel_call(body, inputs, outputs, scratch=(), pieces=0, cost=0, name=None):
    n_in, n_out = len(inputs), len(outputs)
    extra = []
    for array, place in inputs:
        if place != "hbm":
            space = pltpu.SMEM if place == "smem" else pltpu.VMEM
            extra.append(space(array.shape, array.dtype))
    for shape, place in outputs:
        if place != "hbm":
            extra.append(pltpu.VMEM(shape, jnp.float32))
    n_extra = len(extra)

    def kernel(*refs):
        ins, outs = refs[:n_in], refs[n_in : n_in + n_out]
        buffers = iter(refs[n_in + n_out : n_in + n_out + n_extra])
        sems = refs[n_in + n_out + n_extra]
        rest = refs[n_in + n_out + n_extra + 1 :]
        used = iter(range(n_extra + pieces))
        pending = []

        def start(source, target):
            return Inward(source, target, sems.at[next(used)])

        def send(source, target):
            pending.append(start(source, target))

        def arrive():
            given = []
            for ref, (_, place) in zip(ins, inputs):
                given.append(ref if place == "hbm" else start(ref, next(buffers)))
            return given

        given = arrive()
        made = []
        for ref, (_, place) in zip(outs, outputs):
            if place == "hbm":
                made.append(ref)
            else:
                buffer = next(buffers)
                made.append((buffer, functools.partial(send, buffer, ref)))
        body(start, send, given, made, rest)
        for copy in pending:
            copy.wait()

    anywhere = pl.BlockSpec(memory_space=pl.ANY)
    return pl.pallas_call(
        kernel,
        out_shape=tuple(jax.ShapeDtypeStruct(s, jnp.float32) for s, _ in outputs),
        in_specs=[anywhere] * n_in,
        out_specs=(anywhere,) * n_out,
        scratch_shapes=[
            *extra,
            pltpu.SemaphoreType.DMA((n_extra + pieces,)),
            *scratch,
        ],
        compiler_params=pltpu.CompilerParams(vmem_limit_bytes=62 << 20),
        cost_estimate=pl.CostEstimate(
            flops=cost, bytes_accessed=4 << 20, transcendentals=0
        ),
        name=name,
    )(*[array for array, _ in inputs])


class Field:
    def __init__(self, ref, first, height):
        self.ref, self.first, self.height = ref, first, height

    @staticmethod
    def shape(count, planes, tile):
        return pltpu.VMEM((2, count, (2 * planes + 1) * tile[0], tile[1]), jnp.float32)

    def rows(self, plane, shift=0):
        start = (2 * (plane - self.first) + 1) * self.height + shift
        if shift % self.height == 0:
            start = pl.multiple_of(start, self.height)
        return pl.ds(start, self.height)

    def clear(self):
        edge = self.ref[:, :, : self.height]
        self.ref[:, :, : self.height] = jnp.zeros_like(edge)

    def get(self, part, plane, shift=0):
        return self.ref[part, :, self.rows(plane, shift)]

    def both(self, plane):
        return self.get(0, plane), self.get(1, plane)

    def put(self, part, plane, value):
        self.ref[part, :, self.rows(plane)] = value
        self.ref[part, :, self.rows(plane, self.height)] = jnp.zeros_like(value)

    def put_both(self, plane, value):
        for part in range(2):
            self.put(part, plane, value[part])

    def bump(self, plane, s, value):
        for part in range(2):
            self.ref[part, s, self.rows(plane)] += value[part]

    def around(self, plane, masks):
        heres, totals = [], []
        for part in range(2):
            here = self.get(part, plane)
            breadth = here.shape[-1]
            lanes = here.ndim - 1
            ahead = jnp.where(masks[0], pltpu.roll(here, 1, lanes), 0.0)
            behind = jnp.where(masks[1], pltpu.roll(here, breadth - 1, lanes), 0.0)
            beside = self.get(part, plane, -1) + self.get(part, plane, 1)
            depth = self.get(part, plane - 1) + self.get(part, plane + 1)
            heres.append(here)
            totals.append((beside + depth) + (ahead + behind))
        return tuple(heres), tuple(totals)

    def minus_a(self, plane, diagonal, layer3, masks):
        here, total = self.around(plane, masks)
        return (
            (total[0] - diagonal * here[0]) + layer3 * here[1],
            (total[1] - diagonal * here[1]) - layer3 * here[0],
        )


def lane_masks(tile):
    lane = lax.broadcasted_iota(jnp.int32, tile, 1)
    return lane > 0, lane < tile[1] - 1


def coefficients(squared, layer):
    diagonal = 6.0 - squared
    imag = shift_ratio * squared + damping * layer
    size = diagonal * diagonal + imag * imag
    return diagonal, (relax_weight * diagonal / size, -relax_weight * imag / size)


def wave(absorb, squared, slab):
    size = jnp.exp(-absorb / slab)
    angle = jnp.sqrt(squared)
    return size * jnp.cos(angle), size * jnp.sin(angle)


def region_values(labels, kk_ref):
    squared = jnp.zeros(labels.shape, jnp.float32)
    for region in range(kk_ref.shape[0]):
        squared = jnp.where(labels == region, kk_ref[region], squared)
    return squared


def loop(start, stop, body, carry, unroll=UNROLL):
    trips = (stop - start) // unroll

    def several(trip, carry):
        for i in range(unroll):
            carry = body(start + trip * unroll + i, carry)
        return carry

    if trips > 1:
        carry = lax.fori_loop(0, trips, several, carry)
        start += trips * unroll
    for plane in range(start, stop):
        carry = body(plane, carry)
    return carry


def cuts(planes):
    edges = [planes * i // PIECES for i in range(PIECES + 1)]
    return list(zip(edges[:-1], edges[1:]))


def start_kernel(start, send, given, made, rest):
    plan, kk, damp, sources, absorb, labels, guess = given
    residual, (emits, emits_out), (media, media_out), (power, power_out) = made
    loaded, held, ref = rest
    _, count, slab, height, breadth = guess.shape
    tile = (height, breadth)
    copies = []
    edges = [0] + [min(b + 1, slab) for _, b in cuts(slab)]
    for a, b in zip(edges[:-1], edges[1:]):
        part = pl.ds(a, b - a)
        copies.append(start(guess.at[:, :, part], loaded.at[:, :, part]))
    masks = lane_masks(tile)
    field = Field(ref, -1, height)
    zero = jnp.zeros((count,) + tile, jnp.float32)
    field.clear()
    field.put_both(-1, (zero, zero))
    field.put_both(slab, (zero, zero))

    plan, kk, damp = plan.wait(), kk.wait(), damp.wait()
    row = lax.broadcasted_iota(jnp.int32, tile, 0)
    lane = lax.broadcasted_iota(jnp.int32, tile, 1)
    cell = row * breadth + lane

    def mark(i, hit):
        return jnp.where(cell == damp[i], 1.0, hit)

    layer = loop(0, damp.shape[0], mark, jnp.zeros(tile, jnp.float32), 16)
    sources, absorb, labels = sources.wait(), absorb.wait(), labels.wait()
    squared = region_values(labels[0], kk)
    diagonal, inverse = coefficients(squared, layer)
    layer3 = damping * layer
    factor = wave(absorb[0], squared, slab)
    for i, value in enumerate((*inverse, diagonal, layer3, *factor)):
        media[i] = value
    media_out()

    def load(p):
        for part in range(2):
            field.put(part, p, loaded[part, :, p])

    def plane(k, carry):
        toward_next, toward_prev, w = carry
        power[k, 0], power[k, 1] = w
        r = field.minus_a(k, diagonal, layer3, masks)
        for part in range(2):
            held[part, :, k] = r[part]
        toward_next = add(cmul(factor, toward_next), r)
        toward_prev = add(toward_prev, cmul(w, r))
        return toward_next, toward_prev, cmul(factor, w)

    one = jnp.ones(tile, jnp.float32), jnp.zeros(tile, jnp.float32)
    carry = ((zero, zero), (zero, zero), one)
    for (a, b), copy in zip(cuts(slab), copies):
        copy.wait()
        if a == 0:
            load(0)
        top = min(b, slab - 1)

        def group(trip, carry):
            for i in range(UNROLL):
                load(a + trip * UNROLL + i + 1)
            for i in range(UNROLL):
                carry = plane(a + trip * UNROLL + i, carry)
            return carry

        trips = (top - a) // UNROLL
        carry = lax.fori_loop(0, trips, group, carry)
        for k in range(a + trips * UNROLL, b):
            if k + 1 < slab:
                load(k + 1)
            carry = plane(k, carry)
        part = pl.ds(a, b - a)
        send(held.at[:, :, part], residual.at[:, :, part])
    toward_next, toward_prev, w = carry
    power[slab, 0], power[slab, 1] = w
    power_out()
    for part in range(2):
        emits[0, part] = toward_next[part]
        emits[1, part] = toward_prev[part]
    force_emits(plan, 0, emits, sources, power, slab)
    emits_out()


def force_emits(plan, shift, emits, sources, power, slab):
    first_plane = lax.axis_index("depth") * slab
    for s in range(sources.shape[1]):
        k = plan[s] - first_plane

        @pl.when((k >= 0) & (k < slab))
        def _():
            src = sources[0, s], sources[1, s]
            onward = cmul(tile_of(power, slab - 1 - k), src)
            back = cmul(tile_of(power, k), src)
            for part in range(2):
                emits[0, part, s] += onward[part]
                emits[1, part, s] += back[part]


def fill_send(send, full, passage):
    place = lax.axis_index("depth")
    count = full.shape[2]

    def one(j, unused):
        way = jnp.where(j > place, 0, 1)
        for part in range(2):
            send[j, pl.ds(part * count, count)] = full[way, part]
        if passage is not None:
            send[j, 2 * count] = passage[0]
            send[j, 2 * count + 1] = passage[1]
        return unused

    loop(0, send.shape[0], one, 0, 4)


def arrange_kernel(start, send, given, made, rest):
    got_even, got_odd, emits, power = given
    (full, full_out), (slots, slots_out) = made
    (weights,) = rest
    slab = power.shape[0] - 1
    copy = start(power.at[pl.ds(slab - 1, 2)], weights)
    even = lax.rem(lax.axis_index("depth"), 2) == 0
    got_even, got_odd, emits = got_even.wait(), got_odd.wait(), emits.wait()
    copy.wait()
    count = emits.shape[2]
    weight = tile_of(weights, 0)
    for s in range(count):
        at = [(part * count + s) * DEEP for part in range(2)]
        low = tuple(
            jnp.where(even, got_odd[i + DEEP - 1], got_even[i + DEEP - 1]) for i in at
        )
        high = tuple(jnp.where(even, got_even[i], got_odd[i]) for i in at)
        toward_next = add(add(cmul(weight, low), high), (emits[0, 0, s], emits[0, 1, s]))
        toward_prev = add(add(cmul(weight, high), low), (emits[1, 0, s], emits[1, 1, s]))
        for part in range(2):
            full[0, part, s] = toward_next[part]
            full[1, part, s] = toward_prev[part]
    fill_send(slots, full, tile_of(weights, 1))
    slots_out()
    full_out()


def prepare_kernel(start, send, given, made, rest):
    plan, kk, got_even, got_odd, sources, media, guess = given
    (near, near_out), (res, res_out), (near_media, media_out), (waves, waves_out) = made
    ends, ref = rest
    _, count, slab, height, breadth = guess.shape
    tile = (height, breadth)
    copies = [
        start(guess.at[:, :, slab - 1 if end else 0], ends.at[end]) for end in range(2)
    ]
    plan, kk = plan.wait(), kk.wait()
    got_even, got_odd = got_even.wait(), got_odd.wait()
    sources, media = sources.wait(), media.wait()
    masks = lane_masks(tile)
    place = lax.axis_index("depth")
    last_place = lax.axis_size("depth") - 1
    even = lax.rem(place, 2) == 0
    tiles = 2 * count * DEEP
    layer3 = media[3]
    layer = layer3 / damping
    factors, diagonals = [], []
    for side in range(2):
        first, second = (got_odd, got_even) if side == 0 else (got_even, got_odd)
        for i in range(2 * count):
            rows = pl.ds(i * DEEP, DEEP)
            near[side, i // count, i % count] = jnp.where(
                even, first[rows], second[rows]
            )
        absorb = jnp.where(even, first[tiles], second[tiles])
        labels = jnp.where(even, first[tiles + 1], second[tiles + 1]).astype(jnp.int32)
        squared = region_values(labels, kk)
        diagonal, inverse = coefficients(squared, layer)
        inside = (place > 0) if side == 0 else (place < last_place)
        inverse = tuple(jnp.where(inside, v, 0.0) for v in inverse)
        factor = wave(absorb, squared, slab)
        for i, value in enumerate((*inverse, diagonal, layer3, *factor)):
            near_media[side, i] = value
        factors.append(factor)
        diagonals.append(diagonal)
    near_out()
    media_out()

    ws = list(factors)
    edge = DEEP - 1

    def keep_power(k, ws):
        for side in range(2):
            for way in range(2):
                if side == way:
                    i = k - (slab - edge + 1)
                    i = edge - 1 - i if side else i
                else:
                    i = k - 1
                    i = i if side else edge - 1 - i
                if 0 <= i < edge:
                    for part in range(2):
                        waves[side, way, i, part] = ws[side][part]

    def next_power(k, ws):
        return tuple(cmul(factors[side], ws[side]) for side in range(2))

    k = 1
    while k <= slab:
        if edge < k < slab - edge + 1:
            ws = loop(k, slab - edge + 1, next_power, tuple(ws), 8)
            k = slab - edge + 1
        keep_power(k, ws)
        ws = next_power(k, ws)
        k += 1
    waves_out()
    for copy in copies:
        copy.wait()
    for side in range(2):
        field = Field(ref, 0, height)
        field.clear()
        for i in range(DEEP + 1):
            for part in range(2):
                if side == 0:
                    value = near[0, part, :, i] if i < DEEP else ends[0, part]
                else:
                    value = near[1, part, :, i - 1] if i > 0 else ends[1, part]
                field.put(part, i, value)
        for i in range(1, DEEP):
            r = field.minus_a(i, diagonals[side], layer3, masks)
            for part in range(2):
                res[side, part, :, i - 1] = r[part]
    for s in range(count):
        k = plan[s] - place * slab
        for side, low in ((0, -edge), (1, slab)):
            i = k - low

            @pl.when((i >= 0) & (i < edge))
            def _():
                for part in range(2):
                    res[side, part, s, i] += sources[part, s]

    res_out()


def incoming_waves(got, passages, full, passage):
    place = lax.axis_index("depth")
    last_place = lax.axis_size("depth") - 1
    count = full.shape[2]
    zero = jnp.zeros(full.shape[2:], jnp.float32)

    def step(j, state):
        came = got[j, pl.ds(0, count)], got[j, pl.ds(count, count)]
        return add(cmul(passages(j), state), came)

    below = jnp.maximum(place - 1, 0)
    above = jnp.minimum(place + 1, last_place)
    next_low = lax.fori_loop(0, below, step, (zero, zero))
    next_own = pick(place > 0, step(below, next_low), (zero, zero))
    prev_high = lax.fori_loop(
        0, last_place - above, lambda t, state: step(last_place - t, state), (zero, zero)
    )
    prev_own = pick(place < last_place, step(above, prev_high), (zero, zero))
    next_high = add(cmul(passage, next_own), (full[0, 0], full[0, 1]))
    prev_low = add(cmul(passage, prev_own), (full[1, 0], full[1, 1]))
    return [
        (scale(coupling, a), scale(coupling, b))
        for a, b in ((next_low, prev_low), (next_own, prev_own), (next_high, prev_high))
    ]


def update_passes(
    reach, slab, tile, incoming, residual_of, media, near_media, power, waves,
    refs, ready, after_first, emit, done, masks,
):
    edge = DEEP - 1
    first_update = Field(refs[0], -reach, tile[0])
    second_update = Field(refs[1], 1 - reach, tile[0])
    first_update.clear()
    second_update.clear()
    own = lambda p: (tile_of(power, p + 1), tile_of(power, slab - p))
    low = lambda p: (tile_of(waves, 0, 0, p + edge), tile_of(waves, 0, 1, p + edge))
    high = lambda p: (tile_of(waves, 1, 0, p - slab), tile_of(waves, 1, 1, p - slab))
    sides = (
        (-reach, 0, near_media.at[0], low, incoming[0]),
        (0, slab, media, own, incoming[1]),
        (slab, slab + reach, near_media.at[1], high, incoming[2]),
    )

    def begin(which, p):
        _, _, m, powers, (onward, back) = sides[which]
        on, off = powers(p)
        c = add(cmul(on, onward), cmul(off, back))
        first_update.put_both(p, cmul((m[0], m[1]), add(c, residual_of(which, p))))

    for which in (0, 2):
        for p in range(*sides[which][:2]):
            begin(which, p)
    for piece, (a, b) in enumerate(cuts(slab)):
        ready(piece)
        loop(a, b, lambda p, unused: begin(1, p) or unused, 0)
    after_first(first_update)

    def second(m, p):
        here, total = first_update.around(p, masks)
        u = add(scale(1.0 + keep, here), cmul((m[0], m[1]), total))
        second_update.put_both(p, u)

    def third(which, m, p):
        here, total = second_update.around(p, masks)
        u = add(scale(keep, here), cmul((m[0], m[1]), total))
        emit(which, p, add(u, first_update.both(p)))

    for which, (a, b, m, *_) in enumerate(sides):
        a, b = max(a, 1 - reach), min(b, slab + reach - 1)
        loop(a, b, lambda p, unused: second(m, p) or unused, 0)
    for which, (a, b, m, *_) in enumerate(sides):
        a, b = max(a, 2 - reach), min(b, slab + reach - 2)
        spans = cuts(slab) if which == 1 else [(a, b)]
        for piece, (a, b) in enumerate(spans):
            loop(a, b, lambda p, unused: third(which, m, p) or unused, 0)
            if which == 1:
                done(piece)


def middle_kernel(start, send, given, made, rest):
    (
        plan, got, full, sources, media, near_media, waves, near, near_residual, power,
        residual, guess,
    ) = given
    new_field, new_residual, (next_full, full_out), (slots, slots_out) = made
    held, loaded, next_held, *refs = rest
    _, count, slab, height, breadth = guess.shape
    tile = (height, breadth)
    halves = [pl.ds(a, b - a) for a, b in cuts(slab)]
    res_copies = [start(residual.at[:, :, h], held.at[:, :, h]) for h in halves]
    field_copies = [start(guess.at[:, :, h], loaded.at[:, :, h]) for h in halves]
    masks = lane_masks(tile)
    place = lax.axis_index("depth")
    reach = DEEP - 1
    ext = reach - 2
    more = ext - 1
    new = Field(refs[2], -ext, height)
    new.clear()
    plan, got, full, sources = plan.wait(), got.wait(), full.wait(), sources.wait()
    media, near_media, waves = media.wait(), near_media.wait(), waves.wait()
    near, near_residual, power = near.wait(), near_residual.wait(), power.wait()
    incoming = incoming_waves(
        got, lambda j: (got[j, 2 * count], got[j, 2 * count + 1]), full, tile_of(power, slab)
    )

    def residual_of(which, p):
        if which == 1:
            return held[0, :, p], held[1, :, p]
        i = p + reach if which == 0 else p - slab
        return near_residual[which // 2, 0, :, i], near_residual[which // 2, 1, :, i]

    def ready(piece):
        res_copies[piece].wait()

    def after_first(update):
        inverse = media[0], media[1]
        for side, (p, i) in enumerate(((0, DEEP - 1), (slab - 1, 0))):
            lacks = cmul(inverse, (near[side, 0, :, i], near[side, 1, :, i]))
            update.put_both(p, add(update.both(p), lacks))
        for s in range(count):
            k = plan[s] - place * slab

            @pl.when((k >= 0) & (k < slab))
            def _():
                update.bump(k, s, cmul(inverse, (sources[0, s], sources[1, s])))

        for copy in field_copies:
            copy.wait()

    def emit(which, p, u):
        for part in range(2):
            if which == 1:
                value = loaded[part, :, p] + u[part]
                loaded[part, :, p] = value
            else:
                i = p + DEEP if which == 0 else p - slab
                value = near[which // 2, part, :, i] + u[part]
            new.put(part, p, value)

    def done(piece):
        send(loaded.at[:, :, halves[piece]], new_field.at[:, :, halves[piece]])

    update_passes(
        reach, slab, tile, incoming, residual_of, media, near_media, power, waves,
        refs, ready, after_first, emit, done, masks,
    )

    layer3 = media[3]
    factor = media[4], media[5]

    def outside(side):
        def one(p, unused):
            r = new.minus_a(p, near_media[side, 2], layer3, masks)
            for part in range(2):
                next_held[part, :, p + more] = r[part]
            return unused

        return one

    loop(-more, 0, outside(0), 0)
    loop(slab, slab + more, outside(1), 0)
    diagonal = media[2]

    def inside(p, carry):
        toward_next, toward_prev = carry
        r = new.minus_a(p, diagonal, layer3, masks)
        for part in range(2):
            next_held[part, :, p + more] = r[part]
        toward_next = add(cmul(factor, toward_next), r)
        toward_prev = add(toward_prev, cmul(tile_of(power, p), r))
        return toward_next, toward_prev

    zero = jnp.zeros((count,) + tile, jnp.float32)
    carry = ((zero, zero), (zero, zero))
    for piece, (a, b) in enumerate(cuts(slab)):
        carry = loop(a, b, inside, carry)
        low = a + more if piece else 0
        high = b + more if piece < PIECES - 1 else slab + 2 * more
        part = pl.ds(low, high - low)
        send(next_held.at[:, :, part], new_residual.at[:, :, part])
    for way in range(2):
        for part in range(2):
            next_full[way, part] = carry[way][part]
    force_emits(plan, 0, next_full, sources, power, slab)
    fill_send(slots, next_full, None)
    slots_out()
    full_out()


def final_kernel(start, send, given, made, rest):
    (
        plan, got, full, sources, media, near_media, waves, power, passages,
        residual, field,
    ) = given
    (out,) = made
    passage_of, held, loaded, *refs = rest
    _, count, slab, height, breadth = field.shape
    tile = (height, breadth)
    copy = start(passages.at[:, pl.ds(2 * count, 2)], passage_of)
    halves = [pl.ds(a, b - a) for a, b in cuts(slab)]
    reach = 2
    res_copies = []
    for piece, (a, b) in enumerate(cuts(slab)):
        low = a + reach if piece else 0
        high = b + reach if piece < PIECES - 1 else slab + 2 * reach
        part = pl.ds(low, high - low)
        res_copies.append(start(residual.at[:, :, part], held.at[:, :, part]))
    field_copies = [start(field.at[:, :, h], loaded.at[:, :, h]) for h in halves]
    masks = lane_masks(tile)
    place = lax.axis_index("depth")
    plan, got, full, sources = plan.wait(), got.wait(), full.wait(), sources.wait()
    media, near_media, waves = media.wait(), near_media.wait(), waves.wait()
    power = power.wait()
    copy.wait()
    incoming = incoming_waves(
        got, lambda j: tile_of(passage_of, j), full, tile_of(power, slab)
    )
    for copy in (res_copies[0], res_copies[-1]):
        copy.wait()

    def residual_of(which, p):
        return held[0, :, p + reach], held[1, :, p + reach]

    def ready(piece):
        if 0 < piece < PIECES - 1:
            res_copies[piece].wait()

    def after_first(update):
        for s in range(count):
            k = plan[s] - place * slab
            src = sources[0, s], sources[1, s]
            for m, a, b in (
                (media, 0, slab),
                (near_media.at[0], -reach, 0),
                (near_media.at[1], slab, slab + reach),
            ):

                @pl.when((k >= a) & (k < b))
                def _():
                    update.bump(k, s, cmul((m[0], m[1]), src))

        for copy in field_copies:
            copy.wait()

    def emit(which, p, u):
        for part in range(2):
            loaded[part, :, p] += u[part]

    def done(piece):
        send(loaded.at[:, :, halves[piece]], out.at[:, :, halves[piece]])

    update_passes(
        reach, slab, tile, incoming, residual_of, media, near_media, power, waves,
        refs, ready, after_first, emit, done, masks,
    )


def local(sources, plan, absorb, labels, region_kk, damp_cells, guess):
    size = lax.axis_size("depth")
    place = lax.axis_index("depth")
    _, count, slab, height, breadth = guess.shape
    tile = (height, breadth)
    edge = DEEP - 1
    planes = lambda n: (2, count, n) + tile
    scratch = lambda shape: pltpu.VMEM(shape, jnp.float32)

    even = place % 2 == 0
    top = slab - DEEP

    def payload(first):
        part = lax.dynamic_slice_in_dim(guess, first, DEEP, axis=2)
        return jnp.concatenate(
            [part.reshape((-1,) + tile), absorb, labels.astype(jnp.float32)], axis=0
        )

    even_pairs = [(i, i ^ 1) for i in range(size) if i ^ 1 < size]
    odd_pairs = [(i, i + 1) for i in range(1, size - 1, 2)]
    odd_pairs += [(b, a) for a, b in odd_pairs]
    got_odd = lax.ppermute(payload(jnp.where(even, 0, top)), "depth", odd_pairs)
    got_even = lax.ppermute(payload(jnp.where(even, top, 0)), "depth", even_pairs)

    residual, emits, media, power = kernel_call(
        start_kernel,
        [
            (plan, "smem"), (region_kk, "smem"), (damp_cells, "smem"),
            (sources, "vmem"), (absorb, "vmem"), (labels, "vmem"), (guess, "hbm"),
        ],
        [
            (planes(slab), "hbm"), ((2, 2, count) + tile, "vmem"),
            ((6,) + tile, "vmem"), ((slab + 1, 2) + tile, "vmem"),
        ],
        [scratch(planes(slab)), scratch(planes(slab)), Field.shape(count, slab + 2, tile)],
        pieces=2 * PIECES, cost=20_000_000, name="start",
    )
    full, slots = kernel_call(
        arrange_kernel,
        [(got_even, "vmem"), (got_odd, "vmem"), (emits, "vmem"), (power, "hbm")],
        [((2, 2, count) + tile, "vmem"), ((size, 2 * count + 2) + tile, "vmem")],
        [scratch((2, 2) + tile)],
        pieces=1, cost=1_000_000, name="arrange",
    )
    first_got = lax.all_to_all(slots, "depth", 0, 0)
    near, near_residual, near_media, waves = kernel_call(
        prepare_kernel,
        [
            (plan, "smem"), (region_kk, "smem"), (got_even, "vmem"), (got_odd, "vmem"),
            (sources, "vmem"), (media, "vmem"), (guess, "hbm"),
        ],
        [
            ((2, 2, count, DEEP) + tile, "vmem"), ((2, 2, count, edge) + tile, "vmem"),
            ((2, 6) + tile, "vmem"), ((2, 2, edge, 2) + tile, "vmem"),
        ],
        [scratch((2, 2, count) + tile), Field.shape(count, DEEP + 1, tile)],
        pieces=2, cost=4_000_000, name="prepare",
    )
    new_field, new_residual, next_full, slots = kernel_call(
        middle_kernel,
        [
            (plan, "smem"), (first_got, "vmem"), (full, "vmem"), (sources, "vmem"),
            (media, "vmem"), (near_media, "vmem"), (waves, "vmem"), (near, "vmem"),
            (near_residual, "vmem"), (power, "vmem"), (residual, "hbm"), (guess, "hbm"),
        ],
        [
            (planes(slab), "hbm"), (planes(slab + 2 * (DEEP - 4)), "hbm"),
            ((2, 2, count) + tile, "vmem"), ((size, 2 * count) + tile, "vmem"),
        ],
        [
            scratch(planes(slab)), scratch(planes(slab)),
            scratch(planes(slab + 2 * (DEEP - 4))),
            Field.shape(count, slab + 2 * edge, tile),
            Field.shape(count, slab + 2 * edge - 2, tile),
            Field.shape(count, slab + 2 * edge - 4, tile),
        ],
        pieces=4 * PIECES, cost=80_000_000, name="middle",
    )
    got = lax.all_to_all(slots, "depth", 0, 0)
    (out,) = kernel_call(
        final_kernel,
        [
            (plan, "smem"), (got, "vmem"), (next_full, "vmem"), (sources, "vmem"),
            (media, "vmem"), (near_media, "vmem"), (waves, "vmem"), (power, "vmem"),
            (first_got, "hbm"), (new_residual, "hbm"), (new_field, "hbm"),
        ],
        [(planes(slab), "hbm")],
        [
            scratch((size, 2) + tile),
            scratch(planes(slab + 2 * (DEEP - 4))), scratch(planes(slab)),
            Field.shape(count, slab + 4, tile), Field.shape(count, slab + 2, tile),
        ],
        pieces=3 * PIECES + 1, cost=60_000_000, name="final",
    )
    return out


def solution(mesh):
    return jax.shard_map(
        local,
        mesh=mesh,
        in_specs=(
            P(None, "groups", None, None),
            P("groups"),
            P("depth", "groups", None),
            P("depth", "groups", None),
            P(),
            P("groups"),
            P(None, "groups", "depth", None, None),
        ),
        out_specs=P(None, "groups", "depth", None, None),
        check_vma=False,
    )
```

time: 242 us -> 78.6 us (0.32)
  the two profiles are of different devices: /device:TPU:25 before, /device:TPU:0 now
where the time goes in v2:
time: 78.6 us; the launch traced here: 78.1 us
  Pallas kernels  29.9 us (38%)
  blocking collectives  19.1 us (24%)
  waiting for transfers between devices  14.2 us (18%)
  starting transfers between devices  10.9 us (14%)
  local copies, waits for them, and re-layouts  2.63 us (3%)
  other arithmetic  1.41 us (2%)
    pallas_call x5, Pallas kernels, kernel_call(): pl.pallas_call(kernel, out_shape=tuple((jax.ShapeDtypeStruct(s, jnp.float...  29.9 us
    all_to_all x1, blocking collectives, local(): got = lax.all_to_all(slots, 'depth', 0, 0)  19.1 us
    all_to_all x1, waiting for transfers between devices, local(): first_got = lax.all_to_all(slots, 'depth', 0, 0)  14.2 us
    all_to_all x1, starting transfers between devices, local(): first_got = lax.all_to_all(slots, 'depth', 0, 0)  5.88 us
    ppermute x1, starting transfers between devices, local(): lax.ppermute(payload(jnp.where(even, top, 0)), 'depth', even_pairs)  4.38 us
    unnamed x6, local copies, waits for them, and re-layouts  1.58 us
  transfers between devices with their start and end apart: 3, of which 1 were waited for; matrix products, arithmetic and copies ran while one was open for 0% of the time, Pallas kernels for 9%

profile of v2, /device:TPU:0, one launch (start us, length us, event | category | flops | bytes accessed | tf_op | source)
XLA Modules:
  0.0 78.1 jit_solution(10027613244155692469)
XLA Ops:
  0.0 0.7 convert_element_type.4
  0.7 1.0 %constant_dynamic-slice_fusion = (f32[2,4,6,8,128]{4,3,2,1,0:T(8,128)S(1)}, f32[2,4,6,8,128]{4,3,2,1,0:T(8,128)S(1)}) fusion(f32[2,4,64,8,128]{4,3,2,1,0:T(8,128)} %refs_11_.1, s32[]{:T(128)S(6)} %select_n.18, s32[]{:T(128)S(6)} %select_n.17), kind=kLoop, calls=%fused_computation.4 | loop fusion | bytes 786440 | tf_op jit(solution)/shard_map/dynamic_slice | solution.py:729
  1.7 0.7 pad_maximum_fusion
  2.5 0.7 collective-permute-start.1
  3.1 4.4 %collective-permute-start = (f32[50,8,128]{2,1,0:T(8,128)S(1)}, f32[50,8,128]{2,1,0:T(8,128)S(1)}, u32[]{:S(2)}, u32[]{:S(2)}) collective-permute-start(f32[50,8,128]{2,1,0:T(8,128)S(1)} %get-tuple-element.36), channel_id=1, source_target_pairs={{0,1},{1,0},{2,3},{3,2},{4,5},{5,4},{6,7},{7,6},{8,9},{9,8},{10,11... | collective-permute-start | bytes 614408 | tf_op jit(solution)/shard_map/ppermute | solution.py:738
  7.5 4.7 %start.1 = (f32[2,4,64,8,128]{4,3,2,1,0:T(8,128)}, f32[2,2,4,8,128]{4,3,2,1,0:T(8,128)}, f32[6,8,128]{2,1,0:T(8,128)}, f32[65,2,8,128]{3,2,1,0:T(8,128)}) custom-call(s32[4]{0:T(128)} %refs_0_.7, f32[8]{0:T(128)} %refs_1_.3, s32[128]{0:T(128)} %refs_2_.1, f32[2,4,8,128]{3,2,1,0:T(8,128)} %refs_3_.5, f32[1,8,128]{2,1,0:T(8,128)} %refs_4_.2, ...), custom_call_target="tpu_custom_call" | custom-call | flops 20000000 | bytes 4194304 | tf_op jit(solution)/shard_map/start/pallas_call | solution.py:97
  12.2 0.0 collective-permute-done.1.refs_1_.refs_3_
  12.2 0.0 copy-start.1
  12.3 0.0 collective-permute-done.refs_0_.refs_2_
  12.3 0.0 copy-start.2
  12.3 0.6 copy-done.1
  12.9 0.1 copy-done.2
  13.0 2.0 %arrange.1 = (f32[2,2,4,8,128]{4,3,2,1,0:T(8,128)}, f32[16,10,8,128]{3,2,1,0:T(8,128)}) custom-call(f32[50,8,128]{2,1,0:T(8,128)} %copy-done.2, f32[50,8,128]{2,1,0:T(8,128)} %copy-done.1, f32[2,2,4,8,128]{4,3,2,1,0:T(8,128)} %get-tuple-element.19.refs_2_, f32[65,2,8,128]{3,2,1,0:T(8,128)} %get-tuple-element.20.refs_3_.refs_9_.refs_7_), custom_call_target="tpu_custom_call" | custom-call | flops 1000000 | bytes 4194304 | tf_op jit(solution)/shard_map/arrange/pallas_call | solution.py:97
  15.0 5.9 %all-to-all-start = ((f32[16,10,8,128]{3,2,1,0:T(8,128)}), f32[16,10,8,128]{3,2,1,0:T(8,128)S(1)}, u32[]{:S(2)}, u32[]{:S(2)}) async-start(f32[16,10,8,128]{3,2,1,0:T(8,128)} %get-tuple-element.21), calls=%async_computation | async-start | bytes 1310720 | tf_op jit(solution)/shard_map/all_to_all | solution.py:760
  20.9 2.4 %prepare.1 = (f32[2,2,4,6,8,128]{5,4,3,2,1,0:T(8,128)}, f32[2,2,4,5,8,128]{5,4,3,2,1,0:T(8,128)}, f32[2,6,8,128]{3,2,1,0:T(8,128)}, f32[2,2,5,2,8,128]{5,4,3,2,1,0:T(8,128)}) custom-call(s32[4]{0:T(128)} %refs_0_.7, f32[8]{0:T(128)} %refs_1_.3, f32[50,8,128]{2,1,0:T(8,128)} %copy-done.2, f32[50,8,128]{2,1,0:T(8,128)} %copy-done.1, f32[2,4,8,128]{3,2,1,0:T(8,128)} %refs_3_.5, ...), custom_call_target="tpu_custom_call" | custom-call | flops 4000000 | bytes 4194304 | tf_op jit(solution)/shard_map/prepare/pallas_call | solution.py:97
  23.3 14.2 %all-to-all-done.refs_1_.refs_8_ = f32[16,10,8,128]{3,2,1,0:T(8,128)S(1)} async-done(((f32[16,10,8,128]{3,2,1,0:T(8,128)}), f32[16,10,8,128]{3,2,1,0:T(8,128)S(1)}, u32[]{:S(2)}, u32[]{:S(2)}) %all-to-all-start) | async-done | bytes 655392 | tf_op jit(solution)/shard_map/all_to_all | solution.py:760
  37.5 0.0 copy-start
  37.5 0.9 %copy-done = f32[16,10,8,128]{3,2,1,0:T(8,128)} copy-done((f32[16,10,8,128]{3,2,1,0:T(8,128)}, f32[16,10,8,128]{3,2,1,0:T(8,128)S(1)}, u32[]{:S(2)}) %copy-start) | copy-done | bytes 655384
  38.3 11.8 %middle.1 = (f32[2,4,64,8,128]{4,3,2,1,0:T(8,128)}, f32[2,4,68,8,128]{4,3,2,1,0:T(8,128)}, f32[2,2,4,8,128]{4,3,2,1,0:T(8,128)}, f32[16,8,8,128]{3,2,1,0:T(8,128)}) custom-call(s32[4]{0:T(128)} %refs_0_.7, f32[16,10,8,128]{3,2,1,0:T(8,128)} %copy-done, f32[2,2,4,8,128]{4,3,2,1,0:T(8,128)} %get-tuple-element.22.refs_2_, f32[2,4,8,128]{3,2,1,0:T(8,128)} %refs_3_.5, ...), custom_call_target="tpu_custom_call" | custom-call | flops 80000000 | bytes 4194304 | tf_op jit(solution)/shard_map/middle/pallas_call | solution.py:97
  50.1 19.1 %all_to_all.10.refs_1_ = f32[16,8,8,128]{3,2,1,0:T(8,128)} all-to-all(f32[16,8,8,128]{3,2,1,0:T(8,128)} %get-tuple-element.29), channel_id=1, replica_groups=mesh['groups'=2,'depth'=16] {'depth'}, dimensions={0} | all-to-all | bytes 1048576 | tf_op jit(solution)/shard_map/all_to_all | solution.py:794
  69.2 9.0 %final.1 = f32[2,4,64,8,128]{4,3,2,1,0:T(8,128)} custom-call(s32[4]{0:T(128)} %refs_0_.7, f32[16,8,8,128]{3,2,1,0:T(8,128)} %all_to_all.10.refs_1_, f32[2,2,4,8,128]{4,3,2,1,0:T(8,128)} %get-tuple-element.30.refs_2_, f32[2,4,8,128]{3,2,1,0:T(8,128)} %refs_3_.5, f32[6,8,128]{2,1,0:T(8,128)} %get-tuple-element.23.refs_5_.refs_4_, ...), custom_call_target="tpu_custom_call" | custom-call | flops 60000000 | bytes 4194304 | tf_op jit(solution)/shard_map/final/pallas_call | solution.py:97
Async XLA Ops:
  2.5 9.8 %collective-permute-start.1 = (f32[50,8,128]{2,1,0:T(8,128)S(1)}, f32[50,8,128]{2,1,0:T(8,128)S(1)}, u32[]{:S(2)}, u32[]{:S(2)}) collective-permute-start(f32[50,8,128]{2,1,0:T(8,128)S(1)} %get-tuple-element.35), channel_id=1, source_target_pairs={{1,2},{3,4},{5,6},{7,8},{9,10},{11,12},{13,14},{2,1},{4,3},{6,5},{... | collective-permute-start | bytes 614408 | tf_op jit(solution)/shard_map/ppermute | solution.py:737
  3.1 9.1 %collective-permute-start = (f32[50,8,128]{2,1,0:T(8,128)S(1)}, f32[50,8,128]{2,1,0:T(8,128)S(1)}, u32[]{:S(2)}, u32[]{:S(2)}) collective-permute-start(f32[50,8,128]{2,1,0:T(8,128)S(1)} %get-tuple-element.36), channel_id=1, source_target_pairs={{0,1},{1,0},{2,3},{3,2},{4,5},{5,4},{6,7},{7,6},{8,9},{9,8},{10,11... | collective-permute-start | bytes 614408 | tf_op jit(solution)/shard_map/ppermute | solution.py:738
  12.2 0.7 copy-start.1
  12.3 0.7 copy-start.2
  15.0 22.5 %all-to-all-start = ((f32[16,10,8,128]{3,2,1,0:T(8,128)}), f32[16,10,8,128]{3,2,1,0:T(8,128)S(1)}, u32[]{:S(2)}, u32[]{:S(2)}) async-start(f32[16,10,8,128]{3,2,1,0:T(8,128)} %get-tuple-element.21), calls=%async_computation | async-start | bytes 1310720 | tf_op jit(solution)/shard_map/all_to_all | solution.py:760
  37.5 0.9 %copy-start = (f32[16,10,8,128]{3,2,1,0:T(8,128)}, f32[16,10,8,128]{3,2,1,0:T(8,128)S(1)}, u32[]{:S(2)}) copy-start(f32[16,10,8,128]{3,2,1,0:T(8,128)S(1)} %all-to-all-done.refs_1_.refs_8_) | copy-start | bytes 1966084

commit v3 on v2

v3 whole, which is shorter than its diff:
```python
import functools

import jax
import jax.numpy as jnp
from jax import lax
from jax.experimental import pallas as pl
from jax.experimental.pallas import tpu as pltpu
from jax.sharding import PartitionSpec as P

relax_weight = 0.8
shift_ratio = 0.5
damping = 3.0
coupling = 0.25
keep = 1.0 - relax_weight

DEEP = 6
UNROLL = 4
PIECES = 4


def cmul(a, b):
    return a[0] * b[0] - a[1] * b[1], a[0] * b[1] + a[1] * b[0]


def add(a, b):
    return a[0] + b[0], a[1] + b[1]


def scale(c, a):
    return c * a[0], c * a[1]


def pick(cond, a, b):
    return jnp.where(cond, a[0], b[0]), jnp.where(cond, a[1], b[1])


def tile_of(ref, *at):
    return ref[at + (0,)], ref[at + (1,)]


class Inward:
    def __init__(self, source, target, sem):
        self.ref = target
        self.copy = pltpu.make_async_copy(source, target, sem)
        self.copy.start()

    def wait(self):
        self.copy.wait()
        return self.ref


def kernel_call(body, inputs, outputs, scratch=(), pieces=0, cost=0, name=None, limit=62):
    n_in, n_out = len(inputs), len(outputs)
    extra = []
    for array, place in inputs:
        if place in ("vmem", "smem"):
            space = pltpu.SMEM if place == "smem" else pltpu.VMEM
            extra.append(space(array.shape, array.dtype))
    for shape, place in outputs:
        if place == "vmem":
            extra.append(pltpu.VMEM(shape, jnp.float32))
    n_extra = len(extra)

    def kernel(*refs):
        ins, outs = refs[:n_in], refs[n_in : n_in + n_out]
        buffers = iter(refs[n_in + n_out : n_in + n_out + n_extra])
        sems = refs[n_in + n_out + n_extra]
        rest = refs[n_in + n_out + n_extra + 1 :]
        used = iter(range(n_extra + pieces))
        pending = []

        def start(source, target):
            return Inward(source, target, sems.at[next(used)])

        def send(source, target):
            pending.append(start(source, target))

        def arrive():
            given = []
            for ref, (_, place) in zip(ins, inputs):
                copied = place in ("vmem", "smem")
                given.append(start(ref, next(buffers)) if copied else ref)
            return given

        given = arrive()
        made = []
        for ref, (_, place) in zip(outs, outputs):
            if place != "vmem":
                made.append(ref)
            else:
                buffer = next(buffers)
                made.append((buffer, functools.partial(send, buffer, ref)))
        body(start, send, given, made, rest)
        for copy in pending:
            copy.wait()

    def spec(place):
        return pl.BlockSpec(memory_space=pltpu.VMEM if place == "direct" else pl.ANY)

    return pl.pallas_call(
        kernel,
        out_shape=tuple(jax.ShapeDtypeStruct(s, jnp.float32) for s, _ in outputs),
        in_specs=[spec(place) for _, place in inputs],
        out_specs=tuple(spec(place) for _, place in outputs),
        scratch_shapes=[
            *extra,
            pltpu.SemaphoreType.DMA((max(1, n_extra + pieces),)),
            *scratch,
        ],
        compiler_params=pltpu.CompilerParams(vmem_limit_bytes=limit << 20),
        cost_estimate=pl.CostEstimate(
            flops=cost, bytes_accessed=4 << 20, transcendentals=0
        ),
        name=name,
    )(*[array for array, _ in inputs])


def lane_sum(here, masks):
    breadth = here.shape[-1]
    axis = here.ndim - 1
    ahead = jnp.where(masks[0], pltpu.roll(here, 1, axis), 0.0)
    behind = jnp.where(masks[1], pltpu.roll(here, breadth - 1, axis), 0.0)
    return ahead + behind


class Field:
    def __init__(self, ref, first, height):
        self.ref, self.first, self.height = ref, first, height

    @staticmethod
    def shape(count, planes, tile):
        return pltpu.VMEM((2, count, (2 * planes + 1) * tile[0], tile[1]), jnp.float32)

    def rows(self, plane, shift=0):
        start = (2 * (plane - self.first) + 1) * self.height + shift
        if shift % self.height == 0:
            start = pl.multiple_of(start, self.height)
        return pl.ds(start, self.height)

    def clear(self):
        edge = self.ref[:, :, : self.height]
        self.ref[:, :, : self.height] = jnp.zeros_like(edge)

    def get(self, part, plane, shift=0):
        return self.ref[part, :, self.rows(plane, shift)]

    def both(self, plane):
        return self.get(0, plane), self.get(1, plane)

    def put(self, part, plane, value):
        self.ref[part, :, self.rows(plane)] = value
        self.ref[part, :, self.rows(plane, self.height)] = jnp.zeros_like(value)

    def put_both(self, plane, value):
        for part in range(2):
            self.put(part, plane, value[part])

    def bump(self, plane, s, value):
        for part in range(2):
            self.ref[part, s, self.rows(plane)] += value[part]

    def lanes(self, part, plane, masks):
        return lane_sum(self.get(part, plane), masks)

    def around(self, plane, lanes):
        heres, totals = [], []
        for part in range(2):
            here = self.get(part, plane)
            beside = self.get(part, plane, -1) + self.get(part, plane, 1)
            depth = self.get(part, plane - 1) + self.get(part, plane + 1)
            heres.append(here)
            totals.append((beside + depth) + lanes(part, plane))
        return tuple(heres), tuple(totals)

    def minus_a(self, plane, diagonal, layer3, lanes):
        here, total = self.around(plane, lanes)
        return (
            (total[0] - diagonal * here[0]) + layer3 * here[1],
            (total[1] - diagonal * here[1]) - layer3 * here[0],
        )


class Lanes:
    def __init__(self, field, ref, masks):
        self.field, self.ref, self.masks = field, ref, masks

    def now(self, part, plane):
        return self.field.lanes(part, plane, self.masks)

    def kept(self, part, plane):
        return self.ref[part, :, plane]

    def fill(self, plane):
        for part in range(2):
            self.ref[part, :, plane] = self.now(part, plane)

    def sweep(self, start, stop, total, body, carry, before=None):
        trips = (stop - start) // UNROLL
        assert trips * UNROLL == stop - start

        def group(base, carry, ahead):
            if before is not None:
                for i in range(UNROLL):
                    before(base + i)
            if ahead:
                for i in range(UNROLL):
                    self.fill(base + UNROLL + i)
            for i in range(UNROLL):
                carry = body(base + i, carry)
            return carry

        ahead = trips if stop < total else trips - 1
        carry = lax.fori_loop(
            0, ahead, lambda t, c: group(start + t * UNROLL, c, True), carry
        )
        if ahead < trips:
            carry = group(stop - UNROLL, carry, False)
        return carry


def lane_masks(tile):
    lane = lax.broadcasted_iota(jnp.int32, tile, 1)
    return lane > 0, lane < tile[1] - 1


INVERSE, DIAGONAL, LAYER, WAVE, SECOND, THIRD, MEDIA = 0, 2, 3, 4, 6, 8, 10


def set_media(ref, squared, layer, absorb, slab, inside=None):
    diagonal = 6.0 - squared
    imag = shift_ratio * squared + damping * layer
    size = diagonal * diagonal + imag * imag
    inverse = relax_weight * diagonal / size, -relax_weight * imag / size
    if inside is not None:
        inverse = tuple(jnp.where(inside, v, 0.0) for v in inverse)
    grow = 1.0 + keep
    decay = jnp.exp(-absorb / slab)
    angle = jnp.sqrt(squared)
    factor = decay * jnp.cos(angle), decay * jnp.sin(angle)
    values = (
        *inverse, diagonal, damping * layer, *factor,
        *scale(1.0 / grow, inverse), *scale(grow, inverse),
    )
    for i, value in enumerate(values):
        ref[i] = value
    return factor


def pair(ref, i):
    return ref[i], ref[i + 1]


def region_values(labels, kk_ref):
    squared = jnp.zeros(labels.shape, jnp.float32)
    for region in range(kk_ref.shape[0]):
        squared = jnp.where(labels == region, kk_ref[region], squared)
    return squared


def loop(start, stop, body, carry, unroll=UNROLL):
    trips = (stop - start) // unroll

    def several(trip, carry):
        for i in range(unroll):
            carry = body(start + trip * unroll + i, carry)
        return carry

    if trips > 1:
        carry = lax.fori_loop(0, trips, several, carry)
        start += trips * unroll
    for plane in range(start, stop):
        carry = body(plane, carry)
    return carry


def cuts(planes, pieces=PIECES):
    edges = [planes * i // pieces for i in range(pieces + 1)]
    return list(zip(edges[:-1], edges[1:]))


def start_kernel(start, send, given, made, rest):
    plan, kk, damp, sources, absorb, labels, guess = given
    residual, (emits, emits_out), (media, media_out), (power, power_out) = made
    loaded, held, side, ref = rest
    _, count, slab, height, breadth = guess.shape
    tile = (height, breadth)
    copies = []
    edges = [0] + [min(b + UNROLL, slab) for _, b in cuts(slab)]
    for a, b in zip(edges[:-1], edges[1:]):
        part = pl.ds(a, b - a)
        copies.append(start(guess.at[:, :, part], loaded.at[:, :, part]))
    masks = lane_masks(tile)
    field = Field(ref, -1, height)
    zero = jnp.zeros((count,) + tile, jnp.float32)
    field.clear()
    field.put_both(-1, (zero, zero))
    field.put_both(slab, (zero, zero))
    lanes = Lanes(field, side, masks)

    def fill(p):
        for part in range(2):
            value = loaded[part, :, p]
            field.put(part, p, value)
            side[part, :, p] = lane_sum(value, masks)

    lanes.fill = fill

    plan, kk, damp = plan.wait(), kk.wait(), damp.wait()
    row = lax.broadcasted_iota(jnp.int32, tile, 0)
    lane = lax.broadcasted_iota(jnp.int32, tile, 1)
    cell = row * breadth + lane

    def mark(i, hit):
        return jnp.where(cell == damp[i], 1.0, hit)

    layer = loop(0, damp.shape[0], mark, jnp.zeros(tile, jnp.float32), 16)
    sources, absorb, labels = sources.wait(), absorb.wait(), labels.wait()
    squared = region_values(labels[0], kk)
    factor = set_media(media, squared, layer, absorb[0], slab)
    diagonal, layer3 = media[DIAGONAL], media[LAYER]
    media_out()

    def plane(k, carry):
        toward_next, toward_prev, w = carry
        power[k, 0], power[k, 1] = w
        r = field.minus_a(k, diagonal, layer3, lanes.kept)
        for part in range(2):
            held[part, :, k] = r[part]
        toward_next = add(cmul(factor, toward_next), r)
        toward_prev = add(toward_prev, cmul(w, r))
        return toward_next, toward_prev, cmul(factor, w)

    one = jnp.ones(tile, jnp.float32), jnp.zeros(tile, jnp.float32)
    carry = ((zero, zero), (zero, zero), one)
    for (a, b), copy in zip(cuts(slab), copies):
        copy.wait()
        if a == 0:
            for p in range(UNROLL):
                fill(p)
        carry = lanes.sweep(a, b, slab, plane, carry)
        part = pl.ds(a, b - a)
        send(held.at[:, :, part], residual.at[:, :, part])
    toward_next, toward_prev, w = carry
    power[slab, 0], power[slab, 1] = w
    power_out()
    for part in range(2):
        emits[0, part] = toward_next[part]
        emits[1, part] = toward_prev[part]
    force_emits(plan, emits, sources, power, slab)
    emits_out()


def force_emits(plan, emits, sources, power, slab):
    first_plane = lax.axis_index("depth") * slab
    for s in range(sources.shape[1]):
        k = plan[s] - first_plane

        @pl.when((k >= 0) & (k < slab))
        def _():
            src = sources[0, s], sources[1, s]
            onward = cmul(tile_of(power, slab - 1 - k), src)
            back = cmul(tile_of(power, k), src)
            for part in range(2):
                emits[0, part, s] += onward[part]
                emits[1, part, s] += back[part]


def halves(count):
    return (0, count // 2), (count // 2, count)


def fill_send(slots, full, passage):
    place = lax.axis_index("depth")

    def one(chip, unused):
        for core, (a, b) in enumerate(halves(full.shape[2])):
            j = 2 * chip + core
            way = jnp.where(j > place, 0, 1)
            for part in range(2):
                slots[j, pl.ds(part * (b - a), b - a)] = full[way, part, a:b]
            if passage is not None:
                slots[j, 2 * (b - a)] = passage[0]
                slots[j, 2 * (b - a) + 1] = passage[1]
        return unused

    loop(0, slots.shape[0] // 2, one, 0, 4)


def arrange_kernel(start, send, given, made, rest):
    got_even, got_odd, emits, power = given
    (full, full_out), (slots, slots_out), (near, near_out), (extra, extra_out) = made
    (weights,) = rest
    slab = power.shape[0] - 1
    copy = start(power.at[pl.ds(slab - 1, 2)], weights)
    even = lax.rem(lax.axis_index("depth"), 2) == 0
    emits = emits.wait()
    copy.wait()
    count = emits.shape[2]
    weight = tile_of(weights, 0)
    for s in range(count):
        at = [(part * count + s) * DEEP for part in range(2)]
        low = tuple(
            jnp.where(even, got_odd[i + DEEP - 1], got_even[i + DEEP - 1]) for i in at
        )
        high = tuple(jnp.where(even, got_even[i], got_odd[i]) for i in at)
        toward_next = add(add(cmul(weight, low), high), (emits[0, 0, s], emits[0, 1, s]))
        toward_prev = add(add(cmul(weight, high), low), (emits[1, 0, s], emits[1, 1, s]))
        for part in range(2):
            full[0, part, s] = toward_next[part]
            full[1, part, s] = toward_prev[part]
    fill_send(slots, full, tile_of(weights, 1))
    slots_out()
    full_out()
    for side in range(2):
        first, second = (got_odd, got_even) if side == 0 else (got_even, got_odd)
        for i in range(2 * count):
            rows = pl.ds(i * DEEP, DEEP)
            near[side, i // count, i % count] = jnp.where(
                even, first[rows], second[rows]
            )
        for i in range(2):
            at = 2 * count * DEEP + i
            extra[side, i] = jnp.where(even, first[at], second[at])
    near_out()
    extra_out()


def prepare_kernel(start, send, given, made, rest):
    plan, kk, near, extra, sources, media, guess = given
    (res, res_out), (near_media, media_out), (waves, waves_out) = made
    ends, ref = rest
    _, count, slab, height, breadth = guess.shape
    tile = (height, breadth)
    copies = [
        start(guess.at[:, :, slab - 1 if end else 0], ends.at[end]) for end in range(2)
    ]
    plan, kk = plan.wait(), kk.wait()
    near, extra = near.wait(), extra.wait()
    sources, media = sources.wait(), media.wait()
    masks = lane_masks(tile)
    place = lax.axis_index("depth")
    last_place = lax.axis_size("depth") - 1
    layer3 = media[LAYER]
    layer = layer3 / damping
    factors = []
    for side in range(2):
        squared = region_values(extra[side, 1].astype(jnp.int32), kk)
        inside = (place > 0) if side == 0 else (place < last_place)
        factors.append(
            set_media(near_media.at[side], squared, layer, extra[side, 0], slab, inside)
        )
    media_out()

    ws = list(factors)
    edge = DEEP - 1

    def keep_power(k, ws):
        for side in range(2):
            for way in range(2):
                if side == way:
                    i = k - (slab - edge + 1)
                    i = edge - 1 - i if side else i
                else:
                    i = k - 1
                    i = i if side else edge - 1 - i
                if 0 <= i < edge:
                    for part in range(2):
                        waves[side, way, i, part] = ws[side][part]

    def next_power(k, ws):
        return tuple(cmul(factors[side], ws[side]) for side in range(2))

    k = 1
    while k <= slab:
        if edge < k < slab - edge + 1:
            ws = loop(k, slab - edge + 1, next_power, tuple(ws), 8)
            k = slab - edge + 1
        keep_power(k, ws)
        ws = next_power(k, ws)
        k += 1
    waves_out()
    for copy in copies:
        copy.wait()
    for side in range(2):
        field = Field(ref, 0, height)
        field.clear()
        for i in range(DEEP + 1):
            for part in range(2):
                if side == 0:
                    value = near[0, part, :, i] if i < DEEP else ends[0, part]
                else:
                    value = near[1, part, :, i - 1] if i > 0 else ends[1, part]
                field.put(part, i, value)
        lanes = Lanes(field, None, masks)
        for i in range(1, DEEP):
            r = field.minus_a(i, near_media[side, DIAGONAL], layer3, lanes.now)
            for part in range(2):
                res[side, part, :, i - 1] = r[part]
    for s in range(count):
        k = plan[s] - place * slab
        for side, low in ((0, -edge), (1, slab)):
            i = k - low

            @pl.when((i >= 0) & (i < edge))
            def _():
                for part in range(2):
                    res[side, part, s, i] += sources[part, s]

    res_out()


def chain_kernel(at, start, send, given, made, rest):
    got, passages, full = given
    mine, theirs = made
    full = full.wait()
    place = lax.axis_index("depth")
    last_place = lax.axis_size("depth") - 1
    count = full.shape[2]
    even = lax.rem(place, 2) == 0
    low = place - lax.rem(place, 2)
    high = low + 1
    (a, b), (c, d) = halves(count)
    width = b - a
    zero = jnp.zeros((width,) + full.shape[3:], jnp.float32)
    passage = lambda j: (passages[j, at], passages[j, at + 1])
    emit = lambda way: tuple(
        jnp.where(even, full[way, part, a:b], full[way, part, c:d]) for part in range(2)
    )
    came = lambda j: (got[j, pl.ds(0, width)], got[j, pl.ds(width, width)])

    def step(j, state):
        return add(cmul(passage(j), state), came(j))

    below = jnp.maximum(low - 1, 0)
    above = jnp.minimum(high + 1, last_place)
    next_before = lax.fori_loop(0, below, step, (zero, zero))
    next_low = pick(low > 0, step(below, next_before), (zero, zero))
    next_high = add(cmul(passage(low), next_low), pick(even, emit(0), came(low)))
    prev_after = lax.fori_loop(
        0, last_place - above, lambda t, state: step(last_place - t, state), (zero, zero)
    )
    prev_high = pick(high < last_place, step(above, prev_after), (zero, zero))
    prev_low = add(cmul(passage(high), prev_high), pick(even, came(high), emit(1)))
    for_low = next_before, next_low, prev_low, prev_high
    for_high = next_low, next_high, prev_high, prev_after
    for i in range(4):
        own, other = pick(even, for_low[i], for_high[i]), pick(even, for_high[i], for_low[i])
        for part in range(2):
            mine[i, part] = own[part]
            theirs[i, part] = other[part]


def set_incoming(ref, mine, theirs, full, passage):
    even = lax.rem(lax.axis_index("depth"), 2) == 0
    count = full.shape[2]
    spots = ((0, 0), (1, 0), (1, 1), (2, 1))
    for half, (a, b) in enumerate(halves(count)):
        own = even if half == 0 else jnp.logical_not(even)
        waves = [
            tuple(jnp.where(own, mine[i, part], theirs[i, part]) for part in range(2))
            for i in range(4)
        ]
        here = lambda way: (full[way, 0, a:b], full[way, 1, a:b])
        onward = add(cmul(passage, waves[1]), here(0))
        back = add(cmul(passage, waves[2]), here(1))
        for (side, way), value in zip(
            spots + ((2, 0), (0, 1)), [*waves, onward, back]
        ):
            for part in range(2):
                ref[side, way, part, a:b] = coupling * value[part]


def update_passes(
    reach, slab, tile, incoming, residual_of, media, near_media, power, waves,
    refs, side_ref, ready, after_first, emit, pieces, done, masks,
):
    edge = DEEP - 1
    first_update = Field(refs[0], -reach, tile[0])
    second_update = Field(refs[1], 1 - reach, tile[0])
    first_update.clear()
    second_update.clear()
    own = lambda p: (tile_of(power, p + 1), tile_of(power, slab - p))
    low = lambda p: (tile_of(waves, 0, 0, p + edge), tile_of(waves, 0, 1, p + edge))
    high = lambda p: (tile_of(waves, 1, 0, p - slab), tile_of(waves, 1, 1, p - slab))
    sides = (
        (-reach, 0, near_media.at[0], low),
        (0, slab, media, own),
        (slab, slab + reach, near_media.at[1], high),
    )

    def begin(which, p):
        _, _, m, powers = sides[which]
        on, off = powers(p)
        onward = incoming[which, 0, 0], incoming[which, 0, 1]
        back = incoming[which, 1, 0], incoming[which, 1, 1]
        c = add(cmul(on, onward), cmul(off, back))
        first_update.put_both(p, cmul(pair(m, INVERSE), add(c, residual_of(which, p))))

    for which in (0, 2):
        for p in range(*sides[which][:2]):
            begin(which, p)
    for piece, (a, b) in enumerate(cuts(slab)):
        ready(piece)
        loop(a, b, lambda p, unused: begin(1, p) or unused, 0)
    after_first(first_update)

    def smooth(field, margin, body, own_pieces, own_done):
        lanes = Lanes(field, side_ref, masks)
        for p in range(UNROLL):
            lanes.fill(p)
        for which in (0, 2, 1):
            a, b, m, _ = sides[which]
            a, b = max(a, margin - reach), min(b, slab + reach - margin)
            if which != 1:
                for p in range(a, b):
                    body(which, m, p, lanes.now)
                continue
            for piece, (a, b) in enumerate(cuts(slab, own_pieces)):
                lanes.sweep(
                    a, b, slab, lambda p, c: body(1, media, p, lanes.kept) or c, 0
                )
                own_done(piece)

    def second(which, m, p, lanes):
        here, total = first_update.around(p, lanes)
        second_update.put_both(p, add(here, cmul(pair(m, SECOND), total)))

    def third(which, m, p, lanes):
        here, total = second_update.around(p, lanes)
        u = add(scale(keep * (1.0 + keep), here), cmul(pair(m, THIRD), total))
        emit(which, p, add(u, first_update.both(p)))

    smooth(first_update, 1, second, 1, lambda piece: None)
    smooth(second_update, 2, third, pieces, done)


def middle_kernel(start, send, given, made, rest):
    (
        mine, theirs, plan, full, sources, media, near_media, waves, near,
        near_residual, power, residual, guess,
    ) = given
    new_field, new_residual, (next_full, full_out), (slots, slots_out) = made
    held, loaded, next_held, incoming, side_ref, *refs = rest
    _, count, slab, height, breadth = guess.shape
    tile = (height, breadth)
    spans = [pl.ds(a, b - a) for a, b in cuts(slab)]
    res_copies = [start(residual.at[:, :, h], held.at[:, :, h]) for h in spans]
    field_copies = [start(guess.at[:, :, h], loaded.at[:, :, h]) for h in spans]
    masks = lane_masks(tile)
    place = lax.axis_index("depth")
    reach = DEEP - 1
    ext = reach - 2
    more = ext - 1
    new = Field(refs[2], -ext, height)
    new.clear()
    plan, full, sources = plan.wait(), full.wait(), sources.wait()
    media, near_media, waves = media.wait(), near_media.wait(), waves.wait()
    near, near_residual, power = near.wait(), near_residual.wait(), power.wait()
    set_incoming(incoming, mine, theirs, full, tile_of(power, slab))

    def residual_of(which, p):
        if which == 1:
            return held[0, :, p], held[1, :, p]
        i = p + reach if which == 0 else p - slab
        return near_residual[which // 2, 0, :, i], near_residual[which // 2, 1, :, i]

    def ready(piece):
        res_copies[piece].wait()

    def after_first(update):
        inverse = pair(media, INVERSE)
        for side, (p, i) in enumerate(((0, DEEP - 1), (slab - 1, 0))):
            lacks = cmul(inverse, (near[side, 0, :, i], near[side, 1, :, i]))
            update.put_both(p, add(update.both(p), lacks))
        for s in range(count):
            k = plan[s] - place * slab

            @pl.when((k >= 0) & (k < slab))
            def _():
                update.bump(k, s, cmul(inverse, (sources[0, s], sources[1, s])))

        for copy in field_copies:
            copy.wait()

    def emit(which, p, u):
        for part in range(2):
            if which == 1:
                value = loaded[part, :, p] + u[part]
                loaded[part, :, p] = value
            else:
                i = p + DEEP if which == 0 else p - slab
                value = near[which // 2, part, :, i] + u[part]
            new.put(part, p, value)

    def done(piece):
        send(loaded, new_field)

    update_passes(
        reach, slab, tile, incoming, residual_of, media, near_media, power, waves,
        refs, side_ref, ready, after_first, emit, 1, done, masks,
    )

    layer3 = media[LAYER]
    factor = pair(media, WAVE)
    lanes = Lanes(new, side_ref, masks)
    for p in range(UNROLL):
        lanes.fill(p)

    def put(p, r):
        for part in range(2):
            next_held[part, :, p + more] = r[part]

    for p in range(-more, 0):
        put(p, new.minus_a(p, near_media[0, DIAGONAL], layer3, lanes.now))
    for p in range(slab, slab + more):
        put(p, new.minus_a(p, near_media[1, DIAGONAL], layer3, lanes.now))
    diagonal = media[DIAGONAL]

    def inside(p, carry):
        toward_next, toward_prev = carry
        r = new.minus_a(p, diagonal, layer3, lanes.kept)
        put(p, r)
        toward_next = add(cmul(factor, toward_next), r)
        toward_prev = add(toward_prev, cmul(tile_of(power, p), r))
        return toward_next, toward_prev

    zero = jnp.zeros((count,) + tile, jnp.float32)
    carry = ((zero, zero), (zero, zero))
    for piece, (a, b) in enumerate(cuts(slab)):
        carry = lanes.sweep(a, b, slab, inside, carry)
        low = a + more if piece else 0
        high = b + more if piece < PIECES - 1 else slab + 2 * more
        part = pl.ds(low, high - low)
        send(next_held.at[:, :, part], new_residual.at[:, :, part])
    for way in range(2):
        for part in range(2):
            next_full[way, part] = carry[way][part]
    force_emits(plan, next_full, sources, power, slab)
    fill_send(slots, next_full, None)
    slots_out()
    full_out()


def final_kernel(start, send, given, made, rest):
    (
        mine, theirs, plan, full, sources, media, near_media, waves, power,
        residual, field,
    ) = given
    (out,) = made
    held, loaded, incoming, side_ref, *refs = rest
    _, count, slab, height, breadth = field.shape
    tile = (height, breadth)
    spans = [pl.ds(a, b - a) for a, b in cuts(slab)]
    reach = 2
    res_copies = []
    for piece, (a, b) in enumerate(cuts(slab)):
        low = a + reach if piece else 0
        high = b + reach if piece < PIECES - 1 else slab + 2 * reach
        part = pl.ds(low, high - low)
        res_copies.append(start(residual.at[:, :, part], held.at[:, :, part]))
    field_copies = [start(field.at[:, :, h], loaded.at[:, :, h]) for h in spans]
    masks = lane_masks(tile)
    place = lax.axis_index("depth")
    plan, full, sources = plan.wait(), full.wait(), sources.wait()
    media, near_media, waves = media.wait(), near_media.wait(), waves.wait()
    power = power.wait()
    set_incoming(incoming, mine, theirs, full, tile_of(power, slab))
    for copy in (res_copies[0], res_copies[-1]):
        copy.wait()

    def residual_of(which, p):
        return held[0, :, p + reach], held[1, :, p + reach]

    def ready(piece):
        if 0 < piece < PIECES - 1:
            res_copies[piece].wait()

    def after_first(update):
        for s in range(count):
            k = plan[s] - place * slab
            src = sources[0, s], sources[1, s]
            for m, a, b in (
                (media, 0, slab),
                (near_media.at[0], -reach, 0),
                (near_media.at[1], slab, slab + reach),
            ):

                @pl.when((k >= a) & (k < b))
                def _():
                    update.bump(k, s, cmul(pair(m, INVERSE), src))

        for copy in field_copies:
            copy.wait()

    def emit(which, p, u):
        for part in range(2):
            loaded[part, :, p] += u[part]

    def done(piece):
        send(loaded.at[:, :, spans[piece]], out.at[:, :, spans[piece]])

    update_passes(
        reach, slab, tile, incoming, residual_of, media, near_media, power, waves,
        refs, side_ref, ready, after_first, emit, PIECES, done, masks,
    )


def local(sources, plan, absorb, labels, region_kk, damp_cells, guess):
    size = lax.axis_size("depth")
    place = lax.axis_index("depth")
    _, count, slab, height, breadth = guess.shape
    tile = (height, breadth)
    edge = DEEP - 1
    planes = lambda n: (2, count, n) + tile
    scratch = lambda shape: pltpu.VMEM(shape, jnp.float32)

    even = place % 2 == 0
    top = slab - DEEP

    def payload(first):
        part = lax.dynamic_slice_in_dim(guess, first, DEEP, axis=2)
        return jnp.concatenate(
            [part.reshape((-1,) + tile), absorb, labels.astype(jnp.float32)], axis=0
        )

    even_pairs = [(i, i ^ 1) for i in range(size)]
    odd_pairs = [(i, i + 1) for i in range(1, size - 1, 2)]
    odd_pairs += [(b, a) for a, b in odd_pairs]
    got_odd = lax.ppermute(payload(jnp.where(even, 0, top)), "depth", odd_pairs)
    got_even = lax.ppermute(payload(jnp.where(even, top, 0)), "depth", even_pairs)

    residual, emits, media, power = kernel_call(
        start_kernel,
        [
            (plan, "smem"), (region_kk, "smem"), (damp_cells, "smem"),
            (sources, "vmem"), (absorb, "vmem"), (labels, "vmem"), (guess, "hbm"),
        ],
        [
            (planes(slab), "hbm"), ((2, 2, count) + tile, "vmem"),
            ((MEDIA,) + tile, "vmem"), ((slab + 1, 2) + tile, "vmem"),
        ],
        [
            scratch(planes(slab)), scratch(planes(slab)), scratch(planes(slab)),
            Field.shape(count, slab + 2, tile),
        ],
        pieces=2 * PIECES, cost=20_000_000, name="start",
    )
    width = count // 2
    full, slots, near, extra = kernel_call(
        arrange_kernel,
        [(got_even, "direct"), (got_odd, "direct"), (emits, "vmem"), (power, "hbm")],
        [
            ((2, 2, count) + tile, "vmem"), ((size, 2 * width + 2) + tile, "vmem"),
            ((2, 2, count, DEEP) + tile, "vmem"), ((2, 2) + tile, "vmem"),
        ],
        [scratch((2, 2) + tile)],
        pieces=1, cost=1_000_000, name="arrange", limit=16,
    )
    first_got = lax.all_to_all(slots, "depth", 0, 0)
    near_residual, near_media, waves = kernel_call(
        prepare_kernel,
        [
            (plan, "smem"), (region_kk, "smem"), (near, "vmem"), (extra, "vmem"),
            (sources, "vmem"), (media, "vmem"), (guess, "hbm"),
        ],
        [
            ((2, 2, count, edge) + tile, "vmem"), ((2, MEDIA) + tile, "vmem"),
            ((2, 2, edge, 2) + tile, "vmem"),
        ],
        [scratch((2, 2, count) + tile), Field.shape(count, DEEP + 1, tile)],
        pieces=2, cost=4_000_000, name="prepare",
    )

    def chain(got, full):
        mine, theirs = kernel_call(
            functools.partial(chain_kernel, 2 * width),
            [(got, "direct"), (first_got, "direct"), (full, "vmem")],
            [((4, 2, width) + tile, "direct")] * 2,
            cost=1_000_000, name="chain", limit=16,
        )
        return mine, lax.ppermute(theirs, "depth", even_pairs)

    mine, theirs = chain(first_got, full)
    new_field, new_residual, next_full, slots = kernel_call(
        middle_kernel,
        [
            (mine, "direct"), (theirs, "direct"),
            (plan, "smem"), (full, "vmem"), (sources, "vmem"),
            (media, "vmem"), (near_media, "vmem"), (waves, "vmem"), (near, "vmem"),
            (near_residual, "vmem"), (power, "vmem"), (residual, "hbm"), (guess, "hbm"),
        ],
        [
            (planes(slab), "hbm"), (planes(slab + 2 * (DEEP - 4)), "hbm"),
            ((2, 2, count) + tile, "vmem"), ((size, 2 * width) + tile, "vmem"),
        ],
        [
            scratch(planes(slab)), scratch(planes(slab)),
            scratch(planes(slab + 2 * (DEEP - 4))), scratch((3, 2, 2, count) + tile),
            scratch(planes(slab)),
            Field.shape(count, slab + 2 * edge, tile),
            Field.shape(count, slab + 2 * edge - 2, tile),
            Field.shape(count, slab + 2 * edge - 4, tile),
        ],
        pieces=3 * PIECES + 1, cost=80_000_000, name="middle",
    )
    mine, theirs = chain(lax.all_to_all(slots, "depth", 0, 0), next_full)
    (out,) = kernel_call(
        final_kernel,
        [
            (mine, "direct"), (theirs, "direct"),
            (plan, "smem"), (next_full, "vmem"), (sources, "vmem"),
            (media, "vmem"), (near_media, "vmem"), (waves, "vmem"), (power, "vmem"),
            (new_residual, "hbm"), (new_field, "hbm"),
        ],
        [(planes(slab), "hbm")],
        [
            scratch(planes(slab + 2 * (DEEP - 4))), scratch(planes(slab)),
            scratch((3, 2, 2, count) + tile), scratch(planes(slab)),
            Field.shape(count, slab + 4, tile), Field.shape(count, slab + 2, tile),
        ],
        pieces=3 * PIECES, cost=60_000_000, name="final",
    )
    return out


def solution(mesh):
    return jax.shard_map(
        local,
        mesh=mesh,
        in_specs=(
            P(None, "groups", None, None),
            P("groups"),
            P("depth", "groups", None),
            P("depth", "groups", None),
            P(),
            P("groups"),
            P(None, "groups", "depth", None, None),
        ),
        out_specs=P(None, "groups", "depth", None, None),
        check_vma=False,
    )
```

time: 78.6 us -> 77.5 us (0.986)
  waiting for transfers between devices: 14.2 us -> 1.26 us
  blocking collectives: 19.1 us -> 31.3 us
  starting transfers between devices: 10.9 us -> 5.17 us
  local copies, waits for them, and re-layouts: 2.63 us -> 7.56 us
    all_to_all x1 -> x0, waiting for transfers between devices: 14.2 us -> none  [local(): first_got = lax.all_to_all(slots, 'depth', 0, 0)]
    all_to_all x1 -> x2, blocking collectives: 19.1 us -> 31.3 us  [the longest x1 17.6 us: local(): first_got = lax.all_to_all(slots, 'depth', 0, 0)]
    all_to_all x1 -> x0, starting transfers between devices: 5.88 us -> none  [local(): first_got = lax.all_to_all(slots, 'depth', 0, 0)]
    unnamed x6 -> x20, local copies, waits for them, and re-layouts: 1.58 us -> 6.51 us
    ppermute x0 -> x2, waiting for transfers between devices: none -> 1.25 us  [chain(): return (mine, lax.ppermute(theirs, 'depth', even_pairs))]
    pallas_call x5 -> x7, Pallas kernels: 29.9 us -> 30 us  [kernel_call(): pl.pallas_call(kernel, out_shape=tuple((jax.ShapeDtypeStruct(s, jnp.float...]
  transfers between devices with their start and end apart: 3 -> 4, of which waited for: 1 -> 1; matrix products, arithmetic and copies ran while one was open for 0% -> 0% of each run, Pallas kernels for 9% -> 9%
where the time goes in v3:
time: 77.5 us; the launch traced here: 76.9 us
  blocking collectives  31.3 us (40%)
  Pallas kernels  30 us (39%)
  local copies, waits for them, and re-layouts  7.56 us (10%)
  starting transfers between devices  5.17 us (7%)
  other arithmetic  1.41 us (2%)
  waiting for transfers between devices  1.26 us (2%)
    pallas_call x7, Pallas kernels, kernel_call(): pl.pallas_call(kernel, out_shape=tuple((jax.ShapeDtypeStruct(s, jnp.float...  30 us
    all_to_all x1, blocking collectives, local(): first_got = lax.all_to_all(slots, 'depth', 0, 0)  17.6 us
    all_to_all x1, blocking collectives, local(): mine, theirs = chain(lax.all_to_all(slots, 'depth', 0, 0), next_full)  13.7 us
    unnamed x20, local copies, waits for them, and re-layouts  6.51 us
    ppermute x1, starting transfers between devices, local(): lax.ppermute(payload(jnp.where(even, top, 0)), 'depth', even_pairs)  4.38 us
  transfers between devices with their start and end apart: 4, of which 1 were waited for; matrix products, arithmetic and copies ran while one was open for 0% of the time, Pallas kernels for 9%

profile of v3, /device:TPU:0, one launch (start us, length us, event | category | flops | bytes accessed | tf_op | source)
XLA Modules:
  0.0 76.9 jit_solution(9012523146258577403)
XLA Ops:
  0.0 0.7 convert_element_type.4
  0.7 1.0 %constant_dynamic-slice_fusion = (f32[2,4,6,8,128]{4,3,2,1,0:T(8,128)S(1)}, f32[2,4,6,8,128]{4,3,2,1,0:T(8,128)S(1)}) fusion(f32[2,4,64,8,128]{4,3,2,1,0:T(8,128)} %refs_12_.1, s32[]{:T(128)S(6)} %select_n.18, s32[]{:T(128)S(6)} %select_n.17), kind=kLoop, calls=%fused_computation.4 | loop fusion | bytes 786440 | tf_op jit(solution)/shard_map/dynamic_slice | solution.py:821
  1.7 0.7 pad_maximum_fusion
  2.5 0.7 collective-permute-start.1
  3.1 4.4 %collective-permute-start = (f32[50,8,128]{2,1,0:T(8,128)S(1)}, f32[50,8,128]{2,1,0:T(8,128)S(1)}, u32[]{:S(2)}, u32[]{:S(2)}) collective-permute-start(f32[50,8,128]{2,1,0:T(8,128)S(1)} %get-tuple-element.46), channel_id=1, source_target_pairs={{0,1},{1,0},{2,3},{3,2},{4,5},{5,4},{6,7},{7,6},{8,9},{9,8},{10,11... | collective-permute-start | bytes 614408 | tf_op jit(solution)/shard_map/ppermute | solution.py:830
  7.5 4.9 %start.1 = (f32[2,4,64,8,128]{4,3,2,1,0:T(8,128)}, f32[2,2,4,8,128]{4,3,2,1,0:T(8,128)}, f32[10,8,128]{2,1,0:T(8,128)}, f32[65,2,8,128]{3,2,1,0:T(8,128)}) custom-call(s32[4]{0:T(128)} %refs_2_.5, f32[8]{0:T(128)} %refs_1_.3, s32[128]{0:T(128)} %refs_2_.3, f32[2,4,8,128]{3,2,1,0:T(8,128)} %refs_4_.7, f32[1,8,128]{2,1,0:T(8,128)} %refs_4_.4, ...), custom_call_target="tpu_custom_call" | custom-call | flops 20000000 | bytes 4194304 | tf_op jit(solution)/shard_map/start/pallas_call | solution.py:100
  12.4 0.0 collective-permute-done.1.refs_1_
  12.5 0.0 collective-permute-done.refs_0_
  12.5 0.0 copy-start
  12.5 1.0 %copy-done = f32[65,2,8,128]{3,2,1,0:T(8,128)S(1)} copy-done((f32[65,2,8,128]{3,2,1,0:T(8,128)S(1)}, f32[65,2,8,128]{3,2,1,0:T(8,128)}, u32[]{:S(2)}) %copy-start) | copy-done | bytes 532504
  13.5 0.8 %copy-done.6 = f32[2,2,4,8,128]{4,3,2,1,0:T(8,128)S(1)} copy-done((f32[2,2,4,8,128]{4,3,2,1,0:T(8,128)S(1)}, f32[2,2,4,8,128]{4,3,2,1,0:T(8,128)}, u32[]{:S(2)}) %copy-start.6) | copy-done | bytes 65560
  14.3 0.7 arrange.1
  15.1 0.0 copy-start.1
  15.1 0.7 copy-done.1
  15.8 0.6 copy-done.7
  16.4 17.6 %all_to_all.10.refs_0_.refs_1_ = f32[16,6,8,128]{3,2,1,0:T(8,128)S(1)} all-to-all(f32[16,6,8,128]{3,2,1,0:T(8,128)S(1)} %get-tuple-element.26), channel_id=1, replica_groups=mesh['groups'=2,'depth'=16] {'depth'}, dimensions={0} | all-to-all | bytes 786432 | tf_op jit(solution)/shard_map/all_to_all | solution.py:859
  34.0 0.2 chain.2
  34.2 0.6 copy-done.4
  34.8 0.1 collective-permute-start.2
  34.9 2.3 %prepare.1 = (f32[2,2,4,5,8,128]{5,4,3,2,1,0:T(8,128)}, f32[2,10,8,128]{3,2,1,0:T(8,128)}, f32[2,2,5,2,8,128]{5,4,3,2,1,0:T(8,128)}) custom-call(s32[4]{0:T(128)} %refs_2_.5, f32[8]{0:T(128)} %refs_1_.3, f32[2,2,4,6,8,128]{5,4,3,2,1,0:T(8,128)} %copy-done.1, f32[2,2,8,128]{3,2,1,0:T(8,128)} %copy-done.7, f32[2,4,8,128]{3,2,1,0:T(8,128)} %refs_4_.7, ...), custom_call_target="tpu_custom_call" | custom-call | flops 4000000 | bytes 4194304 | tf_op jit(solution)/shard_map/prepare/pallas_call | solution.py:100
  37.3 0.0 copy-done.2
  37.3 0.0 collective-permute-done.2.refs_1_
  37.3 0.6 copy-done.8
  37.9 12.1 %middle.1 = (f32[2,4,64,8,128]{4,3,2,1,0:T(8,128)}, f32[2,4,68,8,128]{4,3,2,1,0:T(8,128)}, f32[2,2,4,8,128]{4,3,2,1,0:T(8,128)}, f32[16,4,8,128]{3,2,1,0:T(8,128)}) custom-call(f32[4,2,2,8,128]{4,3,2,1,0:T(8,128)} %copy-done.4, f32[4,2,2,8,128]{4,3,2,1,0:T(8,128)} %copy-done.8, s32[4]{0:T(128)} %refs_2_.5, f32[2,2,4,8,128]{4,3,2,1,0:T(8,128)} %copy-done.2, ...), custom_call_target="tpu_custom_call" | custom-call | flops 80000000 | bytes 4194304 | tf_op jit(solution)/shard_map/middle/pallas_call | solution.py:100
  50.1 13.7 %all_to_all.11.refs_0_ = f32[16,4,8,128]{3,2,1,0:T(8,128)S(1)} all-to-all(f32[16,4,8,128]{3,2,1,0:T(8,128)} %get-tuple-element.37), channel_id=1, replica_groups=mesh['groups'=2,'depth'=16] {'depth'}, dimensions={0} | all-to-all | bytes 524288 | tf_op jit(solution)/shard_map/all_to_all | solution.py:906
  63.8 0.8 %copy-done.3 = f32[2,2,4,8,128]{4,3,2,1,0:T(8,128)S(1)} copy-done((f32[2,2,4,8,128]{4,3,2,1,0:T(8,128)S(1)}, f32[2,2,4,8,128]{4,3,2,1,0:T(8,128)}, u32[]{:S(2)}) %copy-start.3) | copy-done | bytes 65560
  64.6 0.2 chain.3
  64.8 0.6 copy-done.5
  65.4 0.0 collective-permute-start.3
  65.5 1.3 %collective-permute-done.3.refs_1_ = f32[4,2,2,8,128]{4,3,2,1,0:T(8,128)S(1)} collective-permute-done((f32[4,2,2,8,128]{4,3,2,1,0:T(8,128)S(1)}, f32[4,2,2,8,128]{4,3,2,1,0:T(8,128)S(1)}, u32[]{:S(2)}, u32[]{:S(2)}) %collective-permute-start.3) | collective-permute-done | bytes 65568 | tf_op jit(solution)/shard_map/ppermute | solution.py:881
  66.7 0.6 copy-done.9
  67.3 9.5 %final.1 = f32[2,4,64,8,128]{4,3,2,1,0:T(8,128)} custom-call(f32[4,2,2,8,128]{4,3,2,1,0:T(8,128)} %copy-done.5, f32[4,2,2,8,128]{4,3,2,1,0:T(8,128)} %copy-done.9, s32[4]{0:T(128)} %refs_2_.5, f32[2,2,4,8,128]{4,3,2,1,0:T(8,128)} %get-tuple-element.38.refs_2_.refs_3_, f32[2,4,8,128]{3,2,1,0:T(8,128)} %refs_4_.7, f32[10,8,128]{2,1,0:T(8,128)} %get-tuple-element.30.refs_5_, ...), custom_call_target="tpu_custom_call" | custom-call | flops 60000000 | bytes 4194304 | tf_op jit(solution)/shard_map/final/pallas_call | solution.py:100
  (8 shorter events, 0.0 us)
Async XLA Ops:
  2.5 10.0 %collective-permute-start.1 = (f32[50,8,128]{2,1,0:T(8,128)S(1)}, f32[50,8,128]{2,1,0:T(8,128)S(1)}, u32[]{:S(2)}, u32[]{:S(2)}) collective-permute-start(f32[50,8,128]{2,1,0:T(8,128)S(1)} %get-tuple-element.45), channel_id=1, source_target_pairs={{1,2},{3,4},{5,6},{7,8},{9,10},{11,12},{13,14},{2,1},{4,3},{6,5},{... | collective-permute-start | bytes 614408 | tf_op jit(solution)/shard_map/ppermute | solution.py:829
  3.1 9.3 %collective-permute-start = (f32[50,8,128]{2,1,0:T(8,128)S(1)}, f32[50,8,128]{2,1,0:T(8,128)S(1)}, u32[]{:S(2)}, u32[]{:S(2)}) collective-permute-start(f32[50,8,128]{2,1,0:T(8,128)S(1)} %get-tuple-element.46), channel_id=1, source_target_pairs={{0,1},{1,0},{2,3},{3,2},{4,5},{5,4},{6,7},{7,6},{8,9},{9,8},{10,11... | collective-permute-start | bytes 614408 | tf_op jit(solution)/shard_map/ppermute | solution.py:830
  12.5 1.0 %copy-start = (f32[65,2,8,128]{3,2,1,0:T(8,128)S(1)}, f32[65,2,8,128]{3,2,1,0:T(8,128)}, u32[]{:S(2)}) copy-start(f32[65,2,8,128]{3,2,1,0:T(8,128)} %get-tuple-element.25.refs_3_.refs_10_.refs_8_) | copy-start | bytes 1597444
  13.5 0.8 %copy-start.6 = (f32[2,2,4,8,128]{4,3,2,1,0:T(8,128)S(1)}, f32[2,2,4,8,128]{4,3,2,1,0:T(8,128)}, u32[]{:S(2)}) copy-start(f32[2,2,4,8,128]{4,3,2,1,0:T(8,128)} %get-tuple-element.24.refs_2_) | copy-start | bytes 196612
  15.1 0.7 copy-start.1
  15.8 0.6 copy-start.7
  16.4 20.9 %copy-start.2 = (f32[2,2,4,8,128]{4,3,2,1,0:T(8,128)}, f32[2,2,4,8,128]{4,3,2,1,0:T(8,128)S(1)}, u32[]{:S(2)}) copy-start(f32[2,2,4,8,128]{4,3,2,1,0:T(8,128)S(1)} %get-tuple-element.27.refs_2_.refs_3_) | copy-start | bytes 196612
  34.2 0.6 copy-start.4
  34.8 2.5 %collective-permute-start.2 = (f32[4,2,2,8,128]{4,3,2,1,0:T(8,128)S(1)}, f32[4,2,2,8,128]{4,3,2,1,0:T(8,128)S(1)}, u32[]{:S(2)}, u32[]{:S(2)}) collective-permute-start(f32[4,2,2,8,128]{4,3,2,1,0:T(8,128)S(1)} %get-tuple-element.29), channel_id=1, source_target_pairs={{0,1},{1,0},{2,3},{3,2},{4,5},{5,4},{6,7},{7,6},{8,9},{9,8},{10,11... | collective-permute-start | bytes 196616 | tf_op jit(solution)/shard_map/ppermute | solution.py:881
  37.3 0.6 copy-start.8
  63.8 0.8 %copy-start.3 = (f32[2,2,4,8,128]{4,3,2,1,0:T(8,128)S(1)}, f32[2,2,4,8,128]{4,3,2,1,0:T(8,128)}, u32[]{:S(2)}) copy-start(f32[2,2,4,8,128]{4,3,2,1,0:T(8,128)} %get-tuple-element.38.refs_2_.refs_3_) | copy-start | bytes 196612
  64.8 0.6 copy-start.5
  65.4 1.3 %collective-permute-start.3 = (f32[4,2,2,8,128]{4,3,2,1,0:T(8,128)S(1)}, f32[4,2,2,8,128]{4,3,2,1,0:T(8,128)S(1)}, u32[]{:S(2)}, u32[]{:S(2)}) collective-permute-start(f32[4,2,2,8,128]{4,3,2,1,0:T(8,128)S(1)} %get-tuple-element.40), channel_id=1, source_target_pairs={{0,1},{1,0},{2,3},{3,2},{4,5},{5,4},{6,7},{7,6},{8,9},{9,8},{10,11... | collective-permute-start | bytes 196616 | tf_op jit(solution)/shard_map/ppermute | solution.py:881
  66.7 0.6 copy-start.9

commit v4 on v3

--- a/solution.py
+++ b/solution.py
@@ -15,6 +15,7 @@
 
 DEEP = 6
 UNROLL = 4
+LAG = UNROLL + 1
 PIECES = 4
 
 
@@ -49,7 +50,7 @@
         return self.ref
 
 
-def kernel_call(body, inputs, outputs, scratch=(), pieces=0, cost=0, name=None, limit=62):
+def kernel_call(body, inputs, outputs, scratch=(), pieces=0, cost=0, name=None, limit=56):
     n_in, n_out = len(inputs), len(outputs)
     extra = []
     for array, place in inputs:
@@ -95,7 +96,7 @@
             copy.wait()
 
     def spec(place):
-        return pl.BlockSpec(memory_space=pltpu.VMEM if place == "direct" else pl.ANY)
+        return pl.BlockSpec(memory_space=pltpu.VMEM if place == "direct" else pltpu.HBM)
 
     return pl.pallas_call(
         kernel,
@@ -181,41 +182,11 @@
 
 
 class Lanes:
-    def __init__(self, field, ref, masks):
-        self.field, self.ref, self.masks = field, ref, masks
+    def __init__(self, field, masks):
+        self.field, self.masks = field, masks
 
     def now(self, part, plane):
         return self.field.lanes(part, plane, self.masks)
-
-    def kept(self, part, plane):
-        return self.ref[part, :, plane]
-
-    def fill(self, plane):
-        for part in range(2):
-            self.ref[part, :, plane] = self.now(part, plane)
-
-    def sweep(self, start, stop, total, body, carry, before=None):
-        trips = (stop - start) // UNROLL
-        assert trips * UNROLL == stop - start
-
-        def group(base, carry, ahead):
-            if before is not None:
-                for i in range(UNROLL):
-                    before(base + i)
-            if ahead:
-                for i in range(UNROLL):
-                    self.fill(base + UNROLL + i)
-            for i in range(UNROLL):
-                carry = body(base + i, carry)
-            return carry
-
-        ahead = trips if stop < total else trips - 1
-        carry = lax.fori_loop(
-            0, ahead, lambda t, c: group(start + t * UNROLL, c, True), carry
-        )
-        if ahead < trips:
-            carry = group(stop - UNROLL, carry, False)
-        return carry
 
 
 def lane_masks(tile):
@@ -278,12 +249,21 @@
     return list(zip(edges[:-1], edges[1:]))
 
 
+def media_of(pack):
+    return pack.at[pl.ds(0, MEDIA)]
+
+
+def emit_tiles(count, way, part):
+    return pl.ds(MEDIA + 4 + (2 * way + part) * count, count)
+
+
 def start_kernel(start, send, given, made, rest):
     plan, kk, damp, sources, absorb, labels, guess = given
-    residual, (emits, emits_out), (media, media_out), (power, power_out) = made
-    loaded, held, side, ref = rest
+    residual, (pack, pack_out), (power, power_out) = made
+    loaded, held, emits, ref = rest
     _, count, slab, height, breadth = guess.shape
     tile = (height, breadth)
+    media = media_of(pack)
     copies = []
     edges = [0] + [min(b + UNROLL, slab) for _, b in cuts(slab)]
     for a, b in zip(edges[:-1], edges[1:]):
@@ -295,15 +275,12 @@
     field.clear()
     field.put_both(-1, (zero, zero))
     field.put_both(slab, (zero, zero))
-    lanes = Lanes(field, side, masks)
+    lanes = Lanes(field, masks)
 
     def fill(p):
         for part in range(2):
             value = loaded[part, :, p]
             field.put(part, p, value)
-            side[part, :, p] = lane_sum(value, masks)
-
-    lanes.fill = fill
 
     plan, kk, damp = plan.wait(), kk.wait(), damp.wait()
     row = lax.broadcasted_iota(jnp.int32, tile, 0)
@@ -318,12 +295,11 @@
     squared = region_values(labels[0], kk)
     factor = set_media(media, squared, layer, absorb[0], slab)
     diagonal, layer3 = media[DIAGONAL], media[LAYER]
-    media_out()
 
     def plane(k, carry):
         toward_next, toward_prev, w = carry
         power[k, 0], power[k, 1] = w
-        r = field.minus_a(k, diagonal, layer3, lanes.kept)
+        r = field.minus_a(k, diagonal, layer3, lanes.now)
         for part in range(2):
             held[part, :, k] = r[part]
         toward_next = add(cmul(factor, toward_next), r)
@@ -335,9 +311,23 @@
     for (a, b), copy in zip(cuts(slab), copies):
         copy.wait()
         if a == 0:
-            for p in range(UNROLL):
-                fill(p)
-        carry = lanes.sweep(a, b, slab, plane, carry)
+            fill(0)
+
+        def group(trip, carry):
+            base = a + trip * UNROLL
+            for i in range(UNROLL):
+                fill(base + i + 1)
+            for i in range(UNROLL):
+                carry = plane(base + i, carry)
+            return carry
+
+        trips = (min(b, slab - 1) - a) // UNROLL
+        carry = lax.fori_loop(0, trips, group, carry)
+        for k in range(a + trips * UNROLL, b):
+            if k + 1 < slab:
+                fill(k + 1)
+            carry = plane(k, carry)
+        add_forcing(plan, held, sources, 0, slab, a, b)
         part = pl.ds(a, b - a)
         send(held.at[:, :, part], residual.at[:, :, part])
     toward_next, toward_prev, w = carry
@@ -346,8 +336,26 @@
     for part in range(2):
         emits[0, part] = toward_next[part]
         emits[1, part] = toward_prev[part]
+        pack[MEDIA + part] = power[slab - 1, part]
+        pack[MEDIA + 2 + part] = power[slab, part]
     force_emits(plan, emits, sources, power, slab)
-    emits_out()
+    for way in range(2):
+        for part in range(2):
+            pack[emit_tiles(count, way, part)] = emits[way, part]
+    pack_out()
+
+
+def add_forcing(plan, held, sources, reach, slab, low=None, high=None):
+    first_plane = lax.axis_index("depth") * slab
+    low = -reach if low is None else low
+    high = slab + reach if high is None else high
+    for s in range(sources.shape[1]):
+        k = plan[s] - first_plane
+
+        @pl.when((k >= low) & (k < high))
+        def _():
+            for part in range(2):
+                held[part, s, k + reach] += sources[part, s]
 
 
 def force_emits(plan, emits, sources, power, slab):
@@ -387,30 +395,24 @@
 
 
 def arrange_kernel(start, send, given, made, rest):
-    got_even, got_odd, emits, power = given
-    (full, full_out), (slots, slots_out), (near, near_out), (extra, extra_out) = made
-    (weights,) = rest
-    slab = power.shape[0] - 1
-    copy = start(power.at[pl.ds(slab - 1, 2)], weights)
+    got_even, got_odd, pack = given
+    full, slots, near, extra = made
     even = lax.rem(lax.axis_index("depth"), 2) == 0
-    emits = emits.wait()
-    copy.wait()
-    count = emits.shape[2]
-    weight = tile_of(weights, 0)
+    count = full.shape[2]
+    weight, passage = pair(pack, MEDIA), pair(pack, MEDIA + 2)
+    emits = [[pack[emit_tiles(count, way, part)] for part in range(2)] for way in range(2)]
     for s in range(count):
         at = [(part * count + s) * DEEP for part in range(2)]
         low = tuple(
             jnp.where(even, got_odd[i + DEEP - 1], got_even[i + DEEP - 1]) for i in at
         )
         high = tuple(jnp.where(even, got_even[i], got_odd[i]) for i in at)
-        toward_next = add(add(cmul(weight, low), high), (emits[0, 0, s], emits[0, 1, s]))
-        toward_prev = add(add(cmul(weight, high), low), (emits[1, 0, s], emits[1, 1, s]))
+        toward_next = add(add(cmul(weight, low), high), (emits[0][0][s], emits[0][1][s]))
+        toward_prev = add(add(cmul(weight, high), low), (emits[1][0][s], emits[1][1][s]))
         for part in range(2):
             full[0, part, s] = toward_next[part]
             full[1, part, s] = toward_prev[part]
-    fill_send(slots, full, tile_of(weights, 1))
-    slots_out()
-    full_out()
+    fill_send(slots, full, passage)
     for side in range(2):
         first, second = (got_odd, got_even) if side == 0 else (got_even, got_odd)
         for i in range(2 * count):
@@ -421,26 +423,19 @@
         for i in range(2):
             at = 2 * count * DEEP + i
             extra[side, i] = jnp.where(even, first[at], second[at])
-    near_out()
-    extra_out()
 
 
 def prepare_kernel(start, send, given, made, rest):
-    plan, kk, near, extra, sources, media, guess = given
-    (res, res_out), (near_media, media_out), (waves, waves_out) = made
-    ends, ref = rest
+    plan, kk, near, extra, sources, pack, guess = given
+    res, near_media, waves = made
+    (ref,) = rest
     _, count, slab, height, breadth = guess.shape
     tile = (height, breadth)
-    copies = [
-        start(guess.at[:, :, slab - 1 if end else 0], ends.at[end]) for end in range(2)
-    ]
     plan, kk = plan.wait(), kk.wait()
-    near, extra = near.wait(), extra.wait()
-    sources, media = sources.wait(), media.wait()
     masks = lane_masks(tile)
     place = lax.axis_index("depth")
     last_place = lax.axis_size("depth") - 1
-    layer3 = media[LAYER]
+    layer3 = media_of(pack)[LAYER]
     layer = layer3 / damping
     factors = []
     for side in range(2):
@@ -449,7 +444,6 @@
         factors.append(
             set_media(near_media.at[side], squared, layer, extra[side, 0], slab, inside)
         )
-    media_out()
 
     ws = list(factors)
     edge = DEEP - 1
@@ -478,20 +472,17 @@
         keep_power(k, ws)
         ws = next_power(k, ws)
         k += 1
-    waves_out()
-    for copy in copies:
-        copy.wait()
     for side in range(2):
         field = Field(ref, 0, height)
         field.clear()
         for i in range(DEEP + 1):
             for part in range(2):
                 if side == 0:
-                    value = near[0, part, :, i] if i < DEEP else ends[0, part]
+                    value = near[0, part, :, i] if i < DEEP else guess[part, :, 0]
                 else:
-                    value = near[1, part, :, i - 1] if i > 0 else ends[1, part]
+                    value = near[1, part, :, i - 1] if i > 0 else guess[part, :, slab - 1]
                 field.put(part, i, value)
-        lanes = Lanes(field, None, masks)
+        lanes = Lanes(field, masks)
         for i in range(1, DEEP):
             r = field.minus_a(i, near_media[side, DIAGONAL], layer3, lanes.now)
             for part in range(2):
@@ -506,13 +497,10 @@
                 for part in range(2):
                     res[side, part, s, i] += sources[part, s]
 
-    res_out()
-
 
 def chain_kernel(at, start, send, given, made, rest):
     got, passages, full = given
     mine, theirs = made
-    full = full.wait()
     place = lax.axis_index("depth")
     last_place = lax.axis_size("depth") - 1
     count = full.shape[2]
@@ -570,239 +558,216 @@
                 ref[side, way, part, a:b] = coupling * value[part]
 
 
-def update_passes(
+class Stage:
+    def __init__(self, below, own, above):
+        self.below, self.own, self.above = below, own, above
+
+
+def pipeline(stages, slab, carry, halfway):
+    offsets = [LAG * (len(stages) - 1 - i) for i in range(len(stages))]
+    trips = (slab - offsets[0]) // UNROLL
+
+    def run(i, p, carry):
+        out = stages[i].own(p, carry)
+        return carry if out is None else out
+
+    def own(i, start, stop, carry):
+        body = lambda p, c: run(i, p, c)
+        if start == 0 and stop > 0:
+            carry = body(0, carry)
+            start = 1
+        if stop == slab and start < slab:
+            return body(slab - 1, loop(start, slab - 1, body, carry))
+        return loop(start, stop, body, carry)
+
+    stages[0].below()
+    stages[0].above()
+    for i, stage in enumerate(stages):
+        if i:
+            stage.below()
+        carry = own(i, 0, offsets[i], carry)
+
+    def trip(t, carry):
+        for i in reversed(range(len(stages))):
+            for u in range(UNROLL):
+                carry = run(i, t * UNROLL + offsets[i] + u, carry)
+        return carry
+
+    first = trips // 2
+    carry = lax.fori_loop(0, first, trip, carry)
+    halfway(0, [first * UNROLL + o for o in offsets])
+    carry = lax.fori_loop(first, trips, trip, carry)
+    halfway(1, [trips * UNROLL + o for o in offsets])
+    for i, stage in enumerate(stages):
+        carry = own(i, trips * UNROLL + offsets[i], slab, carry)
+        if i:
+            stage.above()
+    return carry
+
+
+def update_stages(
     reach, slab, tile, incoming, residual_of, media, near_media, power, waves,
-    refs, side_ref, ready, after_first, emit, pieces, done, masks,
+    refs, emit, masks,
 ):
     edge = DEEP - 1
     first_update = Field(refs[0], -reach, tile[0])
     second_update = Field(refs[1], 1 - reach, tile[0])
     first_update.clear()
     second_update.clear()
-    own = lambda p: (tile_of(power, p + 1), tile_of(power, slab - p))
-    low = lambda p: (tile_of(waves, 0, 0, p + edge), tile_of(waves, 0, 1, p + edge))
-    high = lambda p: (tile_of(waves, 1, 0, p - slab), tile_of(waves, 1, 1, p - slab))
-    sides = (
-        (-reach, 0, near_media.at[0], low),
-        (0, slab, media, own),
-        (slab, slab + reach, near_media.at[1], high),
-    )
+    powers = (
+        lambda p: (tile_of(waves, 0, 0, p + edge), tile_of(waves, 0, 1, p + edge)),
+        lambda p: (tile_of(power, p + 1), tile_of(power, slab - p)),
+        lambda p: (tile_of(waves, 1, 0, p - slab), tile_of(waves, 1, 1, p - slab)),
+    )
+    coefficients = near_media.at[0], media, near_media.at[1]
+    first_lanes = Lanes(first_update, masks)
+    second_lanes = Lanes(second_update, masks)
 
     def begin(which, p):
-        _, _, m, powers = sides[which]
-        on, off = powers(p)
+        on, off = powers[which](p)
         onward = incoming[which, 0, 0], incoming[which, 0, 1]
         back = incoming[which, 1, 0], incoming[which, 1, 1]
         c = add(cmul(on, onward), cmul(off, back))
-        first_update.put_both(p, cmul(pair(m, INVERSE), add(c, residual_of(which, p))))
-
-    for which in (0, 2):
-        for p in range(*sides[which][:2]):
-            begin(which, p)
-    for piece, (a, b) in enumerate(cuts(slab)):
-        ready(piece)
-        loop(a, b, lambda p, unused: begin(1, p) or unused, 0)
-    after_first(first_update)
-
-    def smooth(field, margin, body, own_pieces, own_done):
-        lanes = Lanes(field, side_ref, masks)
-        for p in range(UNROLL):
-            lanes.fill(p)
-        for which in (0, 2, 1):
-            a, b, m, _ = sides[which]
-            a, b = max(a, margin - reach), min(b, slab + reach - margin)
-            if which != 1:
-                for p in range(a, b):
-                    body(which, m, p, lanes.now)
-                continue
-            for piece, (a, b) in enumerate(cuts(slab, own_pieces)):
-                lanes.sweep(
-                    a, b, slab, lambda p, c: body(1, media, p, lanes.kept) or c, 0
-                )
-                own_done(piece)
-
-    def second(which, m, p, lanes):
-        here, total = first_update.around(p, lanes)
-        second_update.put_both(p, add(here, cmul(pair(m, SECOND), total)))
-
-    def third(which, m, p, lanes):
-        here, total = second_update.around(p, lanes)
-        u = add(scale(keep * (1.0 + keep), here), cmul(pair(m, THIRD), total))
+        inverse = pair(coefficients[which], INVERSE)
+        first_update.put_both(p, cmul(inverse, add(c, residual_of(which, p))))
+
+    def second(which, p):
+        here, total = first_update.around(p, first_lanes.now)
+        smoothed = cmul(pair(coefficients[which], SECOND), total)
+        second_update.put_both(p, add(here, smoothed))
+
+    def third(which, p):
+        here, total = second_update.around(p, second_lanes.now)
+        smoothed = cmul(pair(coefficients[which], THIRD), total)
+        u = add(scale(keep * (1.0 + keep), here), smoothed)
         emit(which, p, add(u, first_update.both(p)))
 
-    smooth(first_update, 1, second, 1, lambda piece: None)
-    smooth(second_update, 2, third, pieces, done)
+    def stage(body, margin):
+        def beyond(which, a, b):
+            for p in range(a, b):
+                body(which, p)
+
+        return Stage(
+            lambda: beyond(0, margin - reach, 0),
+            lambda p, unused: body(1, p),
+            lambda: beyond(2, slab, slab + reach - margin),
+        )
+
+    return [stage(begin, 0), stage(second, 1), stage(third, 2)]
 
 
 def middle_kernel(start, send, given, made, rest):
     (
-        mine, theirs, plan, full, sources, media, near_media, waves, near,
+        mine, theirs, plan, full, sources, pack, near_media, waves, near,
         near_residual, power, residual, guess,
     ) = given
-    new_field, new_residual, (next_full, full_out), (slots, slots_out) = made
-    held, loaded, next_held, incoming, side_ref, *refs = rest
+    media = media_of(pack)
+    new_field, new_residual, next_full, slots = made
+    incoming, *refs = rest
     _, count, slab, height, breadth = guess.shape
     tile = (height, breadth)
-    spans = [pl.ds(a, b - a) for a, b in cuts(slab)]
-    res_copies = [start(residual.at[:, :, h], held.at[:, :, h]) for h in spans]
-    field_copies = [start(guess.at[:, :, h], loaded.at[:, :, h]) for h in spans]
     masks = lane_masks(tile)
-    place = lax.axis_index("depth")
     reach = DEEP - 1
     ext = reach - 2
     more = ext - 1
     new = Field(refs[2], -ext, height)
     new.clear()
-    plan, full, sources = plan.wait(), full.wait(), sources.wait()
-    media, near_media, waves = media.wait(), near_media.wait(), waves.wait()
-    near, near_residual, power = near.wait(), near_residual.wait(), power.wait()
+    plan = plan.wait()
     set_incoming(incoming, mine, theirs, full, tile_of(power, slab))
 
     def residual_of(which, p):
         if which == 1:
-            return held[0, :, p], held[1, :, p]
+            r = residual[0, :, p], residual[1, :, p]
+            if isinstance(p, int) and p == 0:
+                r = add(r, (near[0, 0, :, DEEP - 1], near[0, 1, :, DEEP - 1]))
+            if isinstance(p, int) and p == slab - 1:
+                r = add(r, (near[1, 0, :, 0], near[1, 1, :, 0]))
+            return r
         i = p + reach if which == 0 else p - slab
         return near_residual[which // 2, 0, :, i], near_residual[which // 2, 1, :, i]
 
-    def ready(piece):
-        res_copies[piece].wait()
-
-    def after_first(update):
-        inverse = pair(media, INVERSE)
-        for side, (p, i) in enumerate(((0, DEEP - 1), (slab - 1, 0))):
-            lacks = cmul(inverse, (near[side, 0, :, i], near[side, 1, :, i]))
-            update.put_both(p, add(update.both(p), lacks))
-        for s in range(count):
-            k = plan[s] - place * slab
-
-            @pl.when((k >= 0) & (k < slab))
-            def _():
-                update.bump(k, s, cmul(inverse, (sources[0, s], sources[1, s])))
-
-        for copy in field_copies:
-            copy.wait()
-
     def emit(which, p, u):
         for part in range(2):
             if which == 1:
-                value = loaded[part, :, p] + u[part]
-                loaded[part, :, p] = value
+                value = guess[part, :, p] + u[part]
+                new_field[part, :, p] = value
             else:
                 i = p + DEEP if which == 0 else p - slab
                 value = near[which // 2, part, :, i] + u[part]
             new.put(part, p, value)
 
-    def done(piece):
-        send(loaded, new_field)
-
-    update_passes(
+    stages = update_stages(
         reach, slab, tile, incoming, residual_of, media, near_media, power, waves,
-        refs, side_ref, ready, after_first, emit, 1, done, masks,
+        refs, emit, masks,
     )
 
     layer3 = media[LAYER]
     factor = pair(media, WAVE)
-    lanes = Lanes(new, side_ref, masks)
-    for p in range(UNROLL):
-        lanes.fill(p)
-
-    def put(p, r):
-        for part in range(2):
-            next_held[part, :, p + more] = r[part]
-
-    for p in range(-more, 0):
-        put(p, new.minus_a(p, near_media[0, DIAGONAL], layer3, lanes.now))
-    for p in range(slab, slab + more):
-        put(p, new.minus_a(p, near_media[1, DIAGONAL], layer3, lanes.now))
-    diagonal = media[DIAGONAL]
+    lanes = Lanes(new, masks)
+
+    def residual_at(p, diagonal):
+        r = new.minus_a(p, diagonal, layer3, lanes.now)
+        for part in range(2):
+            new_residual[part, :, p + more] = r[part]
+        return r
+
+    def beyond(side, a, b):
+        for p in range(a, b):
+            residual_at(p, near_media[side, DIAGONAL])
 
     def inside(p, carry):
         toward_next, toward_prev = carry
-        r = new.minus_a(p, diagonal, layer3, lanes.kept)
-        put(p, r)
+        r = residual_at(p, media[DIAGONAL])
         toward_next = add(cmul(factor, toward_next), r)
         toward_prev = add(toward_prev, cmul(tile_of(power, p), r))
         return toward_next, toward_prev
 
+    stages.append(
+        Stage(lambda: beyond(0, -more, 0), inside, lambda: beyond(1, slab, slab + more))
+    )
     zero = jnp.zeros((count,) + tile, jnp.float32)
-    carry = ((zero, zero), (zero, zero))
-    for piece, (a, b) in enumerate(cuts(slab)):
-        carry = lanes.sweep(a, b, slab, inside, carry)
-        low = a + more if piece else 0
-        high = b + more if piece < PIECES - 1 else slab + 2 * more
-        part = pl.ds(low, high - low)
-        send(next_held.at[:, :, part], new_residual.at[:, :, part])
+    carry = pipeline(stages, slab, ((zero, zero), (zero, zero)), lambda i, reached: None)
     for way in range(2):
         for part in range(2):
             next_full[way, part] = carry[way][part]
     force_emits(plan, next_full, sources, power, slab)
     fill_send(slots, next_full, None)
-    slots_out()
-    full_out()
+    add_forcing(plan, new_residual, sources, more, slab)
 
 
 def final_kernel(start, send, given, made, rest):
     (
-        mine, theirs, plan, full, sources, media, near_media, waves, power,
-        residual, field,
+        mine, theirs, full, pack, near_media, waves, power, residual, field,
     ) = given
     (out,) = made
-    held, loaded, incoming, side_ref, *refs = rest
+    media = media_of(pack)
+    held, incoming, *refs = rest
     _, count, slab, height, breadth = field.shape
     tile = (height, breadth)
-    spans = [pl.ds(a, b - a) for a, b in cuts(slab)]
     reach = 2
-    res_copies = []
-    for piece, (a, b) in enumerate(cuts(slab)):
-        low = a + reach if piece else 0
-        high = b + reach if piece < PIECES - 1 else slab + 2 * reach
-        part = pl.ds(low, high - low)
-        res_copies.append(start(residual.at[:, :, part], held.at[:, :, part]))
-    field_copies = [start(field.at[:, :, h], loaded.at[:, :, h]) for h in spans]
     masks = lane_masks(tile)
-    place = lax.axis_index("depth")
-    plan, full, sources = plan.wait(), full.wait(), sources.wait()
-    media, near_media, waves = media.wait(), near_media.wait(), waves.wait()
-    power = power.wait()
     set_incoming(incoming, mine, theirs, full, tile_of(power, slab))
-    for copy in (res_copies[0], res_copies[-1]):
-        copy.wait()
 
     def residual_of(which, p):
-        return held[0, :, p + reach], held[1, :, p + reach]
-
-    def ready(piece):
-        if 0 < piece < PIECES - 1:
-            res_copies[piece].wait()
-
-    def after_first(update):
-        for s in range(count):
-            k = plan[s] - place * slab
-            src = sources[0, s], sources[1, s]
-            for m, a, b in (
-                (media, 0, slab),
-                (near_media.at[0], -reach, 0),
-                (near_media.at[1], slab, slab + reach),
-            ):
-
-                @pl.when((k >= a) & (k < b))
-                def _():
-                    update.bump(k, s, cmul(pair(m, INVERSE), src))
-
-        for copy in field_copies:
-            copy.wait()
+        return residual[0, :, p + reach], residual[1, :, p + reach]
 
     def emit(which, p, u):
         for part in range(2):
-            loaded[part, :, p] += u[part]
-
-    def done(piece):
-        send(loaded.at[:, :, spans[piece]], out.at[:, :, spans[piece]])
-
-    update_passes(
+            held[part, :, p] = field[part, :, p] + u[part]
+
+    stages = update_stages(
         reach, slab, tile, incoming, residual_of, media, near_media, power, waves,
-        refs, side_ref, ready, after_first, emit, PIECES, done, masks,
-    )
+        refs, emit, masks,
+    )
+    sent = [0]
+
+    def send_field(top):
+        part = pl.ds(sent[0], top - sent[0])
+        send(held.at[:, :, part], out.at[:, :, part])
+        sent[0] = top
+
+    pipeline(stages, slab, 0, lambda i, reached: send_field(reached[2]))
+    send_field(slab)
 
 
 def local(sources, plan, absorb, labels, region_kk, damp_cells, guess):
@@ -829,54 +794,53 @@
     got_odd = lax.ppermute(payload(jnp.where(even, 0, top)), "depth", odd_pairs)
     got_even = lax.ppermute(payload(jnp.where(even, top, 0)), "depth", even_pairs)
 
-    residual, emits, media, power = kernel_call(
+    residual, pack, power = kernel_call(
         start_kernel,
         [
             (plan, "smem"), (region_kk, "smem"), (damp_cells, "smem"),
             (sources, "vmem"), (absorb, "vmem"), (labels, "vmem"), (guess, "hbm"),
         ],
         [
-            (planes(slab), "hbm"), ((2, 2, count) + tile, "vmem"),
-            ((MEDIA,) + tile, "vmem"), ((slab + 1, 2) + tile, "vmem"),
-        ],
-        [
-            scratch(planes(slab)), scratch(planes(slab)), scratch(planes(slab)),
+            (planes(slab), "hbm"), ((MEDIA + 4 + 4 * count,) + tile, "vmem"),
+            ((slab + 1, 2) + tile, "vmem"),
+        ],
+        [
+            scratch(planes(slab)), scratch(planes(slab)), scratch((2, 2, count) + tile),
             Field.shape(count, slab + 2, tile),
         ],
-        pieces=2 * PIECES, cost=20_000_000, name="start",
+        pieces=2 * PIECES, cost=20_000_000, name="start", limit=62,
     )
     width = count // 2
     full, slots, near, extra = kernel_call(
         arrange_kernel,
-        [(got_even, "direct"), (got_odd, "direct"), (emits, "vmem"), (power, "hbm")],
-        [
-            ((2, 2, count) + tile, "vmem"), ((size, 2 * width + 2) + tile, "vmem"),
-            ((2, 2, count, DEEP) + tile, "vmem"), ((2, 2) + tile, "vmem"),
-        ],
-        [scratch((2, 2) + tile)],
-        pieces=1, cost=1_000_000, name="arrange", limit=16,
+        [(got_even, "direct"), (got_odd, "direct"), (pack, "direct")],
+        [
+            ((2, 2, count) + tile, "direct"), ((size, 2 * width + 2) + tile, "direct"),
+            ((2, 2, count, DEEP) + tile, "direct"), ((2, 2) + tile, "direct"),
+        ],
+        cost=1_000_000, name="arrange", limit=4,
     )
     first_got = lax.all_to_all(slots, "depth", 0, 0)
     near_residual, near_media, waves = kernel_call(
         prepare_kernel,
         [
-            (plan, "smem"), (region_kk, "smem"), (near, "vmem"), (extra, "vmem"),
-            (sources, "vmem"), (media, "vmem"), (guess, "hbm"),
-        ],
-        [
-            ((2, 2, count, edge) + tile, "vmem"), ((2, MEDIA) + tile, "vmem"),
-            ((2, 2, edge, 2) + tile, "vmem"),
-        ],
-        [scratch((2, 2, count) + tile), Field.shape(count, DEEP + 1, tile)],
-        pieces=2, cost=4_000_000, name="prepare",
+            (plan, "smem"), (region_kk, "smem"), (near, "direct"), (extra, "direct"),
+            (sources, "direct"), (pack, "direct"), (guess, "direct"),
+        ],
+        [
+            ((2, 2, count, edge) + tile, "direct"), ((2, MEDIA) + tile, "direct"),
+            ((2, 2, edge, 2) + tile, "direct"),
+        ],
+        [Field.shape(count, DEEP + 1, tile)],
+        cost=4_000_000, name="prepare", limit=4,
     )
 
     def chain(got, full):
         mine, theirs = kernel_call(
             functools.partial(chain_kernel, 2 * width),
-            [(got, "direct"), (first_got, "direct"), (full, "vmem")],
+            [(got, "direct"), (first_got, "direct"), (full, "direct")],
             [((4, 2, width) + tile, "direct")] * 2,
-            cost=1_000_000, name="chain", limit=16,
+            cost=1_000_000, name="chain", limit=4,
         )
         return mine, lax.ppermute(theirs, "depth", even_pairs)
 
@@ -885,40 +849,37 @@
         middle_kernel,
         [
             (mine, "direct"), (theirs, "direct"),
-            (plan, "smem"), (full, "vmem"), (sources, "vmem"),
-            (media, "vmem"), (near_media, "vmem"), (waves, "vmem"), (near, "vmem"),
-            (near_residual, "vmem"), (power, "vmem"), (residual, "hbm"), (guess, "hbm"),
-        ],
-        [
-            (planes(slab), "hbm"), (planes(slab + 2 * (DEEP - 4)), "hbm"),
-            ((2, 2, count) + tile, "vmem"), ((size, 2 * width) + tile, "vmem"),
-        ],
-        [
-            scratch(planes(slab)), scratch(planes(slab)),
-            scratch(planes(slab + 2 * (DEEP - 4))), scratch((3, 2, 2, count) + tile),
-            scratch(planes(slab)),
+            (plan, "smem"), (full, "direct"), (sources, "direct"),
+            (pack, "direct"), (near_media, "direct"), (waves, "direct"),
+            (near, "direct"), (near_residual, "direct"), (power, "direct"),
+            (residual, "direct"), (guess, "direct"),
+        ],
+        [
+            (planes(slab), "direct"), (planes(slab + 2 * (DEEP - 4)), "direct"),
+            ((2, 2, count) + tile, "direct"), ((size, 2 * width) + tile, "direct"),
+        ],
+        [
+            scratch((3, 2, 2, count) + tile),
             Field.shape(count, slab + 2 * edge, tile),
             Field.shape(count, slab + 2 * edge - 2, tile),
             Field.shape(count, slab + 2 * edge - 4, tile),
         ],
-        pieces=3 * PIECES + 1, cost=80_000_000, name="middle",
+        cost=80_000_000, name="middle", limit=20,
     )
     mine, theirs = chain(lax.all_to_all(slots, "depth", 0, 0), next_full)
     (out,) = kernel_call(
         final_kernel,
         [
-            (mine, "direct"), (theirs, "direct"),
-            (plan, "smem"), (next_full, "vmem"), (sources, "vmem"),
-            (media, "vmem"), (near_media, "vmem"), (waves, "vmem"), (power, "vmem"),
-            (new_residual, "hbm"), (new_field, "hbm"),
+            (mine, "direct"), (theirs, "direct"), (next_full, "direct"),
+            (pack, "direct"), (near_media, "direct"), (waves, "direct"),
+            (power, "direct"), (new_residual, "direct"), (new_field, "direct"),
         ],
         [(planes(slab), "hbm")],
         [
-            scratch(planes(slab + 2 * (DEEP - 4))), scratch(planes(slab)),
-            scratch((3, 2, 2, count) + tile), scratch(planes(slab)),
+            scratch(planes(slab)), scratch((3, 2, 2, count) + tile),
             Field.shape(count, slab + 4, tile), Field.shape(count, slab + 2, tile),
         ],
-        pieces=3 * PIECES, cost=60_000_000, name="final",
+        pieces=3, cost=60_000_000, name="final", limit=16,
     )
     return out
 

time: 77.5 us -> 60.5 us (0.78)
  Pallas kernels: 30 us -> 17.9 us
  local copies, waits for them, and re-layouts: 7.56 us -> 3.02 us
    pallas_call x7, Pallas kernels: 30 us -> 17.9 us  [kernel_call(): pl.pallas_call(kernel, out_shape=tuple((jax.ShapeDtypeStruct(s, jnp.float...]
    unnamed x20 -> x16, local copies, waits for them, and re-layouts: 6.51 us -> 1.97 us
  transfers between devices with their start and end apart: 4 -> 4, of which waited for: 1 -> 1; matrix products, arithmetic and copies ran while one was open for 0% -> 0% of each run, Pallas kernels for 9% -> 10%
where the time goes in v4:
time: 60.5 us; the launch traced here: 60.2 us
  blocking collectives  31.1 us (51%)
  Pallas kernels  17.9 us (30%)
  starting transfers between devices  5.31 us (9%)
  local copies, waits for them, and re-layouts  3.02 us (5%)
  other arithmetic  1.41 us (2%)
  waiting for transfers between devices  1.25 us (2%)
    pallas_call x7, Pallas kernels, kernel_call(): pl.pallas_call(kernel, out_shape=tuple((jax.ShapeDtypeStruct(s, jnp.float...  17.9 us
    all_to_all x1, blocking collectives, local(): first_got = lax.all_to_all(slots, 'depth', 0, 0)  17.6 us
    all_to_all x1, blocking collectives, local(): mine, theirs = chain(lax.all_to_all(slots, 'depth', 0, 0), next_full)  13.5 us
    ppermute x1, starting transfers between devices, local(): lax.ppermute(payload(jnp.where(even, top, 0)), 'depth', even_pairs)  4.38 us
    unnamed x16, local copies, waits for them, and re-layouts  1.97 us
    ppermute x2, waiting for transfers between devices, chain(): return (mine, lax.ppermute(theirs, 'depth', even_pairs))  1.24 us
  transfers between devices with their start and end apart: 4, of which 1 were waited for; matrix products, arithmetic and copies ran while one was open for 0% of the time, Pallas kernels for 10%

profile of v4, /device:TPU:0, one launch (start us, length us, event | category | flops | bytes accessed | tf_op | source)
XLA Modules:
  0.0 60.2 jit_solution(2365988811711498306)
XLA Ops:
  0.0 0.7 %convert_element_type.4 = f32[1,8,128]{2,1,0:T(8,128)S(1)} convert(s32[1,8,128]{2,1,0:T(8,128)} %refs_5_.1) | non-fusion elementwise | flops 1024 | bytes 8192 | tf_op jit(solution)/shard_map/convert_element_type | solution.py:788
  0.7 1.0 %constant_dynamic-slice_fusion = (f32[2,4,6,8,128]{4,3,2,1,0:T(8,128)S(1)}, f32[2,4,6,8,128]{4,3,2,1,0:T(8,128)S(1)}) fusion(f32[2,4,64,8,128]{4,3,2,1,0:T(8,128)} %refs_12_.1, s32[]{:T(128)S(6)} %select_n.18, s32[]{:T(128)S(6)} %select_n.17), kind=kLoop, calls=%fused_computation.4 | loop fusion | bytes 786440 | tf_op jit(solution)/shard_map/dynamic_slice | solution.py:786
  1.7 0.7 %pad_maximum_fusion = (f32[50,8,128]{2,1,0:T(8,128)S(1)}, f32[50,8,128]{2,1,0:T(8,128)S(1)}) fusion(f32[1,8,128]{2,1,0:T(8,128)S(1)} %convert_element_type.4, f32[1,8,128]{2,1,0:T(8,128)} %refs_4_.3, f32[48,8,128]{2,1,0:T(8,128)S(1)} %bitcast.2, f32[48,8,128]{2,1,0:T(8,128)S(1)} %bitcast.3), kind=kLoop, calls=%fused_computation | loop fusion | flops 204800 | bytes 811008 | tf_op jit(solution)/shard_map/concatenate | solution.py:787
  2.5 0.7 %collective-permute-start.1 = (f32[50,8,128]{2,1,0:T(8,128)S(1)}, f32[50,8,128]{2,1,0:T(8,128)S(1)}, u32[]{:S(2)}, u32[]{:S(2)}) collective-permute-start(f32[50,8,128]{2,1,0:T(8,128)S(1)} %get-tuple-element.43), channel_id=1, source_target_pairs={{1,2},{3,4},{5,6},{7,8},{9,10},{11,12},{13,14},{2,1},{4,3},{6,5},{... | collective-permute-start | bytes 614408 | tf_op jit(solution)/shard_map/ppermute | solution.py:794
  3.1 0.0 copy-start.5
  3.2 0.0 copy-start.6
  3.2 0.0 copy-start.7
  3.2 4.4 %collective-permute-start = (f32[50,8,128]{2,1,0:T(8,128)S(1)}, f32[50,8,128]{2,1,0:T(8,128)S(1)}, u32[]{:S(2)}, u32[]{:S(2)}) collective-permute-start(f32[50,8,128]{2,1,0:T(8,128)S(1)} %get-tuple-element.44), channel_id=1, source_target_pairs={{0,1},{1,0},{2,3},{3,2},{4,5},{5,4},{6,7},{7,6},{8,9},{9,8},{10,11... | collective-permute-start | bytes 614408 | tf_op jit(solution)/shard_map/ppermute | solution.py:795
  7.6 4.9 %start.1 = (f32[2,4,64,8,128]{4,3,2,1,0:T(8,128)}, f32[30,8,128]{2,1,0:T(8,128)}, f32[65,2,8,128]{3,2,1,0:T(8,128)}) custom-call(s32[4]{0:T(128)} %refs_2_.3, f32[8]{0:T(128)} %refs_1_.3, s32[128]{0:T(128)} %refs_2_.2, f32[2,4,8,128]{3,2,1,0:T(8,128)} %refs_4_.5, f32[1,8,128]{2,1,0:T(8,128)} %refs_4_.3, s32[1,8,128]{2,1,0:T(8,128)} %refs_5_.1, ...), custom_call_target="tpu_custom_call" | custom-call | flops 20000000 | bytes 4194304 | tf_op jit(solution)/shard_map/start/pallas_call | solution.py:101
  12.5 0.0 copy-start
  12.5 0.0 collective-permute-done.1.refs_1_
  12.5 0.0 collective-permute-done.refs_0_
  12.5 0.0 copy-start.3
  12.5 1.0 %copy-done.3 = f32[30,8,128]{2,1,0:T(8,128)S(1)} copy-done((f32[30,8,128]{2,1,0:T(8,128)S(1)}, f32[30,8,128]{2,1,0:T(8,128)}, u32[]{:S(2)}) %copy-start.3) | copy-done | bytes 122904
  13.5 0.1 arrange.1
  13.6 0.0 copy-start.1
  13.6 0.0 copy-start.2
  13.7 17.6 %all_to_all.10.refs_0_.refs_1_ = f32[16,6,8,128]{3,2,1,0:T(8,128)S(1)} all-to-all(f32[16,6,8,128]{3,2,1,0:T(8,128)S(1)} %get-tuple-element.24), channel_id=1, replica_groups=mesh['groups'=2,'depth'=16] {'depth'}, dimensions={0} | all-to-all | bytes 786432 | tf_op jit(solution)/shard_map/all_to_all | solution.py:823
  31.2 0.1 chain.2
  31.4 0.2 collective-permute-start.2
  31.5 0.0 copy-done.5
  31.5 0.0 copy-done.6
  31.5 0.0 copy-done.7
  31.6 0.9 %copy-done.4 = f32[30,8,128]{2,1,0:T(8,128)S(1)} copy-done((f32[30,8,128]{2,1,0:T(8,128)S(1)}, f32[30,8,128]{2,1,0:T(8,128)}, u32[]{:S(2)}) %copy-start.4) | copy-done | bytes 122904
  32.5 1.0 %prepare.1 = (f32[2,2,4,5,8,128]{5,4,3,2,1,0:T(8,128)S(1)}, f32[2,10,8,128]{3,2,1,0:T(8,128)S(1)}, f32[2,2,5,2,8,128]{5,4,3,2,1,0:T(8,128)S(1)}) custom-call(s32[4]{0:T(128)S(1)} %copy-done.6, f32[8]{0:T(128)S(1)} %copy-done.7, f32[2,2,4,6,8,128]{5,4,3,2,1,0:T(8,128)S(1)} %get-tuple-element.28.refs_2_.refs_8_, ...), custom_call_target="tpu_custom_call" | custom-call | flops 4000000 | bytes 4194304 | tf_op jit(solution)/shard_map/prepare/pallas_call | solution.py:101
  33.5 0.0 collective-permute-done.2.refs_1_
  33.5 6.9 %middle.1 = (f32[2,4,64,8,128]{4,3,2,1,0:T(8,128)S(1)}, f32[2,4,68,8,128]{4,3,2,1,0:T(8,128)S(1)}, f32[2,2,4,8,128]{4,3,2,1,0:T(8,128)S(1)}, f32[16,4,8,128]{3,2,1,0:T(8,128)S(1)}) custom-call(f32[4,2,2,8,128]{4,3,2,1,0:T(8,128)S(1)} %get-tuple-element.26.refs_0_, f32[4,2,2,8,128]{4,3,2,1,0:T(8,128)S(1)} %collective-permute-done.2.refs_1_, s32[4]{0:T(128)S(1)} %copy-done.6, ...), custom_call_target="tpu_custom_call" | custom-call | flops 80000000 | bytes 4194304 | tf_op jit(solution)/shard_map/middle/pallas_call | solution.py:101
  40.4 13.5 %all_to_all.11.refs_0_ = f32[16,4,8,128]{3,2,1,0:T(8,128)S(1)} all-to-all(f32[16,4,8,128]{3,2,1,0:T(8,128)S(1)} %get-tuple-element.35), channel_id=1, replica_groups=mesh['groups'=2,'depth'=16] {'depth'}, dimensions={0} | all-to-all | bytes 524288 | tf_op jit(solution)/shard_map/all_to_all | solution.py:869
  53.9 0.1 chain.3
  54.1 0.1 collective-permute-start.3
  54.1 1.2 %collective-permute-done.3.refs_1_ = f32[4,2,2,8,128]{4,3,2,1,0:T(8,128)S(1)} collective-permute-done((f32[4,2,2,8,128]{4,3,2,1,0:T(8,128)S(1)}, f32[4,2,2,8,128]{4,3,2,1,0:T(8,128)S(1)}, u32[]{:S(2)}, u32[]{:S(2)}) %collective-permute-start.3) | collective-permute-done | bytes 65568 | tf_op jit(solution)/shard_map/ppermute | solution.py:845
  55.4 4.8 %final.1 = f32[2,4,64,8,128]{4,3,2,1,0:T(8,128)} custom-call(f32[4,2,2,8,128]{4,3,2,1,0:T(8,128)S(1)} %get-tuple-element.37.refs_0_, f32[4,2,2,8,128]{4,3,2,1,0:T(8,128)S(1)} %collective-permute-done.3.refs_1_, f32[2,2,4,8,128]{4,3,2,1,0:T(8,128)S(1)} %get-tuple-element.36.refs_2_, f32[30,8,128]{2,1,0:T(8,128)S(1)} %copy-done.4, ...), custom_call_target="tpu_custom_call" | custom-call | flops 60000000 | bytes 4194304 | tf_op jit(solution)/shard_map/final/pallas_call | solution.py:101
  (4 shorter events, 0.0 us)
Async XLA Ops:
  2.5 10.0 %collective-permute-start.1 = (f32[50,8,128]{2,1,0:T(8,128)S(1)}, f32[50,8,128]{2,1,0:T(8,128)S(1)}, u32[]{:S(2)}, u32[]{:S(2)}) collective-permute-start(f32[50,8,128]{2,1,0:T(8,128)S(1)} %get-tuple-element.43), channel_id=1, source_target_pairs={{1,2},{3,4},{5,6},{7,8},{9,10},{11,12},{13,14},{2,1},{4,3},{6,5},{... | collective-permute-start | bytes 614408 | tf_op jit(solution)/shard_map/ppermute | solution.py:794
  3.1 28.4 %copy-start.5 = (f32[2,4,8,128]{3,2,1,0:T(8,128)S(1)}, f32[2,4,8,128]{3,2,1,0:T(8,128)}, u32[]{:S(2)}) copy-start(f32[2,4,8,128]{3,2,1,0:T(8,128)} %refs_4_.5) | copy-start | bytes 98308
  3.2 28.4 %copy-start.6 = (s32[4]{0:T(128)S(1)}, s32[4]{0:T(128)}, u32[]{:S(2)}) copy-start(s32[4]{0:T(128)} %refs_2_.3) | copy-start | bytes 52
  3.2 28.4 %copy-start.7 = (f32[8]{0:T(128)S(1)}, f32[8]{0:T(128)}, u32[]{:S(2)}) copy-start(f32[8]{0:T(128)} %refs_1_.3) | copy-start | bytes 100
  3.2 9.3 %collective-permute-start = (f32[50,8,128]{2,1,0:T(8,128)S(1)}, f32[50,8,128]{2,1,0:T(8,128)S(1)}, u32[]{:S(2)}, u32[]{:S(2)}) collective-permute-start(f32[50,8,128]{2,1,0:T(8,128)S(1)} %get-tuple-element.44), channel_id=1, source_target_pairs={{0,1},{1,0},{2,3},{3,2},{4,5},{5,4},{6,7},{7,6},{8,9},{9,8},{10,11... | collective-permute-start | bytes 614408 | tf_op jit(solution)/shard_map/ppermute | solution.py:795
  12.5 19.1 %copy-start = (f32[2,4,64,8,128]{4,3,2,1,0:T(8,128)S(1)}, f32[2,4,64,8,128]{4,3,2,1,0:T(8,128)}, u32[]{:S(2)}) copy-start(f32[2,4,64,8,128]{4,3,2,1,0:T(8,128)} %refs_12_.1) | copy-start | bytes 6291460
  12.5 1.0 %copy-start.3 = (f32[30,8,128]{2,1,0:T(8,128)S(1)}, f32[30,8,128]{2,1,0:T(8,128)}, u32[]{:S(2)}) copy-start(f32[30,8,128]{2,1,0:T(8,128)} %get-tuple-element.23.refs_2_.refs_5_.refs_3_) | copy-start | bytes 368644
  13.6 19.9 %copy-start.1 = (f32[65,2,8,128]{3,2,1,0:T(8,128)S(1)}, f32[65,2,8,128]{3,2,1,0:T(8,128)}, u32[]{:S(2)}) copy-start(f32[65,2,8,128]{3,2,1,0:T(8,128)} %get-tuple-element.33.refs_10_.refs_6_) | copy-start | bytes 1597444
  13.6 19.9 %copy-start.2 = (f32[2,4,64,8,128]{4,3,2,1,0:T(8,128)S(1)}, f32[2,4,64,8,128]{4,3,2,1,0:T(8,128)}, u32[]{:S(2)}) copy-start(f32[2,4,64,8,128]{4,3,2,1,0:T(8,128)} %get-tuple-element.34.refs_11_) | copy-start | bytes 6291460
  31.4 2.2 %collective-permute-start.2 = (f32[4,2,2,8,128]{4,3,2,1,0:T(8,128)S(1)}, f32[4,2,2,8,128]{4,3,2,1,0:T(8,128)S(1)}, u32[]{:S(2)}, u32[]{:S(2)}) collective-permute-start(f32[4,2,2,8,128]{4,3,2,1,0:T(8,128)S(1)} %get-tuple-element.27), channel_id=1, source_target_pairs={{0,1},{1,0},{2,3},{3,2},{4,5},{5,4},{6,7},{7,6},{8,9},{9,8},{10,11... | collective-permute-start | bytes 196616 | tf_op jit(solution)/shard_map/ppermute | solution.py:845
  31.6 0.9 %copy-start.4 = (f32[30,8,128]{2,1,0:T(8,128)S(1)}, f32[30,8,128]{2,1,0:T(8,128)}, u32[]{:S(2)}) copy-start(f32[30,8,128]{2,1,0:T(8,128)} %get-tuple-element.23.refs_2_.refs_5_.refs_3_) | copy-start | bytes 368644
  54.1 1.3 %collective-permute-start.3 = (f32[4,2,2,8,128]{4,3,2,1,0:T(8,128)S(1)}, f32[4,2,2,8,128]{4,3,2,1,0:T(8,128)S(1)}, u32[]{:S(2)}, u32[]{:S(2)}) collective-permute-start(f32[4,2,2,8,128]{4,3,2,1,0:T(8,128)S(1)} %get-tuple-element.38), channel_id=1, source_target_pairs={{0,1},{1,0},{2,3},{3,2},{4,5},{5,4},{6,7},{7,6},{8,9},{9,8},{10,11... | collective-permute-start | bytes 196616 | tf_op jit(solution)/shard_map/ppermute | solution.py:845

commit v5 on v4

--- a/solution.py
+++ b/solution.py
@@ -17,6 +17,7 @@
 UNROLL = 4
 LAG = UNROLL + 1
 PIECES = 4
+PACK = 4
 
 
 def cmul(a, b):
@@ -52,6 +53,7 @@
 
 def kernel_call(body, inputs, outputs, scratch=(), pieces=0, cost=0, name=None, limit=56):
     n_in, n_out = len(inputs), len(outputs)
+    pinned = ("hbm", "vmem", "smem")
     extra = []
     for array, place in inputs:
         if place in ("vmem", "smem"):
@@ -113,7 +115,10 @@
             flops=cost, bytes_accessed=4 << 20, transcendentals=0
         ),
         name=name,
-    )(*[array for array, _ in inputs])
+    )(*[
+        pltpu.with_memory_space_constraint(array, pltpu.HBM) if place in pinned else array
+        for array, place in inputs
+    ])
 
 
 def lane_sum(here, masks):
@@ -257,10 +262,28 @@
     return pl.ds(MEDIA + 4 + (2 * way + part) * count, count)
 
 
+def pack_kernel(start, send, given, made, rest):
+    kk, absorb, labels, guess = given
+    _, count, slab, *_ = guess.shape
+    even = lax.rem(lax.axis_index("depth"), 2) == 0
+    top = slab - DEEP
+    for out, first in zip(made, (jnp.where(even, top, 0), jnp.where(even, 0, top))):
+        for i in range(2 * count):
+            send(
+                guess.at[i // count, i % count, pl.ds(first, DEEP)],
+                out.at[pl.ds(i * DEEP, DEEP)],
+            )
+    kk, absorb, labels = kk.wait(), absorb.wait(), labels.wait()
+    squared = region_values(labels[0], kk)
+    for out in made:
+        out[2 * count * DEEP] = absorb[0]
+        out[2 * count * DEEP + 1] = squared
+
+
 def start_kernel(start, send, given, made, rest):
     plan, kk, damp, sources, absorb, labels, guess = given
-    residual, (pack, pack_out), (power, power_out) = made
-    loaded, held, emits, ref = rest
+    residual, pack, power = made
+    loaded, emits, ref = rest
     _, count, slab, height, breadth = guess.shape
     tile = (height, breadth)
     media = media_of(pack)
@@ -301,7 +324,7 @@
         power[k, 0], power[k, 1] = w
         r = field.minus_a(k, diagonal, layer3, lanes.now)
         for part in range(2):
-            held[part, :, k] = r[part]
+            residual[part, :, k] = r[part]
         toward_next = add(cmul(factor, toward_next), r)
         toward_prev = add(toward_prev, cmul(w, r))
         return toward_next, toward_prev, cmul(factor, w)
@@ -327,12 +350,9 @@
             if k + 1 < slab:
                 fill(k + 1)
             carry = plane(k, carry)
-        add_forcing(plan, held, sources, 0, slab, a, b)
-        part = pl.ds(a, b - a)
-        send(held.at[:, :, part], residual.at[:, :, part])
     toward_next, toward_prev, w = carry
     power[slab, 0], power[slab, 1] = w
-    power_out()
+    add_forcing(plan, residual, sources, 0, slab)
     for part in range(2):
         emits[0, part] = toward_next[part]
         emits[1, part] = toward_prev[part]
@@ -342,17 +362,14 @@
     for way in range(2):
         for part in range(2):
             pack[emit_tiles(count, way, part)] = emits[way, part]
-    pack_out()
-
-
-def add_forcing(plan, held, sources, reach, slab, low=None, high=None):
+
+
+def add_forcing(plan, held, sources, reach, slab):
     first_plane = lax.axis_index("depth") * slab
-    low = -reach if low is None else low
-    high = slab + reach if high is None else high
     for s in range(sources.shape[1]):
         k = plan[s] - first_plane
 
-        @pl.when((k >= low) & (k < high))
+        @pl.when((k >= -reach) & (k < slab + reach))
         def _():
             for part in range(2):
                 held[part, s, k + reach] += sources[part, s]
@@ -423,23 +440,23 @@
         for i in range(2):
             at = 2 * count * DEEP + i
             extra[side, i] = jnp.where(even, first[at], second[at])
+    extra[0, 2] = extra[1, 2] = media_of(pack)[LAYER]
 
 
 def prepare_kernel(start, send, given, made, rest):
-    plan, kk, near, extra, sources, pack, guess = given
+    plan, near, extra, sources, guess = given
     res, near_media, waves = made
     (ref,) = rest
     _, count, slab, height, breadth = guess.shape
     tile = (height, breadth)
-    plan, kk = plan.wait(), kk.wait()
     masks = lane_masks(tile)
     place = lax.axis_index("depth")
     last_place = lax.axis_size("depth") - 1
-    layer3 = media_of(pack)[LAYER]
+    layer3 = extra[0, 2]
     layer = layer3 / damping
     factors = []
     for side in range(2):
-        squared = region_values(extra[side, 1].astype(jnp.int32), kk)
+        squared = extra[side, 1]
         inside = (place > 0) if side == 0 else (place < last_place)
         factors.append(
             set_media(near_media.at[side], squared, layer, extra[side, 0], slab, inside)
@@ -487,6 +504,7 @@
             r = field.minus_a(i, near_media[side, DIAGONAL], layer3, lanes.now)
             for part in range(2):
                 res[side, part, :, i - 1] = r[part]
+    plan = plan.wait()
     for s in range(count):
         k = plan[s] - place * slab
         for side, low in ((0, -edge), (1, slab)):
@@ -672,7 +690,6 @@
     more = ext - 1
     new = Field(refs[2], -ext, height)
     new.clear()
-    plan = plan.wait()
     set_incoming(incoming, mine, theirs, full, tile_of(power, slab))
 
     def residual_of(which, p):
@@ -730,6 +747,7 @@
     for way in range(2):
         for part in range(2):
             next_full[way, part] = carry[way][part]
+    plan = plan.wait()
     force_emits(plan, next_full, sources, power, slab)
     fill_send(slots, next_full, None)
     add_forcing(plan, new_residual, sources, more, slab)
@@ -772,27 +790,24 @@
 
 def local(sources, plan, absorb, labels, region_kk, damp_cells, guess):
     size = lax.axis_size("depth")
-    place = lax.axis_index("depth")
     _, count, slab, height, breadth = guess.shape
     tile = (height, breadth)
     edge = DEEP - 1
     planes = lambda n: (2, count, n) + tile
     scratch = lambda shape: pltpu.VMEM(shape, jnp.float32)
 
-    even = place % 2 == 0
-    top = slab - DEEP
-
-    def payload(first):
-        part = lax.dynamic_slice_in_dim(guess, first, DEEP, axis=2)
-        return jnp.concatenate(
-            [part.reshape((-1,) + tile), absorb, labels.astype(jnp.float32)], axis=0
-        )
-
+    tiles = (2 * count * DEEP + 2,) + tile
+    for_even, for_odd = kernel_call(
+        pack_kernel,
+        [(region_kk, "smem"), (absorb, "vmem"), (labels, "vmem"), (guess, "hbm")],
+        [(tiles, "direct")] * 2,
+        pieces=4 * count, cost=1_000_000, name="pack", limit=PACK,
+    )
     even_pairs = [(i, i ^ 1) for i in range(size)]
     odd_pairs = [(i, i + 1) for i in range(1, size - 1, 2)]
     odd_pairs += [(b, a) for a, b in odd_pairs]
-    got_odd = lax.ppermute(payload(jnp.where(even, 0, top)), "depth", odd_pairs)
-    got_even = lax.ppermute(payload(jnp.where(even, top, 0)), "depth", even_pairs)
+    got_odd = lax.ppermute(for_odd, "depth", odd_pairs)
+    got_even = lax.ppermute(for_even, "depth", even_pairs)
 
     residual, pack, power = kernel_call(
         start_kernel,
@@ -801,14 +816,14 @@
             (sources, "vmem"), (absorb, "vmem"), (labels, "vmem"), (guess, "hbm"),
         ],
         [
-            (planes(slab), "hbm"), ((MEDIA + 4 + 4 * count,) + tile, "vmem"),
-            ((slab + 1, 2) + tile, "vmem"),
-        ],
-        [
-            scratch(planes(slab)), scratch(planes(slab)), scratch((2, 2, count) + tile),
+            (planes(slab), "direct"), ((MEDIA + 4 + 4 * count,) + tile, "direct"),
+            ((slab + 1, 2) + tile, "direct"),
+        ],
+        [
+            scratch(planes(slab)), scratch((2, 2, count) + tile),
             Field.shape(count, slab + 2, tile),
         ],
-        pieces=2 * PIECES, cost=20_000_000, name="start", limit=62,
+        pieces=PIECES, cost=20_000_000, name="start", limit=16,
     )
     width = count // 2
     full, slots, near, extra = kernel_call(
@@ -816,7 +831,7 @@
         [(got_even, "direct"), (got_odd, "direct"), (pack, "direct")],
         [
             ((2, 2, count) + tile, "direct"), ((size, 2 * width + 2) + tile, "direct"),
-            ((2, 2, count, DEEP) + tile, "direct"), ((2, 2) + tile, "direct"),
+            ((2, 2, count, DEEP) + tile, "direct"), ((2, 3) + tile, "direct"),
         ],
         cost=1_000_000, name="arrange", limit=4,
     )
@@ -824,8 +839,8 @@
     near_residual, near_media, waves = kernel_call(
         prepare_kernel,
         [
-            (plan, "smem"), (region_kk, "smem"), (near, "direct"), (extra, "direct"),
-            (sources, "direct"), (pack, "direct"), (guess, "direct"),
+            (plan, "smem"), (near, "direct"), (extra, "direct"),
+            (sources, "direct"), (guess, "direct"),
         ],
         [
             ((2, 2, count, edge) + tile, "direct"), ((2, MEDIA) + tile, "direct"),

time: 60.5 us -> 56.5 us (0.934)
  blocking collectives: 31.1 us -> 36.1 us
  starting transfers between devices: 5.31 us -> 1.6 us
  local copies, waits for them, and re-layouts: 3.02 us -> 0.01 us
  other arithmetic: 1.41 us -> 0 us
  Pallas kernels: 17.9 us -> 16.8 us
    all_to_all x1, blocking collectives: 17.6 us -> 22.8 us  [local(): first_got = lax.all_to_all(slots, 'depth', 0, 0)]
    ppermute x2, starting transfers between devices: 5.06 us -> 1.35 us  [the longest x1 0.79 us: local(): got_odd = lax.ppermute(for_odd, 'depth', odd_pairs)]
    unnamed x16 -> x4, local copies, waits for them, and re-layouts: 1.97 us -> 0.01 us
    pallas_call x7 -> x8, Pallas kernels: 17.9 us -> 16.8 us  [kernel_call(): pl.pallas_call(kernel, out_shape=tuple((jax.ShapeDtypeStruct(s, jnp.float...]
    dynamic_slice x1 -> x0, local copies, waits for them, and re-layouts: 1.05 us -> none  [payload(): part = lax.dynamic_slice_in_dim(guess, first, DEEP, axis=2)]
    concatenate x1 -> x0, other arithmetic: 0.72 us -> none  [payload(): jnp.concatenate([part.reshape((-1,) + tile), absorb, labels.astype(jnp.fl...]
    convert_element_type x1 -> x0, other arithmetic: 0.69 us -> none  [payload(): labels.astype(jnp.float32)]
  transfers between devices with their start and end apart: 4 -> 4, of which waited for: 1 -> 2; matrix products, arithmetic and copies ran while one was open for 0% -> 0% of each run, Pallas kernels for 10% -> 8%
where the time goes in v5:
time: 56.5 us; the launch traced here: 56.2 us
  blocking collectives  36.1 us (64%)
  Pallas kernels  16.8 us (30%)
  waiting for transfers between devices  1.64 us (3%)
  starting transfers between devices  1.6 us (3%)
    all_to_all x1, blocking collectives, local(): first_got = lax.all_to_all(slots, 'depth', 0, 0)  22.8 us
    pallas_call x8, Pallas kernels, kernel_call(): pl.pallas_call(kernel, out_shape=tuple((jax.ShapeDtypeStruct(s, jnp.float...  16.8 us
    all_to_all x1, blocking collectives, local(): mine, theirs = chain(lax.all_to_all(slots, 'depth', 0, 0), next_full)  13.3 us
    ppermute x2, waiting for transfers between devices, chain(): return (mine, lax.ppermute(theirs, 'depth', even_pairs))  1.63 us
  transfers between devices with their start and end apart: 4, of which 2 were waited for; matrix products, arithmetic and copies ran while one was open for 0% of the time, Pallas kernels for 8%

profile of v5, /device:TPU:0, one launch (start us, length us, event | category | flops | bytes accessed | tf_op | source)
XLA Modules:
  0.0 56.2 jit_solution(14358647448886930801)
XLA Ops:
  0.0 1.1 %pack.1 = (f32[50,8,128]{2,1,0:T(8,128)S(1)}, f32[50,8,128]{2,1,0:T(8,128)S(1)}) custom-call(f32[8]{0:T(128)} %refs_1_.3, f32[1,8,128]{2,1,0:T(8,128)} %refs_4_.3, s32[1,8,128]{2,1,0:T(8,128)} %refs_5_.1, f32[2,4,64,8,128]{4,3,2,1,0:T(8,128)} %refs_12_.1), custom_call_target="tpu_custom_call" | custom-call | flops 1000000 | bytes 4194304 | tf_op jit(solution)/shard_map/pack/pallas_call | solution.py:103
  1.1 0.6 collective-permute-start
  1.7 0.0 copy-start
  1.7 0.0 copy-start.1
  1.7 0.8 %collective-permute-start.1 = (f32[50,8,128]{2,1,0:T(8,128)S(1)}, f32[50,8,128]{2,1,0:T(8,128)S(1)}, u32[]{:S(2)}, u32[]{:S(2)}) collective-permute-start(f32[50,8,128]{2,1,0:T(8,128)S(1)} %get-tuple-element.26), channel_id=1, source_target_pairs={{1,2},{3,4},{5,6},{7,8},{9,10},{11,12},{13,14},{2,1},{4,3},{6,5},{... | collective-permute-start | bytes 614408 | tf_op jit(solution)/shard_map/ppermute | solution.py:809
  2.5 3.8 %start.1 = (f32[2,4,64,8,128]{4,3,2,1,0:T(8,128)S(1)}, f32[30,8,128]{2,1,0:T(8,128)S(1)}, f32[65,2,8,128]{3,2,1,0:T(8,128)S(1)}) custom-call(s32[4]{0:T(128)} %refs_2_.5, f32[8]{0:T(128)} %refs_1_.3, s32[128]{0:T(128)} %refs_2_.4, f32[2,4,8,128]{3,2,1,0:T(8,128)} %refs_4_.5, f32[1,8,128]{2,1,0:T(8,128)} %refs_4_.3, s32[1,8,128]{2,1,0:T(8,128)} %refs_5_.1, ...), custom_call_target="tpu_custom_call" | custom-call | flops 20000000 | bytes 4194304 | tf_op jit(solution)/shard_map/start/pallas_call | solution.py:103
  6.3 0.0 collective-permute-done.refs_0_
  6.3 0.0 collective-permute-done.1.refs_1_
  6.3 0.1 arrange.1
  6.4 22.8 %all_to_all.10.refs_0_.refs_1_ = f32[16,6,8,128]{3,2,1,0:T(8,128)S(1)} all-to-all(f32[16,6,8,128]{3,2,1,0:T(8,128)S(1)} %get-tuple-element.28), channel_id=1, replica_groups=mesh['groups'=2,'depth'=16] {'depth'}, dimensions={0} | all-to-all | bytes 786432 | tf_op jit(solution)/shard_map/all_to_all | solution.py:838
  29.2 0.1 chain.2
  29.4 0.2 collective-permute-start.2
  29.5 0.0 copy-done
  29.5 0.0 copy-done.1
  29.5 0.7 %prepare.1 = (f32[2,2,4,5,8,128]{5,4,3,2,1,0:T(8,128)S(1)}, f32[2,10,8,128]{3,2,1,0:T(8,128)S(1)}, f32[2,2,5,2,8,128]{5,4,3,2,1,0:T(8,128)S(1)}) custom-call(s32[4]{0:T(128)} %refs_2_.5, f32[2,2,4,6,8,128]{5,4,3,2,1,0:T(8,128)S(1)} %get-tuple-element.32.refs_1_.refs_8_, f32[2,3,8,128]{3,2,1,0:T(8,128)S(1)} %get-tuple-element.33.refs_2_, ...), custom_call_target="tpu_custom_call" | custom-call | flops 4000000 | bytes 4194304 | tf_op jit(solution)/shard_map/prepare/pallas_call | solution.py:103
  30.3 0.4 collective-permute-done.2.refs_1_
  30.7 6.2 %middle.1 = (f32[2,4,64,8,128]{4,3,2,1,0:T(8,128)S(1)}, f32[2,4,68,8,128]{4,3,2,1,0:T(8,128)S(1)}, f32[2,2,4,8,128]{4,3,2,1,0:T(8,128)S(1)}, f32[16,4,8,128]{3,2,1,0:T(8,128)S(1)}) custom-call(f32[4,2,2,8,128]{4,3,2,1,0:T(8,128)S(1)} %get-tuple-element.30.refs_0_, f32[4,2,2,8,128]{4,3,2,1,0:T(8,128)S(1)} %collective-permute-done.2.refs_1_, s32[4]{0:T(128)} %refs_2_.5, ...), custom_call_target="tpu_custom_call" | custom-call | flops 80000000 | bytes 4194304 | tf_op jit(solution)/shard_map/middle/pallas_call | solution.py:103
  36.9 13.3 %all_to_all.11.refs_0_ = f32[16,4,8,128]{3,2,1,0:T(8,128)S(1)} all-to-all(f32[16,4,8,128]{3,2,1,0:T(8,128)S(1)} %get-tuple-element.39), channel_id=1, replica_groups=mesh['groups'=2,'depth'=16] {'depth'}, dimensions={0} | all-to-all | bytes 524288 | tf_op jit(solution)/shard_map/all_to_all | solution.py:884
  50.1 0.1 chain.3
  50.3 0.1 collective-permute-start.3
  50.3 1.2 %collective-permute-done.3.refs_1_ = f32[4,2,2,8,128]{4,3,2,1,0:T(8,128)S(1)} collective-permute-done((f32[4,2,2,8,128]{4,3,2,1,0:T(8,128)S(1)}, f32[4,2,2,8,128]{4,3,2,1,0:T(8,128)S(1)}, u32[]{:S(2)}, u32[]{:S(2)}) %collective-permute-start.3) | collective-permute-done | bytes 65568 | tf_op jit(solution)/shard_map/ppermute | solution.py:860
  51.6 4.6 %final.1 = f32[2,4,64,8,128]{4,3,2,1,0:T(8,128)} custom-call(f32[4,2,2,8,128]{4,3,2,1,0:T(8,128)S(1)} %get-tuple-element.41.refs_0_, f32[4,2,2,8,128]{4,3,2,1,0:T(8,128)S(1)} %collective-permute-done.3.refs_1_, f32[2,2,4,8,128]{4,3,2,1,0:T(8,128)S(1)} %get-tuple-element.40.refs_2_, f32[30,8,128]{2,1,0:T(8,128)S(1)} %get-tuple-element.27.refs_2_.refs_5_.refs_3_, ...), custom_call_target="tpu_custom_call" | custom-call | flops 60000000 | bytes 4194304 | tf_op jit(solution)/shard_map/final/pallas_call | solution.py:103
Async XLA Ops:
  1.1 5.2 %collective-permute-start = (f32[50,8,128]{2,1,0:T(8,128)S(1)}, f32[50,8,128]{2,1,0:T(8,128)S(1)}, u32[]{:S(2)}, u32[]{:S(2)}) collective-permute-start(f32[50,8,128]{2,1,0:T(8,128)S(1)} %get-tuple-element.25), channel_id=1, source_target_pairs={{0,1},{1,0},{2,3},{3,2},{4,5},{5,4},{6,7},{7,6},{8,9},{9,8},{10,11... | collective-permute-start | bytes 614408 | tf_op jit(solution)/shard_map/ppermute | solution.py:810
  1.7 27.9 %copy-start = (f32[2,4,64,8,128]{4,3,2,1,0:T(8,128)S(1)}, f32[2,4,64,8,128]{4,3,2,1,0:T(8,128)}, u32[]{:S(2)}) copy-start(f32[2,4,64,8,128]{4,3,2,1,0:T(8,128)} %refs_12_.1) | copy-start | bytes 6291460
  1.7 27.9 %copy-start.1 = (f32[2,4,8,128]{3,2,1,0:T(8,128)S(1)}, f32[2,4,8,128]{3,2,1,0:T(8,128)}, u32[]{:S(2)}) copy-start(f32[2,4,8,128]{3,2,1,0:T(8,128)} %refs_4_.5) | copy-start | bytes 98308
  1.7 4.6 %collective-permute-start.1 = (f32[50,8,128]{2,1,0:T(8,128)S(1)}, f32[50,8,128]{2,1,0:T(8,128)S(1)}, u32[]{:S(2)}, u32[]{:S(2)}) collective-permute-start(f32[50,8,128]{2,1,0:T(8,128)S(1)} %get-tuple-element.26), channel_id=1, source_target_pairs={{1,2},{3,4},{5,6},{7,8},{9,10},{11,12},{13,14},{2,1},{4,3},{6,5},{... | collective-permute-start | bytes 614408 | tf_op jit(solution)/shard_map/ppermute | solution.py:809
  29.4 1.3 %collective-permute-start.2 = (f32[4,2,2,8,128]{4,3,2,1,0:T(8,128)S(1)}, f32[4,2,2,8,128]{4,3,2,1,0:T(8,128)S(1)}, u32[]{:S(2)}, u32[]{:S(2)}) collective-permute-start(f32[4,2,2,8,128]{4,3,2,1,0:T(8,128)S(1)} %get-tuple-element.31), channel_id=1, source_target_pairs={{0,1},{1,0},{2,3},{3,2},{4,5},{5,4},{6,7},{7,6},{8,9},{9,8},{10,11... | collective-permute-start | bytes 196616 | tf_op jit(solution)/shard_map/ppermute | solution.py:860
  50.3 1.3 %collective-permute-start.3 = (f32[4,2,2,8,128]{4,3,2,1,0:T(8,128)S(1)}, f32[4,2,2,8,128]{4,3,2,1,0:T(8,128)S(1)}, u32[]{:S(2)}, u32[]{:S(2)}) collective-permute-start(f32[4,2,2,8,128]{4,3,2,1,0:T(8,128)S(1)} %get-tuple-element.42), channel_id=1, source_target_pairs={{0,1},{1,0},{2,3},{3,2},{4,5},{5,4},{6,7},{7,6},{8,9},{9,8},{10,11... | collective-permute-start | bytes 196616 | tf_op jit(solution)/shard_map/ppermute | solution.py:860

commit v6 on v5

--- a/solution.py
+++ b/solution.py
@@ -262,27 +262,29 @@
     return pl.ds(MEDIA + 4 + (2 * way + part) * count, count)
 
 
+def side_tiles(count):
+    return 2 * count * DEEP
+
+
 def pack_kernel(start, send, given, made, rest):
     kk, absorb, labels, guess = given
+    (out,) = made
     _, count, slab, *_ = guess.shape
     even = lax.rem(lax.axis_index("depth"), 2) == 0
-    top = slab - DEEP
-    for out, first in zip(made, (jnp.where(even, top, 0), jnp.where(even, 0, top))):
-        for i in range(2 * count):
-            send(
-                guess.at[i // count, i % count, pl.ds(first, DEEP)],
-                out.at[pl.ds(i * DEEP, DEEP)],
-            )
+    first = jnp.where(even, 0, slab - DEEP)
+    for i in range(2 * count):
+        send(
+            guess.at[i // count, i % count, pl.ds(first, DEEP)],
+            out.at[pl.ds(i * DEEP, DEEP)],
+        )
     kk, absorb, labels = kk.wait(), absorb.wait(), labels.wait()
-    squared = region_values(labels[0], kk)
-    for out in made:
-        out[2 * count * DEEP] = absorb[0]
-        out[2 * count * DEEP + 1] = squared
+    out[side_tiles(count)] = absorb[0]
+    out[side_tiles(count) + 1] = region_values(labels[0], kk)
 
 
 def start_kernel(start, send, given, made, rest):
     plan, kk, damp, sources, absorb, labels, guess = given
-    residual, pack, power = made
+    residual, pack, power, for_even = made
     loaded, emits, ref = rest
     _, count, slab, height, breadth = guess.shape
     tile = (height, breadth)
@@ -318,13 +320,13 @@
     squared = region_values(labels[0], kk)
     factor = set_media(media, squared, layer, absorb[0], slab)
     diagonal, layer3 = media[DIAGONAL], media[LAYER]
+    inverse = pair(media, INVERSE)
 
     def plane(k, carry):
         toward_next, toward_prev, w = carry
         power[k, 0], power[k, 1] = w
         r = field.minus_a(k, diagonal, layer3, lanes.now)
-        for part in range(2):
-            residual[part, :, k] = r[part]
+        residual[0, :, k], residual[1, :, k] = cmul(inverse, r)
         toward_next = add(cmul(factor, toward_next), r)
         toward_prev = add(toward_prev, cmul(w, r))
         return toward_next, toward_prev, cmul(factor, w)
@@ -352,7 +354,7 @@
             carry = plane(k, carry)
     toward_next, toward_prev, w = carry
     power[slab, 0], power[slab, 1] = w
-    add_forcing(plan, residual, sources, 0, slab)
+    add_forcing(plan, residual, sources, 0, slab, inverse)
     for part in range(2):
         emits[0, part] = toward_next[part]
         emits[1, part] = toward_prev[part]
@@ -362,17 +364,27 @@
     for way in range(2):
         for part in range(2):
             pack[emit_tiles(count, way, part)] = emits[way, part]
-
-
-def add_forcing(plan, held, sources, reach, slab):
+    first_plane = jnp.where(lax.rem(lax.axis_index("depth"), 2) == 0, slab - DEEP, 0)
+    for i in range(2 * count):
+        for_even[pl.ds(i * DEEP, DEEP)] = loaded[
+            i // count, i % count, pl.ds(first_plane, DEEP)
+        ]
+    for_even[side_tiles(count)] = absorb[0]
+    for_even[side_tiles(count) + 1] = squared
+
+
+def add_forcing(plan, held, sources, reach, slab, inverse=None):
     first_plane = lax.axis_index("depth") * slab
     for s in range(sources.shape[1]):
         k = plan[s] - first_plane
 
         @pl.when((k >= -reach) & (k < slab + reach))
         def _():
+            src = sources[0, s], sources[1, s]
+            if inverse is not None:
+                src = cmul(inverse, src)
             for part in range(2):
-                held[part, s, k + reach] += sources[part, s]
+                held[part, s, k + reach] += src[part]
 
 
 def force_emits(plan, emits, sources, power, slab):
@@ -502,6 +514,7 @@
         lanes = Lanes(field, masks)
         for i in range(1, DEEP):
             r = field.minus_a(i, near_media[side, DIAGONAL], layer3, lanes.now)
+            r = cmul(pair(near_media.at[side], INVERSE), r)
             for part in range(2):
                 res[side, part, :, i - 1] = r[part]
     plan = plan.wait()
@@ -512,8 +525,10 @@
 
             @pl.when((i >= 0) & (i < edge))
             def _():
+                src = sources[0, s], sources[1, s]
+                src = cmul(pair(near_media.at[side], INVERSE), src)
                 for part in range(2):
-                    res[side, part, s, i] += sources[part, s]
+                    res[side, part, s, i] += src[part]
 
 
 def chain_kernel(at, start, send, given, made, rest):
@@ -556,7 +571,11 @@
             theirs[i, part] = other[part]
 
 
-def set_incoming(ref, mine, theirs, full, passage):
+def set_incoming(ref, mine, theirs, full, passage, media, near_media):
+    inverses = [
+        scale(coupling, pair(m, INVERSE))
+        for m in (near_media.at[0], media, near_media.at[1])
+    ]
     even = lax.rem(lax.axis_index("depth"), 2) == 0
     count = full.shape[2]
     spots = ((0, 0), (1, 0), (1, 1), (2, 1))
@@ -572,8 +591,7 @@
         for (side, way), value in zip(
             spots + ((2, 0), (0, 1)), [*waves, onward, back]
         ):
-            for part in range(2):
-                ref[side, way, part, a:b] = coupling * value[part]
+            ref[side, way, 0, a:b], ref[side, way, 1, a:b] = cmul(inverses[side], value)
 
 
 class Stage:
@@ -646,8 +664,7 @@
         onward = incoming[which, 0, 0], incoming[which, 0, 1]
         back = incoming[which, 1, 0], incoming[which, 1, 1]
         c = add(cmul(on, onward), cmul(off, back))
-        inverse = pair(coefficients[which], INVERSE)
-        first_update.put_both(p, cmul(inverse, add(c, residual_of(which, p))))
+        first_update.put_both(p, add(c, residual_of(which, p)))
 
     def second(which, p):
         here, total = first_update.around(p, first_lanes.now)
@@ -690,16 +707,19 @@
     more = ext - 1
     new = Field(refs[2], -ext, height)
     new.clear()
-    set_incoming(incoming, mine, theirs, full, tile_of(power, slab))
+    set_incoming(
+        incoming, mine, theirs, full, tile_of(power, slab), media, near_media
+    )
 
     def residual_of(which, p):
         if which == 1:
             r = residual[0, :, p], residual[1, :, p]
+            lacks = None
             if isinstance(p, int) and p == 0:
-                r = add(r, (near[0, 0, :, DEEP - 1], near[0, 1, :, DEEP - 1]))
+                lacks = near[0, 0, :, DEEP - 1], near[0, 1, :, DEEP - 1]
             if isinstance(p, int) and p == slab - 1:
-                r = add(r, (near[1, 0, :, 0], near[1, 1, :, 0]))
-            return r
+                lacks = near[1, 0, :, 0], near[1, 1, :, 0]
+            return r if lacks is None else add(r, cmul(pair(media, INVERSE), lacks))
         i = p + reach if which == 0 else p - slab
         return near_residual[which // 2, 0, :, i], near_residual[which // 2, 1, :, i]
 
@@ -751,6 +771,23 @@
     force_emits(plan, next_full, sources, power, slab)
     fill_send(slots, next_full, None)
     add_forcing(plan, new_residual, sources, more, slab)
+
+
+def scale_kernel(start, send, given, made, rest):
+    residual, pack, near_media = given
+    (out,) = made
+    planes = residual.shape[2]
+    reach = DEEP - 4
+
+    def one(p, m):
+        value = cmul(pair(m, INVERSE), (residual[0, :, p], residual[1, :, p]))
+        out[0, :, p], out[1, :, p] = value
+
+    media = media_of(pack)
+    for p in range(reach):
+        one(p, near_media.at[0])
+        one(planes - 1 - p, near_media.at[1])
+    loop(reach, planes - reach, lambda p, c: one(p, media) or c, 0, 8)
 
 
 def final_kernel(start, send, given, made, rest):
@@ -764,7 +801,9 @@
     tile = (height, breadth)
     reach = 2
     masks = lane_masks(tile)
-    set_incoming(incoming, mine, theirs, full, tile_of(power, slab))
+    set_incoming(
+        incoming, mine, theirs, full, tile_of(power, slab), media, near_media
+    )
 
     def residual_of(which, p):
         return residual[0, :, p + reach], residual[1, :, p + reach]
@@ -796,20 +835,19 @@
     planes = lambda n: (2, count, n) + tile
     scratch = lambda shape: pltpu.VMEM(shape, jnp.float32)
 
-    tiles = (2 * count * DEEP + 2,) + tile
-    for_even, for_odd = kernel_call(
+    tiles = (side_tiles(count) + 2,) + tile
+    (for_odd,) = kernel_call(
         pack_kernel,
         [(region_kk, "smem"), (absorb, "vmem"), (labels, "vmem"), (guess, "hbm")],
-        [(tiles, "direct")] * 2,
-        pieces=4 * count, cost=1_000_000, name="pack", limit=PACK,
+        [(tiles, "direct")],
+        pieces=2 * count, cost=1_000_000, name="pack", limit=PACK,
     )
     even_pairs = [(i, i ^ 1) for i in range(size)]
     odd_pairs = [(i, i + 1) for i in range(1, size - 1, 2)]
     odd_pairs += [(b, a) for a, b in odd_pairs]
     got_odd = lax.ppermute(for_odd, "depth", odd_pairs)
-    got_even = lax.ppermute(for_even, "depth", even_pairs)
-
-    residual, pack, power = kernel_call(
+
+    residual, pack, power, for_even = kernel_call(
         start_kernel,
         [
             (plan, "smem"), (region_kk, "smem"), (damp_cells, "smem"),
@@ -817,7 +855,7 @@
         ],
         [
             (planes(slab), "direct"), ((MEDIA + 4 + 4 * count,) + tile, "direct"),
-            ((slab + 1, 2) + tile, "direct"),
+            ((slab + 1, 2) + tile, "direct"), (tiles, "direct"),
         ],
         [
             scratch(planes(slab)), scratch((2, 2, count) + tile),
@@ -825,6 +863,7 @@
         ],
         pieces=PIECES, cost=20_000_000, name="start", limit=16,
     )
+    got_even = lax.ppermute(for_even, "depth", even_pairs)
     width = count // 2
     full, slots, near, extra = kernel_call(
         arrange_kernel,
@@ -882,12 +921,18 @@
         cost=80_000_000, name="middle", limit=20,
     )
     mine, theirs = chain(lax.all_to_all(slots, "depth", 0, 0), next_full)
+    (scaled,) = kernel_call(
+        scale_kernel,
+        [(new_residual, "direct"), (pack, "direct"), (near_media, "direct")],
+        [(planes(slab + 2 * (DEEP - 4)), "direct")],
+        cost=4_000_000, name="scale", limit=4,
+    )
     (out,) = kernel_call(
         final_kernel,
         [
             (mine, "direct"), (theirs, "direct"), (next_full, "direct"),
             (pack, "direct"), (near_media, "direct"), (waves, "direct"),
-            (power, "direct"), (new_residual, "direct"), (new_field, "direct"),
+            (power, "direct"), (scaled, "direct"), (new_field, "direct"),
         ],
         [(planes(slab), "hbm")],
         [

time: 56.5 us -> 56 us (level)
  blocking collectives: 36.1 us -> 30.8 us
  starting transfers between devices: 1.6 us -> 5.44 us
  waiting for transfers between devices: 1.64 us -> 2.42 us
    all_to_all x1, blocking collectives: 22.8 us -> 17.6 us  [local(): first_got = lax.all_to_all(slots, 'depth', 0, 0)]
    ppermute x1, starting transfers between devices: 0.56 us -> 4.38 us  [local(): got_even = lax.ppermute(for_even, 'depth', even_pairs)]
    ppermute x1, waiting for transfers between devices: 0.01 us -> 1.08 us  [local(): got_even = lax.ppermute(for_even, 'depth', even_pairs)]
    pallas_call x8 -> x9, Pallas kernels: 16.8 us -> 16.9 us  [kernel_call(): pl.pallas_call(kernel, out_shape=tuple((jax.ShapeDtypeStruct(s, jnp.float...]
  transfers between devices with their start and end apart: 4 -> 4, of which waited for: 2 -> 3; matrix products, arithmetic and copies ran while one was open for 0% -> 0% of each run, Pallas kernels for 8% -> 9%
where the time goes in v6:
time: 56 us; the launch traced here: 55.8 us
  blocking collectives  30.8 us (55%)
  Pallas kernels  16.9 us (30%)
  starting transfers between devices  5.44 us (10%)
  waiting for transfers between devices  2.42 us (4%)
    all_to_all x1, blocking collectives, local(): first_got = lax.all_to_all(slots, 'depth', 0, 0)  17.6 us
    pallas_call x9, Pallas kernels, kernel_call(): pl.pallas_call(kernel, out_shape=tuple((jax.ShapeDtypeStruct(s, jnp.float...  16.9 us
    all_to_all x1, blocking collectives, local(): mine, theirs = chain(lax.all_to_all(slots, 'depth', 0, 0), next_full)  13.3 us
    ppermute x1, starting transfers between devices, local(): got_even = lax.ppermute(for_even, 'depth', even_pairs)  4.38 us
    ppermute x2, waiting for transfers between devices, chain(): return (mine, lax.ppermute(theirs, 'depth', even_pairs))  1.34 us
  transfers between devices with their start and end apart: 4, of which 3 were waited for; matrix products, arithmetic and copies ran while one was open for 0% of the time, Pallas kernels for 9%

profile of v6, /device:TPU:0, one launch (start us, length us, event | category | flops | bytes accessed | tf_op | source)
XLA Modules:
  0.0 55.8 jit_solution(2611675115456142679)
XLA Ops:
  0.0 1.0 %pack.1 = f32[50,8,128]{2,1,0:T(8,128)S(1)} custom-call(f32[8]{0:T(128)} %refs_0_.4, f32[1,8,128]{2,1,0:T(8,128)} %refs_1_.3, s32[1,8,128]{2,1,0:T(8,128)} %refs_2_.4, f32[2,4,64,8,128]{4,3,2,1,0:T(8,128)} %refs_12_.1), custom_call_target="tpu_custom_call" | custom-call | flops 1000000 | bytes 4194304 | tf_op jit(solution)/shard_map/pack/pallas_call | solution.py:103
  1.0 0.0 copy-start
  1.0 0.0 copy-start.1
  1.0 0.8 %collective-permute-start.1 = (f32[50,8,128]{2,1,0:T(8,128)S(1)}, f32[50,8,128]{2,1,0:T(8,128)S(1)}, u32[]{:S(2)}, u32[]{:S(2)}) collective-permute-start(f32[50,8,128]{2,1,0:T(8,128)S(1)} %pack.1), channel_id=1, source_target_pairs={{1,2},{3,4},{5,6},{7,8},{9,10},{11,12},{13,14},{2,1},{4,3},{6,5},{... | collective-permute-start | bytes 614408 | tf_op jit(solution)/shard_map/ppermute | solution.py:848
  1.8 3.9 %start.1 = (f32[2,4,64,8,128]{4,3,2,1,0:T(8,128)S(1)}, f32[30,8,128]{2,1,0:T(8,128)S(1)}, f32[65,2,8,128]{3,2,1,0:T(8,128)S(1)}, f32[50,8,128]{2,1,0:T(8,128)S(1)}) custom-call(s32[4]{0:T(128)} %refs_2_.5, f32[8]{0:T(128)} %refs_0_.4, s32[128]{0:T(128)} %refs_2_.3, f32[2,4,8,128]{3,2,1,0:T(8,128)} %refs_4_.5, f32[1,8,128]{2,1,0:T(8,128)} %refs_1_.3, ...), custom_call_target="tpu_custom_call" | custom-call | flops 20000000 | bytes 4194304 | tf_op jit(solution)/shard_map/start/pallas_call | solution.py:103
  5.7 4.4 %collective-permute-start = (f32[50,8,128]{2,1,0:T(8,128)S(1)}, f32[50,8,128]{2,1,0:T(8,128)S(1)}, u32[]{:S(2)}, u32[]{:S(2)}) collective-permute-start(f32[50,8,128]{2,1,0:T(8,128)S(1)} %get-tuple-element.24), channel_id=1, source_target_pairs={{0,1},{1,0},{2,3},{3,2},{4,5},{5,4},{6,7},{7,6},{8,9},{9,8},{10,11... | collective-permute-start | bytes 614408 | tf_op jit(solution)/shard_map/ppermute | solution.py:866
  10.1 0.0 collective-permute-done.1.refs_1_
  10.1 1.1 %collective-permute-done.refs_0_ = f32[50,8,128]{2,1,0:T(8,128)S(1)} collective-permute-done((f32[50,8,128]{2,1,0:T(8,128)S(1)}, f32[50,8,128]{2,1,0:T(8,128)S(1)}, u32[]{:S(2)}, u32[]{:S(2)}) %collective-permute-start) | collective-permute-done | bytes 204832 | tf_op jit(solution)/shard_map/ppermute | solution.py:866
  11.2 0.1 arrange.1
  11.3 17.6 %all_to_all.10.refs_0_.refs_1_ = f32[16,6,8,128]{3,2,1,0:T(8,128)S(1)} all-to-all(f32[16,6,8,128]{3,2,1,0:T(8,128)S(1)} %get-tuple-element.26), channel_id=1, replica_groups=mesh['groups'=2,'depth'=16] {'depth'}, dimensions={0} | all-to-all | bytes 786432 | tf_op jit(solution)/shard_map/all_to_all | solution.py:877
  28.9 0.1 chain.2
  29.0 0.2 collective-permute-start.2
  29.2 0.0 copy-done
  29.2 0.0 copy-done.1
  29.2 0.7 %prepare.1 = (f32[2,2,4,5,8,128]{5,4,3,2,1,0:T(8,128)S(1)}, f32[2,10,8,128]{3,2,1,0:T(8,128)S(1)}, f32[2,2,5,2,8,128]{5,4,3,2,1,0:T(8,128)S(1)}) custom-call(s32[4]{0:T(128)} %refs_2_.5, f32[2,2,4,6,8,128]{5,4,3,2,1,0:T(8,128)S(1)} %get-tuple-element.30.refs_1_.refs_8_, f32[2,3,8,128]{3,2,1,0:T(8,128)S(1)} %get-tuple-element.31.refs_2_, ...), custom_call_target="tpu_custom_call" | custom-call | flops 4000000 | bytes 4194304 | tf_op jit(solution)/shard_map/prepare/pallas_call | solution.py:103
  29.9 0.4 collective-permute-done.2.refs_1_
  30.3 6.1 %middle.1 = (f32[2,4,64,8,128]{4,3,2,1,0:T(8,128)S(1)}, f32[2,4,68,8,128]{4,3,2,1,0:T(8,128)S(1)}, f32[2,2,4,8,128]{4,3,2,1,0:T(8,128)S(1)}, f32[16,4,8,128]{3,2,1,0:T(8,128)S(1)}) custom-call(f32[4,2,2,8,128]{4,3,2,1,0:T(8,128)S(1)} %get-tuple-element.28.refs_0_, f32[4,2,2,8,128]{4,3,2,1,0:T(8,128)S(1)} %collective-permute-done.2.refs_1_, s32[4]{0:T(128)} %refs_2_.5, ...), custom_call_target="tpu_custom_call" | custom-call | flops 80000000 | bytes 4194304 | tf_op jit(solution)/shard_map/middle/pallas_call | solution.py:103
  36.4 13.3 %all_to_all.11.refs_0_ = f32[16,4,8,128]{3,2,1,0:T(8,128)S(1)} all-to-all(f32[16,4,8,128]{3,2,1,0:T(8,128)S(1)} %get-tuple-element.37), channel_id=1, replica_groups=mesh['groups'=2,'depth'=16] {'depth'}, dimensions={0} | all-to-all | bytes 524288 | tf_op jit(solution)/shard_map/all_to_all | solution.py:923
  49.7 0.1 chain.3
  49.8 0.1 collective-permute-start.3
  49.9 0.3 scale.1.refs_7_
  50.2 1.0 %collective-permute-done.3.refs_1_ = f32[4,2,2,8,128]{4,3,2,1,0:T(8,128)S(1)} collective-permute-done((f32[4,2,2,8,128]{4,3,2,1,0:T(8,128)S(1)}, f32[4,2,2,8,128]{4,3,2,1,0:T(8,128)S(1)}, u32[]{:S(2)}, u32[]{:S(2)}) %collective-permute-start.3) | collective-permute-done | bytes 65568 | tf_op jit(solution)/shard_map/ppermute | solution.py:899
  51.1 4.6 %final.1 = f32[2,4,64,8,128]{4,3,2,1,0:T(8,128)} custom-call(f32[4,2,2,8,128]{4,3,2,1,0:T(8,128)S(1)} %get-tuple-element.39.refs_0_, f32[4,2,2,8,128]{4,3,2,1,0:T(8,128)S(1)} %collective-permute-done.3.refs_1_, f32[2,2,4,8,128]{4,3,2,1,0:T(8,128)S(1)} %get-tuple-element.38.refs_2_, f32[30,8,128]{2,1,0:T(8,128)S(1)} %get-tuple-element.25.refs_2_.refs_5_.refs_1_.refs_3_, ...), custom_call_target="tpu_custom_call" | custom-call | flops 60000000 | bytes 4194304 | tf_op jit(solution)/shard_map/final/pallas_call | solution.py:103
Async XLA Ops:
  1.0 28.2 %copy-start = (f32[2,4,64,8,128]{4,3,2,1,0:T(8,128)S(1)}, f32[2,4,64,8,128]{4,3,2,1,0:T(8,128)}, u32[]{:S(2)}) copy-start(f32[2,4,64,8,128]{4,3,2,1,0:T(8,128)} %refs_12_.1) | copy-start | bytes 6291460
  1.0 28.2 %copy-start.1 = (f32[2,4,8,128]{3,2,1,0:T(8,128)S(1)}, f32[2,4,8,128]{3,2,1,0:T(8,128)}, u32[]{:S(2)}) copy-start(f32[2,4,8,128]{3,2,1,0:T(8,128)} %refs_4_.5) | copy-start | bytes 98308
  1.0 9.1 %collective-permute-start.1 = (f32[50,8,128]{2,1,0:T(8,128)S(1)}, f32[50,8,128]{2,1,0:T(8,128)S(1)}, u32[]{:S(2)}, u32[]{:S(2)}) collective-permute-start(f32[50,8,128]{2,1,0:T(8,128)S(1)} %pack.1), channel_id=1, source_target_pairs={{1,2},{3,4},{5,6},{7,8},{9,10},{11,12},{13,14},{2,1},{4,3},{6,5},{... | collective-permute-start | bytes 614408 | tf_op jit(solution)/shard_map/ppermute | solution.py:848
  5.7 5.5 %collective-permute-start = (f32[50,8,128]{2,1,0:T(8,128)S(1)}, f32[50,8,128]{2,1,0:T(8,128)S(1)}, u32[]{:S(2)}, u32[]{:S(2)}) collective-permute-start(f32[50,8,128]{2,1,0:T(8,128)S(1)} %get-tuple-element.24), channel_id=1, source_target_pairs={{0,1},{1,0},{2,3},{3,2},{4,5},{5,4},{6,7},{7,6},{8,9},{9,8},{10,11... | collective-permute-start | bytes 614408 | tf_op jit(solution)/shard_map/ppermute | solution.py:866
  29.0 1.3 %collective-permute-start.2 = (f32[4,2,2,8,128]{4,3,2,1,0:T(8,128)S(1)}, f32[4,2,2,8,128]{4,3,2,1,0:T(8,128)S(1)}, u32[]{:S(2)}, u32[]{:S(2)}) collective-permute-start(f32[4,2,2,8,128]{4,3,2,1,0:T(8,128)S(1)} %get-tuple-element.29), channel_id=1, source_target_pairs={{0,1},{1,0},{2,3},{3,2},{4,5},{5,4},{6,7},{7,6},{8,9},{9,8},{10,11... | collective-permute-start | bytes 196616 | tf_op jit(solution)/shard_map/ppermute | solution.py:899
  49.8 1.3 %collective-permute-start.3 = (f32[4,2,2,8,128]{4,3,2,1,0:T(8,128)S(1)}, f32[4,2,2,8,128]{4,3,2,1,0:T(8,128)S(1)}, u32[]{:S(2)}, u32[]{:S(2)}) collective-permute-start(f32[4,2,2,8,128]{4,3,2,1,0:T(8,128)S(1)} %get-tuple-element.40), channel_id=1, source_target_pairs={{0,1},{1,0},{2,3},{3,2},{4,5},{5,4},{6,7},{7,6},{8,9},{9,8},{10,11... | collective-permute-start | bytes 196616 | tf_op jit(solution)/shard_map/ppermute | solution.py:899

commit v7 on v6

--- a/solution.py
+++ b/solution.py
@@ -16,8 +16,6 @@
 DEEP = 6
 UNROLL = 4
 LAG = UNROLL + 1
-PIECES = 4
-PACK = 4
 
 
 def cmul(a, b):
@@ -249,11 +247,6 @@
     return carry
 
 
-def cuts(planes, pieces=PIECES):
-    edges = [planes * i // pieces for i in range(pieces + 1)]
-    return list(zip(edges[:-1], edges[1:]))
-
-
 def media_of(pack):
     return pack.at[pl.ds(0, MEDIA)]
 
@@ -267,9 +260,9 @@
 
 
 def pack_kernel(start, send, given, made, rest):
-    kk, absorb, labels, guess = given
-    (out,) = made
-    _, count, slab, *_ = guess.shape
+    kk, damp, absorb, labels, guess = given
+    out, base = made
+    _, count, slab, *tile = guess.shape
     even = lax.rem(lax.axis_index("depth"), 2) == 0
     first = jnp.where(even, 0, slab - DEEP)
     for i in range(2 * count):
@@ -277,23 +270,32 @@
             guess.at[i // count, i % count, pl.ds(first, DEEP)],
             out.at[pl.ds(i * DEEP, DEEP)],
         )
+    row = lax.broadcasted_iota(jnp.int32, tuple(tile), 0)
+    lane = lax.broadcasted_iota(jnp.int32, tuple(tile), 1)
+    cell = row * tile[1] + lane
     kk, absorb, labels = kk.wait(), absorb.wait(), labels.wait()
+    squared = region_values(labels[0], kk)
     out[side_tiles(count)] = absorb[0]
-    out[side_tiles(count) + 1] = region_values(labels[0], kk)
+    out[side_tiles(count) + 1] = squared
+    base[MEDIA] = absorb[0]
+    base[MEDIA + 1] = squared
+    damp = damp.wait()
+
+    def mark(i, hit):
+        return jnp.where(cell == damp[i], 1.0, hit)
+
+    layer = loop(0, damp.shape[0], mark, jnp.zeros(tile, jnp.float32), 16)
+    set_media(base, squared, layer, absorb[0], slab)
 
 
 def start_kernel(start, send, given, made, rest):
-    plan, kk, damp, sources, absorb, labels, guess = given
+    plan, sources, base, guess = given
     residual, pack, power, for_even = made
-    loaded, emits, ref = rest
+    emits, ref = rest
     _, count, slab, height, breadth = guess.shape
     tile = (height, breadth)
     media = media_of(pack)
-    copies = []
-    edges = [0] + [min(b + UNROLL, slab) for _, b in cuts(slab)]
-    for a, b in zip(edges[:-1], edges[1:]):
-        part = pl.ds(a, b - a)
-        copies.append(start(guess.at[:, :, part], loaded.at[:, :, part]))
+    media[...] = base[:MEDIA]
     masks = lane_masks(tile)
     field = Field(ref, -1, height)
     zero = jnp.zeros((count,) + tile, jnp.float32)
@@ -301,26 +303,12 @@
     field.put_both(-1, (zero, zero))
     field.put_both(slab, (zero, zero))
     lanes = Lanes(field, masks)
+    diagonal, layer3 = media[DIAGONAL], media[LAYER]
+    inverse, factor = pair(media, INVERSE), pair(media, WAVE)
 
     def fill(p):
         for part in range(2):
-            value = loaded[part, :, p]
-            field.put(part, p, value)
-
-    plan, kk, damp = plan.wait(), kk.wait(), damp.wait()
-    row = lax.broadcasted_iota(jnp.int32, tile, 0)
-    lane = lax.broadcasted_iota(jnp.int32, tile, 1)
-    cell = row * breadth + lane
-
-    def mark(i, hit):
-        return jnp.where(cell == damp[i], 1.0, hit)
-
-    layer = loop(0, damp.shape[0], mark, jnp.zeros(tile, jnp.float32), 16)
-    sources, absorb, labels = sources.wait(), absorb.wait(), labels.wait()
-    squared = region_values(labels[0], kk)
-    factor = set_media(media, squared, layer, absorb[0], slab)
-    diagonal, layer3 = media[DIAGONAL], media[LAYER]
-    inverse = pair(media, INVERSE)
+            field.put(part, p, guess[part, :, p])
 
     def plane(k, carry):
         toward_next, toward_prev, w = carry
@@ -333,25 +321,23 @@
 
     one = jnp.ones(tile, jnp.float32), jnp.zeros(tile, jnp.float32)
     carry = ((zero, zero), (zero, zero), one)
-    for (a, b), copy in zip(cuts(slab), copies):
-        copy.wait()
-        if a == 0:
-            fill(0)
-
-        def group(trip, carry):
-            base = a + trip * UNROLL
-            for i in range(UNROLL):
-                fill(base + i + 1)
-            for i in range(UNROLL):
-                carry = plane(base + i, carry)
-            return carry
-
-        trips = (min(b, slab - 1) - a) // UNROLL
-        carry = lax.fori_loop(0, trips, group, carry)
-        for k in range(a + trips * UNROLL, b):
-            if k + 1 < slab:
-                fill(k + 1)
-            carry = plane(k, carry)
+    fill(0)
+
+    def group(trip, carry):
+        base = trip * UNROLL
+        for i in range(UNROLL):
+            fill(base + i + 1)
+        for i in range(UNROLL):
+            carry = plane(base + i, carry)
+        return carry
+
+    trips = (slab - 1) // UNROLL
+    carry = lax.fori_loop(0, trips, group, carry)
+    for k in range(trips * UNROLL, slab):
+        if k + 1 < slab:
+            fill(k + 1)
+        carry = plane(k, carry)
+    plan, sources = plan.wait(), sources.wait()
     toward_next, toward_prev, w = carry
     power[slab, 0], power[slab, 1] = w
     add_forcing(plan, residual, sources, 0, slab, inverse)
@@ -366,11 +352,10 @@
             pack[emit_tiles(count, way, part)] = emits[way, part]
     first_plane = jnp.where(lax.rem(lax.axis_index("depth"), 2) == 0, slab - DEEP, 0)
     for i in range(2 * count):
-        for_even[pl.ds(i * DEEP, DEEP)] = loaded[
+        for_even[pl.ds(i * DEEP, DEEP)] = guess[
             i // count, i % count, pl.ds(first_plane, DEEP)
         ]
-    for_even[side_tiles(count)] = absorb[0]
-    for_even[side_tiles(count) + 1] = squared
+    for_even[pl.ds(side_tiles(count), 2)] = base[MEDIA : MEDIA + 2]
 
 
 def add_forcing(plan, held, sources, reach, slab, inverse=None):
@@ -836,11 +821,14 @@
     scratch = lambda shape: pltpu.VMEM(shape, jnp.float32)
 
     tiles = (side_tiles(count) + 2,) + tile
-    (for_odd,) = kernel_call(
+    for_odd, base = kernel_call(
         pack_kernel,
-        [(region_kk, "smem"), (absorb, "vmem"), (labels, "vmem"), (guess, "hbm")],
-        [(tiles, "direct")],
-        pieces=2 * count, cost=1_000_000, name="pack", limit=PACK,
+        [
+            (region_kk, "smem"), (damp_cells, "smem"), (absorb, "vmem"),
+            (labels, "vmem"), (guess, "hbm"),
+        ],
+        [(tiles, "direct"), ((MEDIA + 2,) + tile, "direct")],
+        pieces=2 * count, cost=1_000_000, name="pack", limit=4,
     )
     even_pairs = [(i, i ^ 1) for i in range(size)]
     odd_pairs = [(i, i + 1) for i in range(1, size - 1, 2)]
@@ -850,18 +838,16 @@
     residual, pack, power, for_even = kernel_call(
         start_kernel,
         [
-            (plan, "smem"), (region_kk, "smem"), (damp_cells, "smem"),
-            (sources, "vmem"), (absorb, "vmem"), (labels, "vmem"), (guess, "hbm"),
+            (plan, "smem"), (sources, "vmem"), (base, "direct"), (guess, "direct"),
         ],
         [
             (planes(slab), "direct"), ((MEDIA + 4 + 4 * count,) + tile, "direct"),
             ((slab + 1, 2) + tile, "direct"), (tiles, "direct"),
         ],
         [
-            scratch(planes(slab)), scratch((2, 2, count) + tile),
-            Field.shape(count, slab + 2, tile),
-        ],
-        pieces=PIECES, cost=20_000_000, name="start", limit=16,
+            scratch((2, 2, count) + tile), Field.shape(count, slab + 2, tile),
+        ],
+        cost=20_000_000, name="start", limit=12,
     )
     got_even = lax.ppermute(for_even, "depth", even_pairs)
     width = count // 2

time: 56 us -> 56 us (level)
  blocking collectives: 30.8 us -> 32.1 us
  Pallas kernels: 16.9 us -> 15.9 us
    all_to_all x1, blocking collectives: 17.6 us -> 18.8 us  [local(): first_got = lax.all_to_all(slots, 'depth', 0, 0)]
    pallas_call x9, Pallas kernels: 16.9 us -> 15.9 us  [kernel_call(): pl.pallas_call(kernel, out_shape=tuple((jax.ShapeDtypeStruct(s, jnp.float...]
  transfers between devices with their start and end apart: 4 -> 4, of which waited for: 3 -> 3; matrix products, arithmetic and copies ran while one was open for 0% -> 0% of each run, Pallas kernels for 9% -> 7%
where the time goes in v7:
time: 56 us; the launch traced here: 55.8 us
  blocking collectives  32.1 us (57%)
  Pallas kernels  15.9 us (28%)
  starting transfers between devices  5.3 us (9%)
  waiting for transfers between devices  2.43 us (4%)
    all_to_all x1, blocking collectives, local(): first_got = lax.all_to_all(slots, 'depth', 0, 0)  18.8 us
    pallas_call x9, Pallas kernels, kernel_call(): pl.pallas_call(kernel, out_shape=tuple((jax.ShapeDtypeStruct(s, jnp.float...  15.9 us
    all_to_all x1, blocking collectives, local(): mine, theirs = chain(lax.all_to_all(slots, 'depth', 0, 0), next_full)  13.3 us
    ppermute x1, starting transfers between devices, local(): got_even = lax.ppermute(for_even, 'depth', even_pairs)  4.38 us
    ppermute x2, waiting for transfers between devices, chain(): return (mine, lax.ppermute(theirs, 'depth', even_pairs))  1.35 us
  transfers between devices with their start and end apart: 4, of which 3 were waited for; matrix products, arithmetic and copies ran while one was open for 0% of the time, Pallas kernels for 7%

profile of v7, /device:TPU:0, one launch (start us, length us, event | category | flops | bytes accessed | tf_op | source)
XLA Modules:
  0.0 55.8 jit_solution(12196520623358257572)
XLA Ops:
  0.0 0.0 copy-start
  0.0 1.1 %pack.1 = (f32[50,8,128]{2,1,0:T(8,128)S(1)}, f32[12,8,128]{2,1,0:T(8,128)S(1)}) custom-call(f32[8]{0:T(128)} %refs_0_.3, s32[128]{0:T(128)} %refs_1_.2, f32[1,8,128]{2,1,0:T(8,128)} %refs_2_.2, s32[1,8,128]{2,1,0:T(8,128)} %refs_3_.3, f32[2,4,64,8,128]{4,3,2,1,0:T(8,128)} %refs_12_.1), custom_call_target="tpu_custom_call" | custom-call | flops 1000000 | bytes 4194304 | tf_op jit(solution)/shard_map/pack/pallas_call | solution.py:101
  1.2 0.7 %collective-permute-start.1 = (f32[50,8,128]{2,1,0:T(8,128)S(1)}, f32[50,8,128]{2,1,0:T(8,128)S(1)}, u32[]{:S(2)}, u32[]{:S(2)}) collective-permute-start(f32[50,8,128]{2,1,0:T(8,128)S(1)} %get-tuple-element.28), channel_id=1, source_target_pairs={{1,2},{3,4},{5,6},{7,8},{9,10},{11,12},{13,14},{2,1},{4,3},{6,5},{... | collective-permute-start | bytes 614408 | tf_op jit(solution)/shard_map/ppermute | solution.py:836
  1.8 0.0 copy-done
  1.8 0.0 copy-start.1
  1.9 2.7 %start.1 = (f32[2,4,64,8,128]{4,3,2,1,0:T(8,128)S(1)}, f32[30,8,128]{2,1,0:T(8,128)S(1)}, f32[65,2,8,128]{3,2,1,0:T(8,128)S(1)}, f32[50,8,128]{2,1,0:T(8,128)S(1)}) custom-call(s32[4]{0:T(128)} %refs_2_.3, f32[2,4,8,128]{3,2,1,0:T(8,128)} %refs_4_.5, f32[12,8,128]{2,1,0:T(8,128)S(1)} %get-tuple-element.26.refs_2_, f32[2,4,64,8,128]{4,3,2,1,0:T(8,128)S(1)} %copy-done), custom_call_target="tpu_custom_call" | custom-call | flops 20000000 | bytes 4194304 | tf_op jit(solution)/shard_map/start/pallas_call | solution.py:101
  4.5 4.4 %collective-permute-start = (f32[50,8,128]{2,1,0:T(8,128)S(1)}, f32[50,8,128]{2,1,0:T(8,128)S(1)}, u32[]{:S(2)}, u32[]{:S(2)}) collective-permute-start(f32[50,8,128]{2,1,0:T(8,128)S(1)} %get-tuple-element.27), channel_id=1, source_target_pairs={{0,1},{1,0},{2,3},{3,2},{4,5},{5,4},{6,7},{7,6},{8,9},{9,8},{10,11... | collective-permute-start | bytes 614408 | tf_op jit(solution)/shard_map/ppermute | solution.py:852
  8.9 0.0 collective-permute-done.1.refs_1_
  8.9 1.1 %collective-permute-done.refs_0_ = f32[50,8,128]{2,1,0:T(8,128)S(1)} collective-permute-done((f32[50,8,128]{2,1,0:T(8,128)S(1)}, f32[50,8,128]{2,1,0:T(8,128)S(1)}, u32[]{:S(2)}, u32[]{:S(2)}) %collective-permute-start) | collective-permute-done | bytes 204832 | tf_op jit(solution)/shard_map/ppermute | solution.py:852
  10.0 0.1 arrange.1
  10.1 18.8 %all_to_all.10.refs_0_.refs_1_ = f32[16,6,8,128]{3,2,1,0:T(8,128)S(1)} all-to-all(f32[16,6,8,128]{3,2,1,0:T(8,128)S(1)} %get-tuple-element.30), channel_id=1, replica_groups=mesh['groups'=2,'depth'=16] {'depth'}, dimensions={0} | all-to-all | bytes 786432 | tf_op jit(solution)/shard_map/all_to_all | solution.py:863
  28.9 0.1 chain.2
  29.0 0.2 collective-permute-start.2
  29.2 0.0 copy-done.1
  29.2 0.7 %prepare.1 = (f32[2,2,4,5,8,128]{5,4,3,2,1,0:T(8,128)S(1)}, f32[2,10,8,128]{3,2,1,0:T(8,128)S(1)}, f32[2,2,5,2,8,128]{5,4,3,2,1,0:T(8,128)S(1)}) custom-call(s32[4]{0:T(128)} %refs_2_.3, f32[2,2,4,6,8,128]{5,4,3,2,1,0:T(8,128)S(1)} %get-tuple-element.34.refs_1_.refs_8_, f32[2,3,8,128]{3,2,1,0:T(8,128)S(1)} %get-tuple-element.35.refs_2_, ...), custom_call_target="tpu_custom_call" | custom-call | flops 4000000 | bytes 4194304 | tf_op jit(solution)/shard_map/prepare/pallas_call | solution.py:101
  29.9 0.4 collective-permute-done.2.refs_1_
  30.3 6.1 %middle.1 = (f32[2,4,64,8,128]{4,3,2,1,0:T(8,128)S(1)}, f32[2,4,68,8,128]{4,3,2,1,0:T(8,128)S(1)}, f32[2,2,4,8,128]{4,3,2,1,0:T(8,128)S(1)}, f32[16,4,8,128]{3,2,1,0:T(8,128)S(1)}) custom-call(f32[4,2,2,8,128]{4,3,2,1,0:T(8,128)S(1)} %get-tuple-element.32.refs_0_, f32[4,2,2,8,128]{4,3,2,1,0:T(8,128)S(1)} %collective-permute-done.2.refs_1_, s32[4]{0:T(128)} %refs_2_.3, ...), custom_call_target="tpu_custom_call" | custom-call | flops 80000000 | bytes 4194304 | tf_op jit(solution)/shard_map/middle/pallas_call | solution.py:101
  36.4 13.3 %all_to_all.11.refs_0_ = f32[16,4,8,128]{3,2,1,0:T(8,128)S(1)} all-to-all(f32[16,4,8,128]{3,2,1,0:T(8,128)S(1)} %get-tuple-element.41), channel_id=1, replica_groups=mesh['groups'=2,'depth'=16] {'depth'}, dimensions={0} | all-to-all | bytes 524288 | tf_op jit(solution)/shard_map/all_to_all | solution.py:909
  49.7 0.1 chain.3
  49.8 0.1 collective-permute-start.3
  49.9 0.3 scale.1.refs_7_
  50.2 1.0 %collective-permute-done.3.refs_1_ = f32[4,2,2,8,128]{4,3,2,1,0:T(8,128)S(1)} collective-permute-done((f32[4,2,2,8,128]{4,3,2,1,0:T(8,128)S(1)}, f32[4,2,2,8,128]{4,3,2,1,0:T(8,128)S(1)}, u32[]{:S(2)}, u32[]{:S(2)}) %collective-permute-start.3) | collective-permute-done | bytes 65568 | tf_op jit(solution)/shard_map/ppermute | solution.py:885
  51.2 4.6 %final.1 = f32[2,4,64,8,128]{4,3,2,1,0:T(8,128)} custom-call(f32[4,2,2,8,128]{4,3,2,1,0:T(8,128)S(1)} %get-tuple-element.43.refs_0_, f32[4,2,2,8,128]{4,3,2,1,0:T(8,128)S(1)} %collective-permute-done.3.refs_1_, f32[2,2,4,8,128]{4,3,2,1,0:T(8,128)S(1)} %get-tuple-element.42.refs_2_, f32[30,8,128]{2,1,0:T(8,128)S(1)} %get-tuple-element.29.refs_2_.refs_5_.refs_1_.refs_3_, ...), custom_call_target="tpu_custom_call" | custom-call | flops 60000000 | bytes 4194304 | tf_op jit(solution)/shard_map/final/pallas_call | solution.py:101
Async XLA Ops:
  0.0 1.8 %copy-start = (f32[2,4,64,8,128]{4,3,2,1,0:T(8,128)S(1)}, f32[2,4,64,8,128]{4,3,2,1,0:T(8,128)}, u32[]{:S(2)}) copy-start(f32[2,4,64,8,128]{4,3,2,1,0:T(8,128)} %refs_12_.1) | copy-start | bytes 6291460
  1.2 7.8 %collective-permute-start.1 = (f32[50,8,128]{2,1,0:T(8,128)S(1)}, f32[50,8,128]{2,1,0:T(8,128)S(1)}, u32[]{:S(2)}, u32[]{:S(2)}) collective-permute-start(f32[50,8,128]{2,1,0:T(8,128)S(1)} %get-tuple-element.28), channel_id=1, source_target_pairs={{1,2},{3,4},{5,6},{7,8},{9,10},{11,12},{13,14},{2,1},{4,3},{6,5},{... | collective-permute-start | bytes 614408 | tf_op jit(solution)/shard_map/ppermute | solution.py:836
  1.8 27.3 %copy-start.1 = (f32[2,4,8,128]{3,2,1,0:T(8,128)S(1)}, f32[2,4,8,128]{3,2,1,0:T(8,128)}, u32[]{:S(2)}) copy-start(f32[2,4,8,128]{3,2,1,0:T(8,128)} %refs_4_.5) | copy-start | bytes 98308
  4.5 5.5 %collective-permute-start = (f32[50,8,128]{2,1,0:T(8,128)S(1)}, f32[50,8,128]{2,1,0:T(8,128)S(1)}, u32[]{:S(2)}, u32[]{:S(2)}) collective-permute-start(f32[50,8,128]{2,1,0:T(8,128)S(1)} %get-tuple-element.27), channel_id=1, source_target_pairs={{0,1},{1,0},{2,3},{3,2},{4,5},{5,4},{6,7},{7,6},{8,9},{9,8},{10,11... | collective-permute-start | bytes 614408 | tf_op jit(solution)/shard_map/ppermute | solution.py:852
  29.0 1.3 %collective-permute-start.2 = (f32[4,2,2,8,128]{4,3,2,1,0:T(8,128)S(1)}, f32[4,2,2,8,128]{4,3,2,1,0:T(8,128)S(1)}, u32[]{:S(2)}, u32[]{:S(2)}) collective-permute-start(f32[4,2,2,8,128]{4,3,2,1,0:T(8,128)S(1)} %get-tuple-element.33), channel_id=1, source_target_pairs={{0,1},{1,0},{2,3},{3,2},{4,5},{5,4},{6,7},{7,6},{8,9},{9,8},{10,11... | collective-permute-start | bytes 196616 | tf_op jit(solution)/shard_map/ppermute | solution.py:885
  49.8 1.3 %collective-permute-start.3 = (f32[4,2,2,8,128]{4,3,2,1,0:T(8,128)S(1)}, f32[4,2,2,8,128]{4,3,2,1,0:T(8,128)S(1)}, u32[]{:S(2)}, u32[]{:S(2)}) collective-permute-start(f32[4,2,2,8,128]{4,3,2,1,0:T(8,128)S(1)} %get-tuple-element.44), channel_id=1, source_target_pairs={{0,1},{1,0},{2,3},{3,2},{4,5},{5,4},{6,7},{7,6},{8,9},{9,8},{10,11... | collective-permute-start | bytes 196616 | tf_op jit(solution)/shard_map/ppermute | solution.py:885

commit v8 on v7

--- a/solution.py
+++ b/solution.py
@@ -387,22 +387,58 @@
                 emits[1, part, s] += back[part]
 
 
-def halves(count):
-    return (0, count // 2), (count // 2, count)
+class Split:
+    def __init__(self, tile):
+        self.half = tile[0] // 2
+        self.upper = lax.broadcasted_iota(jnp.int32, tile, 0) < self.half
+
+    def turn(self, value):
+        return pltpu.roll(value, self.half, value.ndim - 2)
+
+    def pack(self, core, first, second):
+        if core == 0:
+            return jnp.where(self.upper, first, self.turn(second))
+        return jnp.where(self.upper, self.turn(first), second)
+
+    def unpack(self, core_0, core_1):
+        first = jnp.where(self.upper, core_0, self.turn(core_1))
+        second = jnp.where(self.upper, self.turn(core_0), core_1)
+        return first, second
+
+    def spread(self, packed):
+        turned = self.turn(packed)
+        return jnp.where(self.upper, packed, turned), jnp.where(self.upper, turned, packed)
+
+
+def pack_waves(split, core, full, way):
+    count = full.shape[2]
+    return tuple(
+        jnp.stack(
+            [
+                split.pack(core, full[way, part, s], full[way, part, s + 1])
+                for s in range(0, count, 2)
+            ]
+        )
+        for part in range(2)
+    )
 
 
 def fill_send(slots, full, passage):
     place = lax.axis_index("depth")
+    width = full.shape[2] // 2
+    split = Split(full.shape[3:])
+    waves = [[pack_waves(split, core, full, way) for way in range(2)] for core in range(2)]
 
     def one(chip, unused):
-        for core, (a, b) in enumerate(halves(full.shape[2])):
+        for core in range(2):
             j = 2 * chip + core
-            way = jnp.where(j > place, 0, 1)
+            onward, back = waves[core]
             for part in range(2):
-                slots[j, pl.ds(part * (b - a), b - a)] = full[way, part, a:b]
+                slots[j, pl.ds(part * width, width)] = jnp.where(
+                    j > place, onward[part], back[part]
+                )
             if passage is not None:
-                slots[j, 2 * (b - a)] = passage[0]
-                slots[j, 2 * (b - a) + 1] = passage[1]
+                slots[j, 2 * width] = split.pack(core, *passage)
         return unused
 
     loop(0, slots.shape[0] // 2, one, 0, 4)
@@ -516,21 +552,20 @@
                     res[side, part, s, i] += src[part]
 
 
-def chain_kernel(at, start, send, given, made, rest):
+def chain_kernel(start, send, given, made, rest):
     got, passages, full = given
     mine, theirs = made
     place = lax.axis_index("depth")
     last_place = lax.axis_size("depth") - 1
-    count = full.shape[2]
+    width = full.shape[2] // 2
+    split = Split(full.shape[3:])
     even = lax.rem(place, 2) == 0
     low = place - lax.rem(place, 2)
     high = low + 1
-    (a, b), (c, d) = halves(count)
-    width = b - a
     zero = jnp.zeros((width,) + full.shape[3:], jnp.float32)
-    passage = lambda j: (passages[j, at], passages[j, at + 1])
-    emit = lambda way: tuple(
-        jnp.where(even, full[way, part, a:b], full[way, part, c:d]) for part in range(2)
+    passage = lambda j: split.spread(passages[j, 2 * width])
+    emit = lambda way: pick(
+        even, pack_waves(split, 0, full, way), pack_waves(split, 1, full, way)
     )
     came = lambda j: (got[j, pl.ds(0, width)], got[j, pl.ds(width, width)])
 
@@ -563,20 +598,22 @@
     ]
     even = lax.rem(lax.axis_index("depth"), 2) == 0
     count = full.shape[2]
-    spots = ((0, 0), (1, 0), (1, 1), (2, 1))
-    for half, (a, b) in enumerate(halves(count)):
-        own = even if half == 0 else jnp.logical_not(even)
-        waves = [
-            tuple(jnp.where(own, mine[i, part], theirs[i, part]) for part in range(2))
-            for i in range(4)
-        ]
-        here = lambda way: (full[way, 0, a:b], full[way, 1, a:b])
-        onward = add(cmul(passage, waves[1]), here(0))
-        back = add(cmul(passage, waves[2]), here(1))
-        for (side, way), value in zip(
-            spots + ((2, 0), (0, 1)), [*waves, onward, back]
-        ):
-            ref[side, way, 0, a:b], ref[side, way, 1, a:b] = cmul(inverses[side], value)
+    split = Split(full.shape[3:])
+    waves = []
+    for i in range(4):
+        parts = []
+        for part in range(2):
+            own, other = mine[i, part], theirs[i, part]
+            first, second = split.unpack(
+                jnp.where(even, own, other), jnp.where(even, other, own)
+            )
+            parts.append(jnp.stack([first, second], 1).reshape(full.shape[2:]))
+        waves.append(tuple(parts))
+    onward = add(cmul(passage, waves[1]), (full[0, 0], full[0, 1]))
+    back = add(cmul(passage, waves[2]), (full[1, 0], full[1, 1]))
+    spots = ((0, 0), (1, 0), (1, 1), (2, 1), (2, 0), (0, 1))
+    for (side, way), value in zip(spots, [*waves, onward, back]):
+        ref[side, way, 0], ref[side, way, 1] = cmul(inverses[side], value)
 
 
 class Stage:
@@ -855,7 +892,7 @@
         arrange_kernel,
         [(got_even, "direct"), (got_odd, "direct"), (pack, "direct")],
         [
-            ((2, 2, count) + tile, "direct"), ((size, 2 * width + 2) + tile, "direct"),
+            ((2, 2, count) + tile, "direct"), ((size, 2 * width + 1) + tile, "direct"),
             ((2, 2, count, DEEP) + tile, "direct"), ((2, 3) + tile, "direct"),
         ],
         cost=1_000_000, name="arrange", limit=4,
@@ -877,7 +914,7 @@
 
     def chain(got, full):
         mine, theirs = kernel_call(
-            functools.partial(chain_kernel, 2 * width),
+            chain_kernel,
             [(got, "direct"), (first_got, "direct"), (full, "direct")],
             [((4, 2, width) + tile, "direct")] * 2,
             cost=1_000_000, name="chain", limit=4,

time: 56 us -> 54.6 us (0.975)
  blocking collectives: 32.1 us -> 30.7 us
    all_to_all x1, blocking collectives: 18.8 us -> 17.7 us  [local(): first_got = lax.all_to_all(slots, 'depth', 0, 0)]
where the time goes in v8:
time: 54.6 us; the launch traced here: 54.4 us
  blocking collectives  30.7 us (56%)
  Pallas kernels  15.9 us (29%)
  starting transfers between devices  5.3 us (10%)
  waiting for transfers between devices  2.43 us (4%)
    all_to_all x1, blocking collectives, local(): first_got = lax.all_to_all(slots, 'depth', 0, 0)  17.7 us
    pallas_call x9, Pallas kernels, kernel_call(): pl.pallas_call(kernel, out_shape=tuple((jax.ShapeDtypeStruct(s, jnp.float...  15.9 us
    all_to_all x1, blocking collectives, local(): mine, theirs = chain(lax.all_to_all(slots, 'depth', 0, 0), next_full)  13 us
    ppermute x1, starting transfers between devices, local(): got_even = lax.ppermute(for_even, 'depth', even_pairs)  4.38 us
    ppermute x2, waiting for transfers between devices, chain(): return (mine, lax.ppermute(theirs, 'depth', even_pairs))  1.35 us
  transfers between devices with their start and end apart: 4, of which 3 were waited for; matrix products, arithmetic and copies ran while one was open for 0% of the time, Pallas kernels for 7%

profile of v8, /device:TPU:0, one launch (start us, length us, event | category | flops | bytes accessed | tf_op | source)
XLA Modules:
  0.0 54.4 jit_solution(10887832819729011230)
XLA Ops:
  0.0 0.0 copy-start
  0.0 1.1 %pack.1 = (f32[50,8,128]{2,1,0:T(8,128)S(1)}, f32[12,8,128]{2,1,0:T(8,128)S(1)}) custom-call(f32[8]{0:T(128)} %refs_0_.3, s32[128]{0:T(128)} %refs_1_.2, f32[1,8,128]{2,1,0:T(8,128)} %refs_2_.2, s32[1,8,128]{2,1,0:T(8,128)} %refs_3_.3, f32[2,4,64,8,128]{4,3,2,1,0:T(8,128)} %refs_12_.1), custom_call_target="tpu_custom_call" | custom-call | flops 1000000 | bytes 4194304 | tf_op jit(solution)/shard_map/pack/pallas_call | solution.py:101
  1.2 0.0 copy-start.1
  1.2 0.7 %collective-permute-start.1 = (f32[50,8,128]{2,1,0:T(8,128)S(1)}, f32[50,8,128]{2,1,0:T(8,128)S(1)}, u32[]{:S(2)}, u32[]{:S(2)}) collective-permute-start(f32[50,8,128]{2,1,0:T(8,128)S(1)} %get-tuple-element.28), channel_id=1, source_target_pairs={{1,2},{3,4},{5,6},{7,8},{9,10},{11,12},{13,14},{2,1},{4,3},{6,5},{... | collective-permute-start | bytes 614408 | tf_op jit(solution)/shard_map/ppermute | solution.py:873
  1.9 0.0 copy-done
  1.9 2.7 %start.1 = (f32[2,4,64,8,128]{4,3,2,1,0:T(8,128)S(1)}, f32[30,8,128]{2,1,0:T(8,128)S(1)}, f32[65,2,8,128]{3,2,1,0:T(8,128)S(1)}, f32[50,8,128]{2,1,0:T(8,128)S(1)}) custom-call(s32[4]{0:T(128)} %refs_2_.3, f32[2,4,8,128]{3,2,1,0:T(8,128)} %refs_4_.5, f32[12,8,128]{2,1,0:T(8,128)S(1)} %get-tuple-element.26.refs_2_, f32[2,4,64,8,128]{4,3,2,1,0:T(8,128)S(1)} %copy-done), custom_call_target="tpu_custom_call" | custom-call | flops 20000000 | bytes 4194304 | tf_op jit(solution)/shard_map/start/pallas_call | solution.py:101
  4.5 4.4 %collective-permute-start = (f32[50,8,128]{2,1,0:T(8,128)S(1)}, f32[50,8,128]{2,1,0:T(8,128)S(1)}, u32[]{:S(2)}, u32[]{:S(2)}) collective-permute-start(f32[50,8,128]{2,1,0:T(8,128)S(1)} %get-tuple-element.27), channel_id=1, source_target_pairs={{0,1},{1,0},{2,3},{3,2},{4,5},{5,4},{6,7},{7,6},{8,9},{9,8},{10,11... | collective-permute-start | bytes 614408 | tf_op jit(solution)/shard_map/ppermute | solution.py:889
  8.9 0.0 collective-permute-done.1.refs_1_
  8.9 1.1 %collective-permute-done.refs_0_ = f32[50,8,128]{2,1,0:T(8,128)S(1)} collective-permute-done((f32[50,8,128]{2,1,0:T(8,128)S(1)}, f32[50,8,128]{2,1,0:T(8,128)S(1)}, u32[]{:S(2)}, u32[]{:S(2)}) %collective-permute-start) | collective-permute-done | bytes 204832 | tf_op jit(solution)/shard_map/ppermute | solution.py:889
  10.0 0.1 arrange.1
  10.1 17.7 %all_to_all.10.refs_0_.refs_1_ = f32[16,5,8,128]{3,2,1,0:T(8,128)S(1)} all-to-all(f32[16,5,8,128]{3,2,1,0:T(8,128)S(1)} %get-tuple-element.30), channel_id=1, replica_groups=mesh['groups'=2,'depth'=16] {'depth'}, dimensions={0} | all-to-all | bytes 655360 | tf_op jit(solution)/shard_map/all_to_all | solution.py:900
  27.8 0.1 chain.2
  27.9 0.2 collective-permute-start.2
  28.1 0.0 copy-done.1
  28.1 0.7 %prepare.1 = (f32[2,2,4,5,8,128]{5,4,3,2,1,0:T(8,128)S(1)}, f32[2,10,8,128]{3,2,1,0:T(8,128)S(1)}, f32[2,2,5,2,8,128]{5,4,3,2,1,0:T(8,128)S(1)}) custom-call(s32[4]{0:T(128)} %refs_2_.3, f32[2,2,4,6,8,128]{5,4,3,2,1,0:T(8,128)S(1)} %get-tuple-element.34.refs_1_.refs_8_, f32[2,3,8,128]{3,2,1,0:T(8,128)S(1)} %get-tuple-element.35.refs_2_, ...), custom_call_target="tpu_custom_call" | custom-call | flops 4000000 | bytes 4194304 | tf_op jit(solution)/shard_map/prepare/pallas_call | solution.py:101
  28.8 0.4 collective-permute-done.2.refs_1_
  29.2 6.1 %middle.1 = (f32[2,4,64,8,128]{4,3,2,1,0:T(8,128)S(1)}, f32[2,4,68,8,128]{4,3,2,1,0:T(8,128)S(1)}, f32[2,2,4,8,128]{4,3,2,1,0:T(8,128)S(1)}, f32[16,4,8,128]{3,2,1,0:T(8,128)S(1)}) custom-call(f32[4,2,2,8,128]{4,3,2,1,0:T(8,128)S(1)} %get-tuple-element.32.refs_0_, f32[4,2,2,8,128]{4,3,2,1,0:T(8,128)S(1)} %collective-permute-done.2.refs_1_, s32[4]{0:T(128)} %refs_2_.3, ...), custom_call_target="tpu_custom_call" | custom-call | flops 80000000 | bytes 4194304 | tf_op jit(solution)/shard_map/middle/pallas_call | solution.py:101
  35.4 13.0 %all_to_all.11.refs_0_ = f32[16,4,8,128]{3,2,1,0:T(8,128)S(1)} all-to-all(f32[16,4,8,128]{3,2,1,0:T(8,128)S(1)} %get-tuple-element.41), channel_id=1, replica_groups=mesh['groups'=2,'depth'=16] {'depth'}, dimensions={0} | all-to-all | bytes 524288 | tf_op jit(solution)/shard_map/all_to_all | solution.py:946
  48.3 0.1 chain.3
  48.5 0.1 collective-permute-start.3
  48.6 0.3 scale.1.refs_7_
  48.8 1.0 %collective-permute-done.3.refs_1_ = f32[4,2,2,8,128]{4,3,2,1,0:T(8,128)S(1)} collective-permute-done((f32[4,2,2,8,128]{4,3,2,1,0:T(8,128)S(1)}, f32[4,2,2,8,128]{4,3,2,1,0:T(8,128)S(1)}, u32[]{:S(2)}, u32[]{:S(2)}) %collective-permute-start.3) | collective-permute-done | bytes 65568 | tf_op jit(solution)/shard_map/ppermute | solution.py:922
  49.8 4.6 %final.1 = f32[2,4,64,8,128]{4,3,2,1,0:T(8,128)} custom-call(f32[4,2,2,8,128]{4,3,2,1,0:T(8,128)S(1)} %get-tuple-element.43.refs_0_, f32[4,2,2,8,128]{4,3,2,1,0:T(8,128)S(1)} %collective-permute-done.3.refs_1_, f32[2,2,4,8,128]{4,3,2,1,0:T(8,128)S(1)} %get-tuple-element.42.refs_2_, f32[30,8,128]{2,1,0:T(8,128)S(1)} %get-tuple-element.29.refs_2_.refs_5_.refs_1_.refs_3_, ...), custom_call_target="tpu_custom_call" | custom-call | flops 60000000 | bytes 4194304 | tf_op jit(solution)/shard_map/final/pallas_call | solution.py:101
Async XLA Ops:
  0.0 1.9 %copy-start = (f32[2,4,64,8,128]{4,3,2,1,0:T(8,128)S(1)}, f32[2,4,64,8,128]{4,3,2,1,0:T(8,128)}, u32[]{:S(2)}) copy-start(f32[2,4,64,8,128]{4,3,2,1,0:T(8,128)} %refs_12_.1) | copy-start | bytes 6291460
  1.2 26.9 %copy-start.1 = (f32[2,4,8,128]{3,2,1,0:T(8,128)S(1)}, f32[2,4,8,128]{3,2,1,0:T(8,128)}, u32[]{:S(2)}) copy-start(f32[2,4,8,128]{3,2,1,0:T(8,128)} %refs_4_.5) | copy-start | bytes 98308
  1.2 7.7 %collective-permute-start.1 = (f32[50,8,128]{2,1,0:T(8,128)S(1)}, f32[50,8,128]{2,1,0:T(8,128)S(1)}, u32[]{:S(2)}, u32[]{:S(2)}) collective-permute-start(f32[50,8,128]{2,1,0:T(8,128)S(1)} %get-tuple-element.28), channel_id=1, source_target_pairs={{1,2},{3,4},{5,6},{7,8},{9,10},{11,12},{13,14},{2,1},{4,3},{6,5},{... | collective-permute-start | bytes 614408 | tf_op jit(solution)/shard_map/ppermute | solution.py:873
  4.5 5.5 %collective-permute-start = (f32[50,8,128]{2,1,0:T(8,128)S(1)}, f32[50,8,128]{2,1,0:T(8,128)S(1)}, u32[]{:S(2)}, u32[]{:S(2)}) collective-permute-start(f32[50,8,128]{2,1,0:T(8,128)S(1)} %get-tuple-element.27), channel_id=1, source_target_pairs={{0,1},{1,0},{2,3},{3,2},{4,5},{5,4},{6,7},{7,6},{8,9},{9,8},{10,11... | collective-permute-start | bytes 614408 | tf_op jit(solution)/shard_map/ppermute | solution.py:889
  27.9 1.3 %collective-permute-start.2 = (f32[4,2,2,8,128]{4,3,2,1,0:T(8,128)S(1)}, f32[4,2,2,8,128]{4,3,2,1,0:T(8,128)S(1)}, u32[]{:S(2)}, u32[]{:S(2)}) collective-permute-start(f32[4,2,2,8,128]{4,3,2,1,0:T(8,128)S(1)} %get-tuple-element.33), channel_id=1, source_target_pairs={{0,1},{1,0},{2,3},{3,2},{4,5},{5,4},{6,7},{7,6},{8,9},{9,8},{10,11... | collective-permute-start | bytes 196616 | tf_op jit(solution)/shard_map/ppermute | solution.py:922
  48.5 1.3 %collective-permute-start.3 = (f32[4,2,2,8,128]{4,3,2,1,0:T(8,128)S(1)}, f32[4,2,2,8,128]{4,3,2,1,0:T(8,128)S(1)}, u32[]{:S(2)}, u32[]{:S(2)}) collective-permute-start(f32[4,2,2,8,128]{4,3,2,1,0:T(8,128)S(1)} %get-tuple-element.44), channel_id=1, source_target_pairs={{0,1},{1,0},{2,3},{3,2},{4,5},{5,4},{6,7},{7,6},{8,9},{9,8},{10,11... | collective-permute-start | bytes 196616 | tf_op jit(solution)/shard_map/ppermute | solution.py:922

commit v9 on v8

--- a/solution.py
+++ b/solution.py
@@ -260,9 +260,9 @@
 
 
 def pack_kernel(start, send, given, made, rest):
-    kk, damp, absorb, labels, guess = given
-    out, base = made
-    _, count, slab, *tile = guess.shape
+    kk, absorb, labels, guess = given
+    (out,) = made
+    _, count, slab, *_ = guess.shape
     even = lax.rem(lax.axis_index("depth"), 2) == 0
     first = jnp.where(even, 0, slab - DEEP)
     for i in range(2 * count):
@@ -270,32 +270,18 @@
             guess.at[i // count, i % count, pl.ds(first, DEEP)],
             out.at[pl.ds(i * DEEP, DEEP)],
         )
-    row = lax.broadcasted_iota(jnp.int32, tuple(tile), 0)
-    lane = lax.broadcasted_iota(jnp.int32, tuple(tile), 1)
-    cell = row * tile[1] + lane
     kk, absorb, labels = kk.wait(), absorb.wait(), labels.wait()
-    squared = region_values(labels[0], kk)
     out[side_tiles(count)] = absorb[0]
-    out[side_tiles(count) + 1] = squared
-    base[MEDIA] = absorb[0]
-    base[MEDIA + 1] = squared
-    damp = damp.wait()
-
-    def mark(i, hit):
-        return jnp.where(cell == damp[i], 1.0, hit)
-
-    layer = loop(0, damp.shape[0], mark, jnp.zeros(tile, jnp.float32), 16)
-    set_media(base, squared, layer, absorb[0], slab)
+    out[side_tiles(count) + 1] = region_values(labels[0], kk)
 
 
 def start_kernel(start, send, given, made, rest):
-    plan, sources, base, guess = given
+    plan, damp, sources, for_odd, guess = given
     residual, pack, power, for_even = made
     emits, ref = rest
     _, count, slab, height, breadth = guess.shape
     tile = (height, breadth)
     media = media_of(pack)
-    media[...] = base[:MEDIA]
     masks = lane_masks(tile)
     field = Field(ref, -1, height)
     zero = jnp.zeros((count,) + tile, jnp.float32)
@@ -303,6 +289,17 @@
     field.put_both(-1, (zero, zero))
     field.put_both(slab, (zero, zero))
     lanes = Lanes(field, masks)
+    absorb, squared = pair(for_odd, side_tiles(count))
+    row = lax.broadcasted_iota(jnp.int32, tile, 0)
+    lane = lax.broadcasted_iota(jnp.int32, tile, 1)
+    cell = row * breadth + lane
+    damp = damp.wait()
+
+    def mark(i, hit):
+        return jnp.where(cell == damp[i], 1.0, hit)
+
+    layer = loop(0, damp.shape[0], mark, jnp.zeros(tile, jnp.float32), 16)
+    set_media(media, squared, layer, absorb, slab)
     diagonal, layer3 = media[DIAGONAL], media[LAYER]
     inverse, factor = pair(media, INVERSE), pair(media, WAVE)
 
@@ -355,7 +352,8 @@
         for_even[pl.ds(i * DEEP, DEEP)] = guess[
             i // count, i % count, pl.ds(first_plane, DEEP)
         ]
-    for_even[pl.ds(side_tiles(count), 2)] = base[MEDIA : MEDIA + 2]
+    for_even[side_tiles(count)] = absorb
+    for_even[side_tiles(count) + 1] = squared
 
 
 def add_forcing(plan, held, sources, reach, slab, inverse=None):
@@ -621,7 +619,7 @@
         self.below, self.own, self.above = below, own, above
 
 
-def pipeline(stages, slab, carry, halfway):
+def pipeline(stages, slab, carry, halfway, by_plane):
     offsets = [LAG * (len(stages) - 1 - i) for i in range(len(stages))]
     trips = (slab - offsets[0]) // UNROLL
 
@@ -646,9 +644,11 @@
         carry = own(i, 0, offsets[i], carry)
 
     def trip(t, carry):
-        for i in reversed(range(len(stages))):
-            for u in range(UNROLL):
-                carry = run(i, t * UNROLL + offsets[i] + u, carry)
+        pairs = [(i, u) for i in range(len(stages)) for u in range(UNROLL)]
+        if by_plane:
+            pairs.sort(key=lambda pair: pair[1])
+        for i, u in pairs:
+            carry = run(i, t * UNROLL + offsets[i] + u, carry)
         return carry
 
     first = trips // 2
@@ -785,7 +785,9 @@
         Stage(lambda: beyond(0, -more, 0), inside, lambda: beyond(1, slab, slab + more))
     )
     zero = jnp.zeros((count,) + tile, jnp.float32)
-    carry = pipeline(stages, slab, ((zero, zero), (zero, zero)), lambda i, reached: None)
+    carry = pipeline(
+        stages, slab, ((zero, zero), (zero, zero)), lambda i, reached: None, True
+    )
     for way in range(2):
         for part in range(2):
             next_full[way, part] = carry[way][part]
@@ -845,7 +847,7 @@
         send(held.at[:, :, part], out.at[:, :, part])
         sent[0] = top
 
-    pipeline(stages, slab, 0, lambda i, reached: send_field(reached[2]))
+    pipeline(stages, slab, 0, lambda i, reached: send_field(reached[2]), False)
     send_field(slab)
 
 
@@ -858,13 +860,12 @@
     scratch = lambda shape: pltpu.VMEM(shape, jnp.float32)
 
     tiles = (side_tiles(count) + 2,) + tile
-    for_odd, base = kernel_call(
+    (for_odd,) = kernel_call(
         pack_kernel,
         [
-            (region_kk, "smem"), (damp_cells, "smem"), (absorb, "vmem"),
-            (labels, "vmem"), (guess, "hbm"),
-        ],
-        [(tiles, "direct"), ((MEDIA + 2,) + tile, "direct")],
+            (region_kk, "smem"), (absorb, "vmem"), (labels, "vmem"), (guess, "hbm"),
+        ],
+        [(tiles, "direct")],
         pieces=2 * count, cost=1_000_000, name="pack", limit=4,
     )
     even_pairs = [(i, i ^ 1) for i in range(size)]
@@ -875,7 +876,8 @@
     residual, pack, power, for_even = kernel_call(
         start_kernel,
         [
-            (plan, "smem"), (sources, "vmem"), (base, "direct"), (guess, "direct"),
+            (plan, "smem"), (damp_cells, "smem"), (sources, "vmem"),
+            (for_odd, "direct"), (guess, "direct"),
         ],
         [
             (planes(slab), "direct"), ((MEDIA + 4 + 4 * count,) + tile, "direct"),

time: 54.6 us -> 54.8 us (level)
  blocking collectives: 30.7 us -> 29.9 us
  Pallas kernels: 15.9 us -> 16.7 us
    pallas_call x9, Pallas kernels: 15.9 us -> 16.7 us  [kernel_call(): pl.pallas_call(kernel, out_shape=tuple((jax.ShapeDtypeStruct(s, jnp.float...]
    all_to_all x1, blocking collectives: 17.7 us -> 16.9 us  [local(): first_got = lax.all_to_all(slots, 'depth', 0, 0)]
  transfers between devices with their start and end apart: 4 -> 4, of which waited for: 3 -> 3; matrix products, arithmetic and copies ran while one was open for 0% -> 0% of each run, Pallas kernels for 7% -> 8%
where the time goes in v9:
time: 54.8 us; the launch traced here: 54.5 us
  blocking collectives  29.9 us (55%)
  Pallas kernels  16.7 us (30%)
  starting transfers between devices  5.3 us (10%)
  waiting for transfers between devices  2.43 us (4%)
    all_to_all x1, blocking collectives, local(): first_got = lax.all_to_all(slots, 'depth', 0, 0)  16.9 us
    pallas_call x9, Pallas kernels, kernel_call(): pl.pallas_call(kernel, out_shape=tuple((jax.ShapeDtypeStruct(s, jnp.float...  16.7 us
    all_to_all x1, blocking collectives, local(): mine, theirs = chain(lax.all_to_all(slots, 'depth', 0, 0), next_full)  13 us
    ppermute x1, starting transfers between devices, local(): got_even = lax.ppermute(for_even, 'depth', even_pairs)  4.38 us
    ppermute x2, waiting for transfers between devices, chain(): return (mine, lax.ppermute(theirs, 'depth', even_pairs))  1.35 us
  transfers between devices with their start and end apart: 4, of which 3 were waited for; matrix products, arithmetic and copies ran while one was open for 0% of the time, Pallas kernels for 8%

profile of v9, /device:TPU:0, one launch (start us, length us, event | category | flops | bytes accessed | tf_op | source)
XLA Modules:
  0.0 54.5 jit_solution(1502743090451664661)
XLA Ops:
  0.0 0.0 copy-start
  0.0 1.1 %pack.1.refs_3_ = f32[50,8,128]{2,1,0:T(8,128)S(1)} custom-call(f32[8]{0:T(128)} %refs_0_.3, f32[1,8,128]{2,1,0:T(8,128)} %refs_1_.2, s32[1,8,128]{2,1,0:T(8,128)} %refs_2_.3, f32[2,4,64,8,128]{4,3,2,1,0:T(8,128)} %refs_12_.1), custom_call_target="tpu_custom_call" | custom-call | flops 1000000 | bytes 4194304 | tf_op jit(solution)/shard_map/pack/pallas_call | solution.py:101
  1.1 0.0 copy-start.1
  1.1 0.7 %collective-permute-start.1 = (f32[50,8,128]{2,1,0:T(8,128)S(1)}, f32[50,8,128]{2,1,0:T(8,128)S(1)}, u32[]{:S(2)}, u32[]{:S(2)}) collective-permute-start(f32[50,8,128]{2,1,0:T(8,128)S(1)} %pack.1.refs_3_), channel_id=1, source_target_pairs={{1,2},{3,4},{5,6},{7,8},{9,10},{11,12},{13,14},{2,1},{4,3},{6,5},{... | collective-permute-start | bytes 614408 | tf_op jit(solution)/shard_map/ppermute | solution.py:874
  1.8 0.0 copy-done
  1.8 3.4 %start.1 = (f32[2,4,64,8,128]{4,3,2,1,0:T(8,128)S(1)}, f32[30,8,128]{2,1,0:T(8,128)S(1)}, f32[65,2,8,128]{3,2,1,0:T(8,128)S(1)}, f32[50,8,128]{2,1,0:T(8,128)S(1)}) custom-call(s32[4]{0:T(128)} %refs_2_.5, s32[128]{0:T(128)} %refs_1_.3, f32[2,4,8,128]{3,2,1,0:T(8,128)} %refs_4_.5, f32[50,8,128]{2,1,0:T(8,128)S(1)} %pack.1.refs_3_, ...), custom_call_target="tpu_custom_call" | custom-call | flops 20000000 | bytes 4194304 | tf_op jit(solution)/shard_map/start/pallas_call | solution.py:101
  5.3 4.4 %collective-permute-start = (f32[50,8,128]{2,1,0:T(8,128)S(1)}, f32[50,8,128]{2,1,0:T(8,128)S(1)}, u32[]{:S(2)}, u32[]{:S(2)}) collective-permute-start(f32[50,8,128]{2,1,0:T(8,128)S(1)} %get-tuple-element.24), channel_id=1, source_target_pairs={{0,1},{1,0},{2,3},{3,2},{4,5},{5,4},{6,7},{7,6},{8,9},{9,8},{10,11... | collective-permute-start | bytes 614408 | tf_op jit(solution)/shard_map/ppermute | solution.py:891
  9.6 0.0 collective-permute-done.1.refs_1_
  9.6 1.1 %collective-permute-done.refs_0_ = f32[50,8,128]{2,1,0:T(8,128)S(1)} collective-permute-done((f32[50,8,128]{2,1,0:T(8,128)S(1)}, f32[50,8,128]{2,1,0:T(8,128)S(1)}, u32[]{:S(2)}, u32[]{:S(2)}) %collective-permute-start) | collective-permute-done | bytes 204832 | tf_op jit(solution)/shard_map/ppermute | solution.py:891
  10.7 0.1 arrange.1
  10.8 16.9 %all_to_all.10.refs_0_.refs_1_ = f32[16,5,8,128]{3,2,1,0:T(8,128)S(1)} all-to-all(f32[16,5,8,128]{3,2,1,0:T(8,128)S(1)} %get-tuple-element.26), channel_id=1, replica_groups=mesh['groups'=2,'depth'=16] {'depth'}, dimensions={0} | all-to-all | bytes 655360 | tf_op jit(solution)/shard_map/all_to_all | solution.py:902
  27.7 0.1 chain.2
  27.9 0.2 collective-permute-start.2
  28.1 0.0 copy-done.1
  28.1 0.7 %prepare.1 = (f32[2,2,4,5,8,128]{5,4,3,2,1,0:T(8,128)S(1)}, f32[2,10,8,128]{3,2,1,0:T(8,128)S(1)}, f32[2,2,5,2,8,128]{5,4,3,2,1,0:T(8,128)S(1)}) custom-call(s32[4]{0:T(128)} %refs_2_.5, f32[2,2,4,6,8,128]{5,4,3,2,1,0:T(8,128)S(1)} %get-tuple-element.30.refs_1_.refs_8_, f32[2,3,8,128]{3,2,1,0:T(8,128)S(1)} %get-tuple-element.31.refs_2_, ...), custom_call_target="tpu_custom_call" | custom-call | flops 4000000 | bytes 4194304 | tf_op jit(solution)/shard_map/prepare/pallas_call | solution.py:101
  28.8 0.4 collective-permute-done.2.refs_1_
  29.2 6.1 %middle.1 = (f32[2,4,64,8,128]{4,3,2,1,0:T(8,128)S(1)}, f32[2,4,68,8,128]{4,3,2,1,0:T(8,128)S(1)}, f32[2,2,4,8,128]{4,3,2,1,0:T(8,128)S(1)}, f32[16,4,8,128]{3,2,1,0:T(8,128)S(1)}) custom-call(f32[4,2,2,8,128]{4,3,2,1,0:T(8,128)S(1)} %get-tuple-element.28.refs_0_, f32[4,2,2,8,128]{4,3,2,1,0:T(8,128)S(1)} %collective-permute-done.2.refs_1_, s32[4]{0:T(128)} %refs_2_.5, ...), custom_call_target="tpu_custom_call" | custom-call | flops 80000000 | bytes 4194304 | tf_op jit(solution)/shard_map/middle/pallas_call | solution.py:101
  35.3 13.0 %all_to_all.11.refs_0_ = f32[16,4,8,128]{3,2,1,0:T(8,128)S(1)} all-to-all(f32[16,4,8,128]{3,2,1,0:T(8,128)S(1)} %get-tuple-element.37), channel_id=1, replica_groups=mesh['groups'=2,'depth'=16] {'depth'}, dimensions={0} | all-to-all | bytes 524288 | tf_op jit(solution)/shard_map/all_to_all | solution.py:948
  48.3 0.1 chain.3
  48.5 0.1 collective-permute-start.3
  48.5 0.3 scale.1.refs_7_
  48.8 1.0 %collective-permute-done.3.refs_1_ = f32[4,2,2,8,128]{4,3,2,1,0:T(8,128)S(1)} collective-permute-done((f32[4,2,2,8,128]{4,3,2,1,0:T(8,128)S(1)}, f32[4,2,2,8,128]{4,3,2,1,0:T(8,128)S(1)}, u32[]{:S(2)}, u32[]{:S(2)}) %collective-permute-start.3) | collective-permute-done | bytes 65568 | tf_op jit(solution)/shard_map/ppermute | solution.py:924
  49.8 4.7 %final.1 = f32[2,4,64,8,128]{4,3,2,1,0:T(8,128)} custom-call(f32[4,2,2,8,128]{4,3,2,1,0:T(8,128)S(1)} %get-tuple-element.39.refs_0_, f32[4,2,2,8,128]{4,3,2,1,0:T(8,128)S(1)} %collective-permute-done.3.refs_1_, f32[2,2,4,8,128]{4,3,2,1,0:T(8,128)S(1)} %get-tuple-element.38.refs_2_, f32[30,8,128]{2,1,0:T(8,128)S(1)} %get-tuple-element.25.refs_2_.refs_5_.refs_1_.refs_3_, ...), custom_call_target="tpu_custom_call" | custom-call | flops 60000000 | bytes 4194304 | tf_op jit(solution)/shard_map/final/pallas_call | solution.py:101
Async XLA Ops:
  0.0 1.8 %copy-start = (f32[2,4,64,8,128]{4,3,2,1,0:T(8,128)S(1)}, f32[2,4,64,8,128]{4,3,2,1,0:T(8,128)}, u32[]{:S(2)}) copy-start(f32[2,4,64,8,128]{4,3,2,1,0:T(8,128)} %refs_12_.1) | copy-start | bytes 6291460
  1.1 26.9 %copy-start.1 = (f32[2,4,8,128]{3,2,1,0:T(8,128)S(1)}, f32[2,4,8,128]{3,2,1,0:T(8,128)}, u32[]{:S(2)}) copy-start(f32[2,4,8,128]{3,2,1,0:T(8,128)} %refs_4_.5) | copy-start | bytes 98308
  1.1 8.5 %collective-permute-start.1 = (f32[50,8,128]{2,1,0:T(8,128)S(1)}, f32[50,8,128]{2,1,0:T(8,128)S(1)}, u32[]{:S(2)}, u32[]{:S(2)}) collective-permute-start(f32[50,8,128]{2,1,0:T(8,128)S(1)} %pack.1.refs_3_), channel_id=1, source_target_pairs={{1,2},{3,4},{5,6},{7,8},{9,10},{11,12},{13,14},{2,1},{4,3},{6,5},{... | collective-permute-start | bytes 614408 | tf_op jit(solution)/shard_map/ppermute | solution.py:874
  5.3 5.5 %collective-permute-start = (f32[50,8,128]{2,1,0:T(8,128)S(1)}, f32[50,8,128]{2,1,0:T(8,128)S(1)}, u32[]{:S(2)}, u32[]{:S(2)}) collective-permute-start(f32[50,8,128]{2,1,0:T(8,128)S(1)} %get-tuple-element.24), channel_id=1, source_target_pairs={{0,1},{1,0},{2,3},{3,2},{4,5},{5,4},{6,7},{7,6},{8,9},{9,8},{10,11... | collective-permute-start | bytes 614408 | tf_op jit(solution)/shard_map/ppermute | solution.py:891
  27.9 1.3 %collective-permute-start.2 = (f32[4,2,2,8,128]{4,3,2,1,0:T(8,128)S(1)}, f32[4,2,2,8,128]{4,3,2,1,0:T(8,128)S(1)}, u32[]{:S(2)}, u32[]{:S(2)}) collective-permute-start(f32[4,2,2,8,128]{4,3,2,1,0:T(8,128)S(1)} %get-tuple-element.29), channel_id=1, source_target_pairs={{0,1},{1,0},{2,3},{3,2},{4,5},{5,4},{6,7},{7,6},{8,9},{9,8},{10,11... | collective-permute-start | bytes 196616 | tf_op jit(solution)/shard_map/ppermute | solution.py:924
  48.5 1.3 %collective-permute-start.3 = (f32[4,2,2,8,128]{4,3,2,1,0:T(8,128)S(1)}, f32[4,2,2,8,128]{4,3,2,1,0:T(8,128)S(1)}, u32[]{:S(2)}, u32[]{:S(2)}) collective-permute-start(f32[4,2,2,8,128]{4,3,2,1,0:T(8,128)S(1)} %get-tuple-element.40), channel_id=1, source_target_pairs={{0,1},{1,0},{2,3},{3,2},{4,5},{5,4},{6,7},{7,6},{8,9},{9,8},{10,11... | collective-permute-start | bytes 196616 | tf_op jit(solution)/shard_map/ppermute | solution.py:924

commit v10 on v8

--- a/solution.py
+++ b/solution.py
@@ -200,6 +200,12 @@
 INVERSE, DIAGONAL, LAYER, WAVE, SECOND, THIRD, MEDIA = 0, 2, 3, 4, 6, 8, 10
 
 
+def wave(absorb, squared, order, slab):
+    decay = jnp.exp(-order * absorb / slab)
+    angle = order * jnp.sqrt(squared)
+    return decay * jnp.cos(angle), decay * jnp.sin(angle)
+
+
 def set_media(ref, squared, layer, absorb, slab, inside=None):
     diagonal = 6.0 - squared
     imag = shift_ratio * squared + damping * layer
@@ -208,9 +214,7 @@
     if inside is not None:
         inverse = tuple(jnp.where(inside, v, 0.0) for v in inverse)
     grow = 1.0 + keep
-    decay = jnp.exp(-absorb / slab)
-    angle = jnp.sqrt(squared)
-    factor = decay * jnp.cos(angle), decay * jnp.sin(angle)
+    factor = wave(absorb, squared, 1, slab)
     values = (
         *inverse, diagonal, damping * layer, *factor,
         *scale(1.0 / grow, inverse), *scale(grow, inverse),
@@ -338,8 +342,8 @@
             fill(k + 1)
         carry = plane(k, carry)
     plan, sources = plan.wait(), sources.wait()
-    toward_next, toward_prev, w = carry
-    power[slab, 0], power[slab, 1] = w
+    toward_next, toward_prev, _ = carry
+    power[slab, 0], power[slab, 1] = wave(*pair(base, MEDIA), slab, slab)
     add_forcing(plan, residual, sources, 0, slab, inverse)
     for part in range(2):
         emits[0, part] = toward_next[part]
@@ -621,7 +625,7 @@
         self.below, self.own, self.above = below, own, above
 
 
-def pipeline(stages, slab, carry, halfway):
+def pipeline(stages, slab, carry, halfway, by_plane):
     offsets = [LAG * (len(stages) - 1 - i) for i in range(len(stages))]
     trips = (slab - offsets[0]) // UNROLL
 
@@ -646,9 +650,11 @@
         carry = own(i, 0, offsets[i], carry)
 
     def trip(t, carry):
-        for i in reversed(range(len(stages))):
-            for u in range(UNROLL):
-                carry = run(i, t * UNROLL + offsets[i] + u, carry)
+        pairs = [(i, u) for i in range(len(stages)) for u in range(UNROLL)]
+        if by_plane:
+            pairs.sort(key=lambda pair: pair[1])
+        for i, u in pairs:
+            carry = run(i, t * UNROLL + offsets[i] + u, carry)
         return carry
 
     first = trips // 2
@@ -785,7 +791,9 @@
         Stage(lambda: beyond(0, -more, 0), inside, lambda: beyond(1, slab, slab + more))
     )
     zero = jnp.zeros((count,) + tile, jnp.float32)
-    carry = pipeline(stages, slab, ((zero, zero), (zero, zero)), lambda i, reached: None)
+    carry = pipeline(
+        stages, slab, ((zero, zero), (zero, zero)), lambda i, reached: None, True
+    )
     for way in range(2):
         for part in range(2):
             next_full[way, part] = carry[way][part]
@@ -845,7 +853,7 @@
         send(held.at[:, :, part], out.at[:, :, part])
         sent[0] = top
 
-    pipeline(stages, slab, 0, lambda i, reached: send_field(reached[2]))
+    pipeline(stages, slab, 0, lambda i, reached: send_field(reached[2]), False)
     send_field(slab)
 
 

time: 54.6 us -> 54.7 us (level)
  no operation moved by 1% of the time
where the time goes in v10:
time: 54.7 us; the launch traced here: 54.5 us
  blocking collectives  30.6 us (56%)
  Pallas kernels  16 us (29%)
  starting transfers between devices  5.3 us (10%)
  waiting for transfers between devices  2.43 us (4%)
    all_to_all x1, blocking collectives, local(): first_got = lax.all_to_all(slots, 'depth', 0, 0)  17.7 us
    pallas_call x9, Pallas kernels, kernel_call(): pl.pallas_call(kernel, out_shape=tuple((jax.ShapeDtypeStruct(s, jnp.float...  16 us
    all_to_all x1, blocking collectives, local(): mine, theirs = chain(lax.all_to_all(slots, 'depth', 0, 0), next_full)  13 us
    ppermute x1, starting transfers between devices, local(): got_even = lax.ppermute(for_even, 'depth', even_pairs)  4.38 us
    ppermute x2, waiting for transfers between devices, chain(): return (mine, lax.ppermute(theirs, 'depth', even_pairs))  1.35 us
  transfers between devices with their start and end apart: 4, of which 3 were waited for; matrix products, arithmetic and copies ran while one was open for 0% of the time, Pallas kernels for 7%

profile of v10, /device:TPU:0, one launch (start us, length us, event | category | flops | bytes accessed | tf_op | source)
XLA Modules:
  0.0 54.5 jit_solution(16612295036874997034)
XLA Ops:
  0.0 0.0 copy-start
  0.0 1.1 %pack.1 = (f32[50,8,128]{2,1,0:T(8,128)S(1)}, f32[12,8,128]{2,1,0:T(8,128)S(1)}) custom-call(f32[8]{0:T(128)} %refs_0_.3, s32[128]{0:T(128)} %refs_1_.2, f32[1,8,128]{2,1,0:T(8,128)} %refs_2_.2, s32[1,8,128]{2,1,0:T(8,128)} %refs_3_.3, f32[2,4,64,8,128]{4,3,2,1,0:T(8,128)} %refs_12_.1), custom_call_target="tpu_custom_call" | custom-call | flops 1000000 | bytes 4194304 | tf_op jit(solution)/shard_map/pack/pallas_call | solution.py:101
  1.2 0.0 copy-start.1
  1.2 0.7 %collective-permute-start.1 = (f32[50,8,128]{2,1,0:T(8,128)S(1)}, f32[50,8,128]{2,1,0:T(8,128)S(1)}, u32[]{:S(2)}, u32[]{:S(2)}) collective-permute-start(f32[50,8,128]{2,1,0:T(8,128)S(1)} %get-tuple-element.28), channel_id=1, source_target_pairs={{1,2},{3,4},{5,6},{7,8},{9,10},{11,12},{13,14},{2,1},{4,3},{6,5},{... | collective-permute-start | bytes 614408 | tf_op jit(solution)/shard_map/ppermute | solution.py:881
  1.9 0.0 copy-done
  1.9 2.7 %start.1 = (f32[2,4,64,8,128]{4,3,2,1,0:T(8,128)S(1)}, f32[30,8,128]{2,1,0:T(8,128)S(1)}, f32[65,2,8,128]{3,2,1,0:T(8,128)S(1)}, f32[50,8,128]{2,1,0:T(8,128)S(1)}) custom-call(s32[4]{0:T(128)} %refs_2_.3, f32[2,4,8,128]{3,2,1,0:T(8,128)} %refs_4_.5, f32[12,8,128]{2,1,0:T(8,128)S(1)} %get-tuple-element.26.refs_2_, f32[2,4,64,8,128]{4,3,2,1,0:T(8,128)S(1)} %copy-done), custom_call_target="tpu_custom_call" | custom-call | flops 20000000 | bytes 4194304 | tf_op jit(solution)/shard_map/start/pallas_call | solution.py:101
  4.6 4.4 %collective-permute-start = (f32[50,8,128]{2,1,0:T(8,128)S(1)}, f32[50,8,128]{2,1,0:T(8,128)S(1)}, u32[]{:S(2)}, u32[]{:S(2)}) collective-permute-start(f32[50,8,128]{2,1,0:T(8,128)S(1)} %get-tuple-element.27), channel_id=1, source_target_pairs={{0,1},{1,0},{2,3},{3,2},{4,5},{5,4},{6,7},{7,6},{8,9},{9,8},{10,11... | collective-permute-start | bytes 614408 | tf_op jit(solution)/shard_map/ppermute | solution.py:897
  8.9 0.0 collective-permute-done.1.refs_1_
  8.9 1.1 %collective-permute-done.refs_0_ = f32[50,8,128]{2,1,0:T(8,128)S(1)} collective-permute-done((f32[50,8,128]{2,1,0:T(8,128)S(1)}, f32[50,8,128]{2,1,0:T(8,128)S(1)}, u32[]{:S(2)}, u32[]{:S(2)}) %collective-permute-start) | collective-permute-done | bytes 204832 | tf_op jit(solution)/shard_map/ppermute | solution.py:897
  10.0 0.1 arrange.1
  10.1 17.7 %all_to_all.10.refs_0_.refs_1_ = f32[16,5,8,128]{3,2,1,0:T(8,128)S(1)} all-to-all(f32[16,5,8,128]{3,2,1,0:T(8,128)S(1)} %get-tuple-element.30), channel_id=1, replica_groups=mesh['groups'=2,'depth'=16] {'depth'}, dimensions={0} | all-to-all | bytes 655360 | tf_op jit(solution)/shard_map/all_to_all | solution.py:908
  27.8 0.1 chain.2
  27.9 0.2 collective-permute-start.2
  28.1 0.0 copy-done.1
  28.1 0.7 %prepare.1 = (f32[2,2,4,5,8,128]{5,4,3,2,1,0:T(8,128)S(1)}, f32[2,10,8,128]{3,2,1,0:T(8,128)S(1)}, f32[2,2,5,2,8,128]{5,4,3,2,1,0:T(8,128)S(1)}) custom-call(s32[4]{0:T(128)} %refs_2_.3, f32[2,2,4,6,8,128]{5,4,3,2,1,0:T(8,128)S(1)} %get-tuple-element.34.refs_1_.refs_8_, f32[2,3,8,128]{3,2,1,0:T(8,128)S(1)} %get-tuple-element.35.refs_2_, ...), custom_call_target="tpu_custom_call" | custom-call | flops 4000000 | bytes 4194304 | tf_op jit(solution)/shard_map/prepare/pallas_call | solution.py:101
  28.8 0.4 collective-permute-done.2.refs_1_
  29.2 6.1 %middle.1 = (f32[2,4,64,8,128]{4,3,2,1,0:T(8,128)S(1)}, f32[2,4,68,8,128]{4,3,2,1,0:T(8,128)S(1)}, f32[2,2,4,8,128]{4,3,2,1,0:T(8,128)S(1)}, f32[16,4,8,128]{3,2,1,0:T(8,128)S(1)}) custom-call(f32[4,2,2,8,128]{4,3,2,1,0:T(8,128)S(1)} %get-tuple-element.32.refs_0_, f32[4,2,2,8,128]{4,3,2,1,0:T(8,128)S(1)} %collective-permute-done.2.refs_1_, s32[4]{0:T(128)} %refs_2_.3, ...), custom_call_target="tpu_custom_call" | custom-call | flops 80000000 | bytes 4194304 | tf_op jit(solution)/shard_map/middle/pallas_call | solution.py:101
  35.4 13.0 %all_to_all.11.refs_0_ = f32[16,4,8,128]{3,2,1,0:T(8,128)S(1)} all-to-all(f32[16,4,8,128]{3,2,1,0:T(8,128)S(1)} %get-tuple-element.41), channel_id=1, replica_groups=mesh['groups'=2,'depth'=16] {'depth'}, dimensions={0} | all-to-all | bytes 524288 | tf_op jit(solution)/shard_map/all_to_all | solution.py:954
  48.3 0.1 chain.3
  48.5 0.1 collective-permute-start.3
  48.6 0.3 scale.1.refs_7_
  48.9 1.0 %collective-permute-done.3.refs_1_ = f32[4,2,2,8,128]{4,3,2,1,0:T(8,128)S(1)} collective-permute-done((f32[4,2,2,8,128]{4,3,2,1,0:T(8,128)S(1)}, f32[4,2,2,8,128]{4,3,2,1,0:T(8,128)S(1)}, u32[]{:S(2)}, u32[]{:S(2)}) %collective-permute-start.3) | collective-permute-done | bytes 65568 | tf_op jit(solution)/shard_map/ppermute | solution.py:930
  49.8 4.7 %final.1 = f32[2,4,64,8,128]{4,3,2,1,0:T(8,128)} custom-call(f32[4,2,2,8,128]{4,3,2,1,0:T(8,128)S(1)} %get-tuple-element.43.refs_0_, f32[4,2,2,8,128]{4,3,2,1,0:T(8,128)S(1)} %collective-permute-done.3.refs_1_, f32[2,2,4,8,128]{4,3,2,1,0:T(8,128)S(1)} %get-tuple-element.42.refs_2_, f32[30,8,128]{2,1,0:T(8,128)S(1)} %get-tuple-element.29.refs_2_.refs_5_.refs_1_.refs_3_, ...), custom_call_target="tpu_custom_call" | custom-call | flops 60000000 | bytes 4194304 | tf_op jit(solution)/shard_map/final/pallas_call | solution.py:101
Async XLA Ops:
  0.0 1.9 %copy-start = (f32[2,4,64,8,128]{4,3,2,1,0:T(8,128)S(1)}, f32[2,4,64,8,128]{4,3,2,1,0:T(8,128)}, u32[]{:S(2)}) copy-start(f32[2,4,64,8,128]{4,3,2,1,0:T(8,128)} %refs_12_.1) | copy-start | bytes 6291460
  1.2 26.9 %copy-start.1 = (f32[2,4,8,128]{3,2,1,0:T(8,128)S(1)}, f32[2,4,8,128]{3,2,1,0:T(8,128)}, u32[]{:S(2)}) copy-start(f32[2,4,8,128]{3,2,1,0:T(8,128)} %refs_4_.5) | copy-start | bytes 98308
  1.2 7.8 %collective-permute-start.1 = (f32[50,8,128]{2,1,0:T(8,128)S(1)}, f32[50,8,128]{2,1,0:T(8,128)S(1)}, u32[]{:S(2)}, u32[]{:S(2)}) collective-permute-start(f32[50,8,128]{2,1,0:T(8,128)S(1)} %get-tuple-element.28), channel_id=1, source_target_pairs={{1,2},{3,4},{5,6},{7,8},{9,10},{11,12},{13,14},{2,1},{4,3},{6,5},{... | collective-permute-start | bytes 614408 | tf_op jit(solution)/shard_map/ppermute | solution.py:881
  4.6 5.5 %collective-permute-start = (f32[50,8,128]{2,1,0:T(8,128)S(1)}, f32[50,8,128]{2,1,0:T(8,128)S(1)}, u32[]{:S(2)}, u32[]{:S(2)}) collective-permute-start(f32[50,8,128]{2,1,0:T(8,128)S(1)} %get-tuple-element.27), channel_id=1, source_target_pairs={{0,1},{1,0},{2,3},{3,2},{4,5},{5,4},{6,7},{7,6},{8,9},{9,8},{10,11... | collective-permute-start | bytes 614408 | tf_op jit(solution)/shard_map/ppermute | solution.py:897
  27.9 1.3 %collective-permute-start.2 = (f32[4,2,2,8,128]{4,3,2,1,0:T(8,128)S(1)}, f32[4,2,2,8,128]{4,3,2,1,0:T(8,128)S(1)}, u32[]{:S(2)}, u32[]{:S(2)}) collective-permute-start(f32[4,2,2,8,128]{4,3,2,1,0:T(8,128)S(1)} %get-tuple-element.33), channel_id=1, source_target_pairs={{0,1},{1,0},{2,3},{3,2},{4,5},{5,4},{6,7},{7,6},{8,9},{9,8},{10,11... | collective-permute-start | bytes 196616 | tf_op jit(solution)/shard_map/ppermute | solution.py:930
  48.5 1.3 %collective-permute-start.3 = (f32[4,2,2,8,128]{4,3,2,1,0:T(8,128)S(1)}, f32[4,2,2,8,128]{4,3,2,1,0:T(8,128)S(1)}, u32[]{:S(2)}, u32[]{:S(2)}) collective-permute-start(f32[4,2,2,8,128]{4,3,2,1,0:T(8,128)S(1)} %get-tuple-element.44), channel_id=1, source_target_pairs={{0,1},{1,0},{2,3},{3,2},{4,5},{5,4},{6,7},{7,6},{8,9},{9,8},{10,11... | collective-permute-start | bytes 196616 | tf_op jit(solution)/shard_map/ppermute | solution.py:930

commit v11 on v8

--- a/solution.py
+++ b/solution.py
@@ -200,6 +200,12 @@
 INVERSE, DIAGONAL, LAYER, WAVE, SECOND, THIRD, MEDIA = 0, 2, 3, 4, 6, 8, 10
 
 
+def wave(absorb, squared, order, slab):
+    decay = jnp.exp(-order * absorb / slab)
+    angle = order * jnp.sqrt(squared)
+    return decay * jnp.cos(angle), decay * jnp.sin(angle)
+
+
 def set_media(ref, squared, layer, absorb, slab, inside=None):
     diagonal = 6.0 - squared
     imag = shift_ratio * squared + damping * layer
@@ -208,9 +214,7 @@
     if inside is not None:
         inverse = tuple(jnp.where(inside, v, 0.0) for v in inverse)
     grow = 1.0 + keep
-    decay = jnp.exp(-absorb / slab)
-    angle = jnp.sqrt(squared)
-    factor = decay * jnp.cos(angle), decay * jnp.sin(angle)
+    factor = wave(absorb, squared, 1, slab)
     values = (
         *inverse, diagonal, damping * layer, *factor,
         *scale(1.0 / grow, inverse), *scale(grow, inverse),
@@ -338,8 +342,8 @@
             fill(k + 1)
         carry = plane(k, carry)
     plan, sources = plan.wait(), sources.wait()
-    toward_next, toward_prev, w = carry
-    power[slab, 0], power[slab, 1] = w
+    toward_next, toward_prev, _ = carry
+    power[slab, 0], power[slab, 1] = wave(*pair(base, MEDIA), slab, slab)
     add_forcing(plan, residual, sources, 0, slab, inverse)
     for part in range(2):
         emits[0, part] = toward_next[part]
@@ -719,14 +723,13 @@
         near_residual, power, residual, guess,
     ) = given
     media = media_of(pack)
-    new_field, new_residual, next_full, slots = made
+    new_field, new_near, new_residual, next_full, slots = made
     incoming, *refs = rest
     _, count, slab, height, breadth = guess.shape
     tile = (height, breadth)
     masks = lane_masks(tile)
     reach = DEEP - 1
     ext = reach - 2
-    more = ext - 1
     new = Field(refs[2], -ext, height)
     new.clear()
     set_incoming(
@@ -753,6 +756,7 @@
             else:
                 i = p + DEEP if which == 0 else p - slab
                 value = near[which // 2, part, :, i] + u[part]
+                new_near[which // 2, part, :, p + ext if which == 0 else i] = value
             new.put(part, p, value)
 
     stages = update_stages(
@@ -767,12 +771,8 @@
     def residual_at(p, diagonal):
         r = new.minus_a(p, diagonal, layer3, lanes.now)
         for part in range(2):
-            new_residual[part, :, p + more] = r[part]
+            new_residual[part, :, p] = r[part]
         return r
-
-    def beyond(side, a, b):
-        for p in range(a, b):
-            residual_at(p, near_media[side, DIAGONAL])
 
     def inside(p, carry):
         toward_next, toward_prev = carry
@@ -781,9 +781,8 @@
         toward_prev = add(toward_prev, cmul(tile_of(power, p), r))
         return toward_next, toward_prev
 
-    stages.append(
-        Stage(lambda: beyond(0, -more, 0), inside, lambda: beyond(1, slab, slab + more))
-    )
+    nothing = lambda: None
+    stages.append(Stage(nothing, inside, nothing))
     zero = jnp.zeros((count,) + tile, jnp.float32)
     carry = pipeline(stages, slab, ((zero, zero), (zero, zero)), lambda i, reached: None)
     for way in range(2):
@@ -792,24 +791,52 @@
     plan = plan.wait()
     force_emits(plan, next_full, sources, power, slab)
     fill_send(slots, next_full, None)
-    add_forcing(plan, new_residual, sources, more, slab)
+    add_forcing(plan, new_residual, sources, 0, slab)
 
 
 def scale_kernel(start, send, given, made, rest):
-    residual, pack, near_media = given
+    plan, residual, field, new_near, pack, near_media, sources = given
     (out,) = made
-    planes = residual.shape[2]
+    (ref,) = rest
+    _, count, slab, height, breadth = residual.shape
     reach = DEEP - 4
-
-    def one(p, m):
-        value = cmul(pair(m, INVERSE), (residual[0, :, p], residual[1, :, p]))
-        out[0, :, p], out[1, :, p] = value
-
+    ext = reach + 1
+    masks = lane_masks((height, breadth))
     media = media_of(pack)
-    for p in range(reach):
-        one(p, near_media.at[0])
-        one(planes - 1 - p, near_media.at[1])
-    loop(reach, planes - reach, lambda p, c: one(p, media) or c, 0, 8)
+
+    def put(p, m, r):
+        out[0, :, p + reach], out[1, :, p + reach] = cmul(pair(m, INVERSE), r)
+
+    loop(
+        0, slab, lambda p, c: put(p, media, (residual[0, :, p], residual[1, :, p])) or c, 0, 8
+    )
+    for side in range(2):
+        beside = Field(ref, 0, height)
+        beside.clear()
+        for i in range(ext + 1):
+            for part in range(2):
+                if side == 0:
+                    value = new_near[0, part, :, i] if i < ext else field[part, :, 0]
+                else:
+                    value = new_near[1, part, :, i - 1] if i else field[part, :, slab - 1]
+                beside.put(part, i, value)
+        m = near_media.at[side]
+        lanes = Lanes(beside, masks)
+        for i in range(1, ext):
+            p = i - ext if side == 0 else slab + i - 1
+            put(p, m, beside.minus_a(i, m[DIAGONAL], media[LAYER], lanes.now))
+    plan = plan.wait()
+    first_plane = lax.axis_index("depth") * slab
+    for s in range(count):
+        k = plan[s] - first_plane
+        for side, low in ((0, -reach), (1, slab)):
+
+            @pl.when((k >= low) & (k < low + reach))
+            def _():
+                src = sources[0, s], sources[1, s]
+                src = cmul(pair(near_media.at[side], INVERSE), src)
+                for part in range(2):
+                    out[part, s, k + reach] += src[part]
 
 
 def final_kernel(start, send, given, made, rest):
@@ -922,7 +949,7 @@
         return mine, lax.ppermute(theirs, "depth", even_pairs)
 
     mine, theirs = chain(first_got, full)
-    new_field, new_residual, next_full, slots = kernel_call(
+    new_field, new_near, new_residual, next_full, slots = kernel_call(
         middle_kernel,
         [
             (mine, "direct"), (theirs, "direct"),
@@ -932,7 +959,8 @@
             (residual, "direct"), (guess, "direct"),
         ],
         [
-            (planes(slab), "direct"), (planes(slab + 2 * (DEEP - 4)), "direct"),
+            (planes(slab), "direct"), ((2, 2, count, DEEP - 3) + tile, "direct"),
+            (planes(slab), "direct"),
             ((2, 2, count) + tile, "direct"), ((size, 2 * width) + tile, "direct"),
         ],
         [
@@ -946,8 +974,13 @@
     mine, theirs = chain(lax.all_to_all(slots, "depth", 0, 0), next_full)
     (scaled,) = kernel_call(
         scale_kernel,
-        [(new_residual, "direct"), (pack, "direct"), (near_media, "direct")],
+        [
+            (plan, "smem"), (new_residual, "direct"), (new_field, "direct"),
+            (new_near, "direct"), (pack, "direct"), (near_media, "direct"),
+            (sources, "direct"),
+        ],
         [(planes(slab + 2 * (DEEP - 4)), "direct")],
+        [Field.shape(count, DEEP - 2, tile)],
         cost=4_000_000, name="scale", limit=4,
     )
     (out,) = kernel_call(

time: 54.6 us -> 54.6 us (level)
  transfers between devices with their start and end apart: 4 -> 4, of which waited for: 3 -> 3; matrix products, arithmetic and copies ran while one was open for 0% -> 0% of each run, Pallas kernels for 7% -> 8%
where the time goes in v11:
time: 54.6 us; the launch traced here: 54.4 us
  blocking collectives  30.6 us (56%)
  Pallas kernels  16.4 us (30%)
  starting transfers between devices  5.3 us (10%)
  waiting for transfers between devices  1.97 us (4%)
    all_to_all x1, blocking collectives, local(): first_got = lax.all_to_all(slots, 'depth', 0, 0)  17.7 us
    pallas_call x9, Pallas kernels, kernel_call(): pl.pallas_call(kernel, out_shape=tuple((jax.ShapeDtypeStruct(s, jnp.float...  16.4 us
    all_to_all x1, blocking collectives, local(): mine, theirs = chain(lax.all_to_all(slots, 'depth', 0, 0), next_full)  13 us
    ppermute x1, starting transfers between devices, local(): got_even = lax.ppermute(for_even, 'depth', even_pairs)  4.38 us
  transfers between devices with their start and end apart: 4, of which 3 were waited for; matrix products, arithmetic and copies ran while one was open for 0% of the time, Pallas kernels for 8%

profile of v11, /device:TPU:0, one launch (start us, length us, event | category | flops | bytes accessed | tf_op | source)
XLA Modules:
  0.0 54.4 jit_solution(16383323266077753187)
XLA Ops:
  0.0 0.0 copy-start
  0.0 1.1 %pack.1 = (f32[50,8,128]{2,1,0:T(8,128)S(1)}, f32[12,8,128]{2,1,0:T(8,128)S(1)}) custom-call(f32[8]{0:T(128)} %refs_0_.4, s32[128]{0:T(128)} %refs_1_.2, f32[1,8,128]{2,1,0:T(8,128)} %refs_2_.2, s32[1,8,128]{2,1,0:T(8,128)} %refs_3_.3, f32[2,4,64,8,128]{4,3,2,1,0:T(8,128)} %refs_12_.1), custom_call_target="tpu_custom_call" | custom-call | flops 1000000 | bytes 4194304 | tf_op jit(solution)/shard_map/pack/pallas_call | solution.py:101
  1.2 0.0 copy-start.1
  1.2 0.7 %collective-permute-start.1 = (f32[50,8,128]{2,1,0:T(8,128)S(1)}, f32[50,8,128]{2,1,0:T(8,128)S(1)}, u32[]{:S(2)}, u32[]{:S(2)}) collective-permute-start(f32[50,8,128]{2,1,0:T(8,128)S(1)} %get-tuple-element.29), channel_id=1, source_target_pairs={{1,2},{3,4},{5,6},{7,8},{9,10},{11,12},{13,14},{2,1},{4,3},{6,5},{... | collective-permute-start | bytes 614408 | tf_op jit(solution)/shard_map/ppermute | solution.py:900
  1.9 0.0 copy-done
  1.9 2.7 %start.1 = (f32[2,4,64,8,128]{4,3,2,1,0:T(8,128)S(1)}, f32[30,8,128]{2,1,0:T(8,128)S(1)}, f32[65,2,8,128]{3,2,1,0:T(8,128)S(1)}, f32[50,8,128]{2,1,0:T(8,128)S(1)}) custom-call(s32[4]{0:T(128)} %refs_0_.7, f32[2,4,8,128]{3,2,1,0:T(8,128)} %refs_6_.1, f32[12,8,128]{2,1,0:T(8,128)S(1)} %get-tuple-element.27.refs_2_, f32[2,4,64,8,128]{4,3,2,1,0:T(8,128)S(1)} %copy-done), custom_call_target="tpu_custom_call" | custom-call | flops 20000000 | bytes 4194304 | tf_op jit(solution)/shard_map/start/pallas_call | solution.py:101
  4.6 4.4 %collective-permute-start = (f32[50,8,128]{2,1,0:T(8,128)S(1)}, f32[50,8,128]{2,1,0:T(8,128)S(1)}, u32[]{:S(2)}, u32[]{:S(2)}) collective-permute-start(f32[50,8,128]{2,1,0:T(8,128)S(1)} %get-tuple-element.28), channel_id=1, source_target_pairs={{0,1},{1,0},{2,3},{3,2},{4,5},{5,4},{6,7},{7,6},{8,9},{9,8},{10,11... | collective-permute-start | bytes 614408 | tf_op jit(solution)/shard_map/ppermute | solution.py:916
  8.9 0.0 collective-permute-done.1.refs_1_
  8.9 1.1 %collective-permute-done.refs_0_ = f32[50,8,128]{2,1,0:T(8,128)S(1)} collective-permute-done((f32[50,8,128]{2,1,0:T(8,128)S(1)}, f32[50,8,128]{2,1,0:T(8,128)S(1)}, u32[]{:S(2)}, u32[]{:S(2)}) %collective-permute-start) | collective-permute-done | bytes 204832 | tf_op jit(solution)/shard_map/ppermute | solution.py:916
  10.0 0.1 arrange.1
  10.1 17.7 %all_to_all.10.refs_0_.refs_1_ = f32[16,5,8,128]{3,2,1,0:T(8,128)S(1)} all-to-all(f32[16,5,8,128]{3,2,1,0:T(8,128)S(1)} %get-tuple-element.31), channel_id=1, replica_groups=mesh['groups'=2,'depth'=16] {'depth'}, dimensions={0} | all-to-all | bytes 655360 | tf_op jit(solution)/shard_map/all_to_all | solution.py:927
  27.8 0.1 chain.2
  27.9 0.2 collective-permute-start.2
  28.1 0.0 copy-done.1
  28.1 0.7 %prepare.1 = (f32[2,2,4,5,8,128]{5,4,3,2,1,0:T(8,128)S(1)}, f32[2,10,8,128]{3,2,1,0:T(8,128)S(1)}, f32[2,2,5,2,8,128]{5,4,3,2,1,0:T(8,128)S(1)}) custom-call(s32[4]{0:T(128)} %refs_0_.7, f32[2,2,4,6,8,128]{5,4,3,2,1,0:T(8,128)S(1)} %get-tuple-element.35.refs_1_.refs_8_, f32[2,3,8,128]{3,2,1,0:T(8,128)S(1)} %get-tuple-element.36.refs_2_, ...), custom_call_target="tpu_custom_call" | custom-call | flops 4000000 | bytes 4194304 | tf_op jit(solution)/shard_map/prepare/pallas_call | solution.py:101
  28.8 0.4 collective-permute-done.2.refs_1_
  29.2 6.1 %middle.1 = (f32[2,4,64,8,128]{4,3,2,1,0:T(8,128)S(1)}, f32[2,2,4,3,8,128]{5,4,3,2,1,0:T(8,128)S(1)}, f32[2,4,64,8,128]{4,3,2,1,0:T(8,128)S(1)}, f32[2,2,4,8,128]{4,3,2,1,0:T(8,128)S(1)}, f32[16,4,8,128]{3,2,1,0:T(8,128)S(1)}) custom-call(f32[4,2,2,8,128]{4,3,2,1,0:T(8,128)S(1)} %get-tuple-element.33.refs_0_, ...), custom_call_target="tpu_custom_call" | custom-call | flops 80000000 | bytes 4194304 | tf_op jit(solution)/shard_map/middle/pallas_call | solution.py:101
  35.3 13.0 %all_to_all.11.refs_0_ = f32[16,4,8,128]{3,2,1,0:T(8,128)S(1)} all-to-all(f32[16,4,8,128]{3,2,1,0:T(8,128)S(1)} %get-tuple-element.42), channel_id=1, replica_groups=mesh['groups'=2,'depth'=16] {'depth'}, dimensions={0} | all-to-all | bytes 524288 | tf_op jit(solution)/shard_map/all_to_all | solution.py:974
  48.3 0.1 chain.3
  48.4 0.1 collective-permute-start.3
  48.5 0.7 %scale.1.refs_7_ = f32[2,4,68,8,128]{4,3,2,1,0:T(8,128)S(1)} custom-call(s32[4]{0:T(128)} %refs_0_.7, f32[2,4,64,8,128]{4,3,2,1,0:T(8,128)S(1)} %get-tuple-element.46.refs_1_, f32[2,4,64,8,128]{4,3,2,1,0:T(8,128)S(1)} %get-tuple-element.47.refs_2_.refs_8_, f32[2,2,4,3,8,128]{5,4,3,2,1,0:T(8,128)S(1)} %get-tuple-element.48.refs_3_, ...), custom_call_target="tpu_custom_call" | custom-call | flops 4000000 | bytes 4194304 | tf_op jit(solution)/shard_map/scale/pallas_call | solution.py:101
  49.3 0.5 collective-permute-done.3.refs_1_
  49.8 4.6 %final.1 = f32[2,4,64,8,128]{4,3,2,1,0:T(8,128)} custom-call(f32[4,2,2,8,128]{4,3,2,1,0:T(8,128)S(1)} %get-tuple-element.44.refs_0_, f32[4,2,2,8,128]{4,3,2,1,0:T(8,128)S(1)} %collective-permute-done.3.refs_1_, f32[2,2,4,8,128]{4,3,2,1,0:T(8,128)S(1)} %get-tuple-element.43.refs_2_, f32[30,8,128]{2,1,0:T(8,128)S(1)} %get-tuple-element.30.refs_2_.refs_5_.refs_4_.refs_3_, ...), custom_call_target="tpu_custom_call" | custom-call | flops 60000000 | bytes 4194304 | tf_op jit(solution)/shard_map/final/pallas_call | solution.py:101
Async XLA Ops:
  0.0 1.9 %copy-start = (f32[2,4,64,8,128]{4,3,2,1,0:T(8,128)S(1)}, f32[2,4,64,8,128]{4,3,2,1,0:T(8,128)}, u32[]{:S(2)}) copy-start(f32[2,4,64,8,128]{4,3,2,1,0:T(8,128)} %refs_12_.1) | copy-start | bytes 6291460
  1.2 26.9 %copy-start.1 = (f32[2,4,8,128]{3,2,1,0:T(8,128)S(1)}, f32[2,4,8,128]{3,2,1,0:T(8,128)}, u32[]{:S(2)}) copy-start(f32[2,4,8,128]{3,2,1,0:T(8,128)} %refs_6_.1) | copy-start | bytes 98308
  1.2 7.8 %collective-permute-start.1 = (f32[50,8,128]{2,1,0:T(8,128)S(1)}, f32[50,8,128]{2,1,0:T(8,128)S(1)}, u32[]{:S(2)}, u32[]{:S(2)}) collective-permute-start(f32[50,8,128]{2,1,0:T(8,128)S(1)} %get-tuple-element.29), channel_id=1, source_target_pairs={{1,2},{3,4},{5,6},{7,8},{9,10},{11,12},{13,14},{2,1},{4,3},{6,5},{... | collective-permute-start | bytes 614408 | tf_op jit(solution)/shard_map/ppermute | solution.py:900
  4.6 5.5 %collective-permute-start = (f32[50,8,128]{2,1,0:T(8,128)S(1)}, f32[50,8,128]{2,1,0:T(8,128)S(1)}, u32[]{:S(2)}, u32[]{:S(2)}) collective-permute-start(f32[50,8,128]{2,1,0:T(8,128)S(1)} %get-tuple-element.28), channel_id=1, source_target_pairs={{0,1},{1,0},{2,3},{3,2},{4,5},{5,4},{6,7},{7,6},{8,9},{9,8},{10,11... | collective-permute-start | bytes 614408 | tf_op jit(solution)/shard_map/ppermute | solution.py:916
  27.9 1.3 %collective-permute-start.2 = (f32[4,2,2,8,128]{4,3,2,1,0:T(8,128)S(1)}, f32[4,2,2,8,128]{4,3,2,1,0:T(8,128)S(1)}, u32[]{:S(2)}, u32[]{:S(2)}) collective-permute-start(f32[4,2,2,8,128]{4,3,2,1,0:T(8,128)S(1)} %get-tuple-element.34), channel_id=1, source_target_pairs={{0,1},{1,0},{2,3},{3,2},{4,5},{5,4},{6,7},{7,6},{8,9},{9,8},{10,11... | collective-permute-start | bytes 196616 | tf_op jit(solution)/shard_map/ppermute | solution.py:949
  48.4 1.3 %collective-permute-start.3 = (f32[4,2,2,8,128]{4,3,2,1,0:T(8,128)S(1)}, f32[4,2,2,8,128]{4,3,2,1,0:T(8,128)S(1)}, u32[]{:S(2)}, u32[]{:S(2)}) collective-permute-start(f32[4,2,2,8,128]{4,3,2,1,0:T(8,128)S(1)} %get-tuple-element.45), channel_id=1, source_target_pairs={{0,1},{1,0},{2,3},{3,2},{4,5},{5,4},{6,7},{7,6},{8,9},{9,8},{10,11... | collective-permute-start | bytes 196616 | tf_op jit(solution)/shard_map/ppermute | solution.py:949

commit v12 on v11

--- a/solution.py
+++ b/solution.py
@@ -14,7 +14,7 @@
 keep = 1.0 - relax_weight
 
 DEEP = 6
-UNROLL = 4
+UNROLL = 8
 LAG = UNROLL + 1
 
 
@@ -655,11 +655,14 @@
                 carry = run(i, t * UNROLL + offsets[i] + u, carry)
         return carry
 
-    first = trips // 2
-    carry = lax.fori_loop(0, first, trip, carry)
-    halfway(0, [first * UNROLL + o for o in offsets])
+    first = 0
+    if halfway is not None:
+        first = trips // 2
+        carry = lax.fori_loop(0, first, trip, carry)
+        halfway(0, [first * UNROLL + o for o in offsets])
     carry = lax.fori_loop(first, trips, trip, carry)
-    halfway(1, [trips * UNROLL + o for o in offsets])
+    if halfway is not None:
+        halfway(1, [trips * UNROLL + o for o in offsets])
     for i, stage in enumerate(stages):
         carry = own(i, trips * UNROLL + offsets[i], slab, carry)
         if i:
@@ -784,7 +787,7 @@
     nothing = lambda: None
     stages.append(Stage(nothing, inside, nothing))
     zero = jnp.zeros((count,) + tile, jnp.float32)
-    carry = pipeline(stages, slab, ((zero, zero), (zero, zero)), lambda i, reached: None)
+    carry = pipeline(stages, slab, ((zero, zero), (zero, zero)), None)
     for way in range(2):
         for part in range(2):
             next_full[way, part] = carry[way][part]

time: 54.6 us -> 54 us (0.989)
  Pallas kernels: 16.4 us -> 15.3 us
    pallas_call x9, Pallas kernels: 16.4 us -> 15.3 us  [kernel_call(): pl.pallas_call(kernel, out_shape=tuple((jax.ShapeDtypeStruct(s, jnp.float...]
  transfers between devices with their start and end apart: 4 -> 4, of which waited for: 3 -> 3; matrix products, arithmetic and copies ran while one was open for 0% -> 0% of each run, Pallas kernels for 8% -> 7%
where the time goes in v12:
time: 54 us; the launch traced here: 53.8 us
  blocking collectives  31.1 us (58%)
  Pallas kernels  15.3 us (28%)
  starting transfers between devices  5.29 us (10%)
  waiting for transfers between devices  1.97 us (4%)
    all_to_all x1, blocking collectives, local(): first_got = lax.all_to_all(slots, 'depth', 0, 0)  18.2 us
    pallas_call x9, Pallas kernels, kernel_call(): pl.pallas_call(kernel, out_shape=tuple((jax.ShapeDtypeStruct(s, jnp.float...  15.3 us
    all_to_all x1, blocking collectives, local(): mine, theirs = chain(lax.all_to_all(slots, 'depth', 0, 0), next_full)  13 us
    ppermute x1, starting transfers between devices, local(): got_even = lax.ppermute(for_even, 'depth', even_pairs)  4.37 us
  transfers between devices with their start and end apart: 4, of which 3 were waited for; matrix products, arithmetic and copies ran while one was open for 0% of the time, Pallas kernels for 7%

profile of v12, /device:TPU:0, one launch (start us, length us, event | category | flops | bytes accessed | tf_op | source)
XLA Modules:
  0.0 53.8 jit_solution(4236453550614153173)
XLA Ops:
  0.0 0.0 copy-start
  0.0 1.1 %pack.1 = (f32[50,8,128]{2,1,0:T(8,128)S(1)}, f32[12,8,128]{2,1,0:T(8,128)S(1)}) custom-call(f32[8]{0:T(128)} %refs_0_.4, s32[128]{0:T(128)} %refs_1_.2, f32[1,8,128]{2,1,0:T(8,128)} %refs_2_.2, s32[1,8,128]{2,1,0:T(8,128)} %refs_3_.3, f32[2,4,64,8,128]{4,3,2,1,0:T(8,128)} %refs_12_.1), custom_call_target="tpu_custom_call" | custom-call | flops 1000000 | bytes 4194304 | tf_op jit(solution)/shard_map/pack/pallas_call | solution.py:101
  1.2 0.0 copy-start.1
  1.2 0.7 %collective-permute-start.1 = (f32[50,8,128]{2,1,0:T(8,128)S(1)}, f32[50,8,128]{2,1,0:T(8,128)S(1)}, u32[]{:S(2)}, u32[]{:S(2)}) collective-permute-start(f32[50,8,128]{2,1,0:T(8,128)S(1)} %get-tuple-element.29), channel_id=1, source_target_pairs={{1,2},{3,4},{5,6},{7,8},{9,10},{11,12},{13,14},{2,1},{4,3},{6,5},{... | collective-permute-start | bytes 614408 | tf_op jit(solution)/shard_map/ppermute | solution.py:903
  1.9 0.0 copy-done
  1.9 2.2 %start.1 = (f32[2,4,64,8,128]{4,3,2,1,0:T(8,128)S(1)}, f32[30,8,128]{2,1,0:T(8,128)S(1)}, f32[65,2,8,128]{3,2,1,0:T(8,128)S(1)}, f32[50,8,128]{2,1,0:T(8,128)S(1)}) custom-call(s32[4]{0:T(128)} %refs_0_.7, f32[2,4,8,128]{3,2,1,0:T(8,128)} %refs_6_.1, f32[12,8,128]{2,1,0:T(8,128)S(1)} %get-tuple-element.27.refs_2_, f32[2,4,64,8,128]{4,3,2,1,0:T(8,128)S(1)} %copy-done), custom_call_target="tpu_custom_call" | custom-call | flops 20000000 | bytes 4194304 | tf_op jit(solution)/shard_map/start/pallas_call | solution.py:101
  4.1 4.4 %collective-permute-start = (f32[50,8,128]{2,1,0:T(8,128)S(1)}, f32[50,8,128]{2,1,0:T(8,128)S(1)}, u32[]{:S(2)}, u32[]{:S(2)}) collective-permute-start(f32[50,8,128]{2,1,0:T(8,128)S(1)} %get-tuple-element.28), channel_id=1, source_target_pairs={{0,1},{1,0},{2,3},{3,2},{4,5},{5,4},{6,7},{7,6},{8,9},{9,8},{10,11... | collective-permute-start | bytes 614408 | tf_op jit(solution)/shard_map/ppermute | solution.py:919
  8.5 0.0 collective-permute-done.1.refs_1_
  8.5 1.1 %collective-permute-done.refs_0_ = f32[50,8,128]{2,1,0:T(8,128)S(1)} collective-permute-done((f32[50,8,128]{2,1,0:T(8,128)S(1)}, f32[50,8,128]{2,1,0:T(8,128)S(1)}, u32[]{:S(2)}, u32[]{:S(2)}) %collective-permute-start) | collective-permute-done | bytes 204832 | tf_op jit(solution)/shard_map/ppermute | solution.py:919
  9.5 0.1 arrange.1
  9.6 18.2 %all_to_all.10.refs_0_.refs_1_ = f32[16,5,8,128]{3,2,1,0:T(8,128)S(1)} all-to-all(f32[16,5,8,128]{3,2,1,0:T(8,128)S(1)} %get-tuple-element.31), channel_id=1, replica_groups=mesh['groups'=2,'depth'=16] {'depth'}, dimensions={0} | all-to-all | bytes 655360 | tf_op jit(solution)/shard_map/all_to_all | solution.py:930
  27.8 0.1 chain.2
  27.9 0.2 collective-permute-start.2
  28.1 0.0 copy-done.1
  28.1 0.7 %prepare.1 = (f32[2,2,4,5,8,128]{5,4,3,2,1,0:T(8,128)S(1)}, f32[2,10,8,128]{3,2,1,0:T(8,128)S(1)}, f32[2,2,5,2,8,128]{5,4,3,2,1,0:T(8,128)S(1)}) custom-call(s32[4]{0:T(128)} %refs_0_.7, f32[2,2,4,6,8,128]{5,4,3,2,1,0:T(8,128)S(1)} %get-tuple-element.35.refs_1_.refs_8_, f32[2,3,8,128]{3,2,1,0:T(8,128)S(1)} %get-tuple-element.36.refs_2_, ...), custom_call_target="tpu_custom_call" | custom-call | flops 4000000 | bytes 4194304 | tf_op jit(solution)/shard_map/prepare/pallas_call | solution.py:101
  28.8 0.4 collective-permute-done.2.refs_1_
  29.2 5.7 %middle.1 = (f32[2,4,64,8,128]{4,3,2,1,0:T(8,128)S(1)}, f32[2,2,4,3,8,128]{5,4,3,2,1,0:T(8,128)S(1)}, f32[2,4,64,8,128]{4,3,2,1,0:T(8,128)S(1)}, f32[2,2,4,8,128]{4,3,2,1,0:T(8,128)S(1)}, f32[16,4,8,128]{3,2,1,0:T(8,128)S(1)}) custom-call(f32[4,2,2,8,128]{4,3,2,1,0:T(8,128)S(1)} %get-tuple-element.33.refs_0_, ...), custom_call_target="tpu_custom_call" | custom-call | flops 80000000 | bytes 4194304 | tf_op jit(solution)/shard_map/middle/pallas_call | solution.py:101
  34.9 13.0 %all_to_all.11.refs_0_ = f32[16,4,8,128]{3,2,1,0:T(8,128)S(1)} all-to-all(f32[16,4,8,128]{3,2,1,0:T(8,128)S(1)} %get-tuple-element.42), channel_id=1, replica_groups=mesh['groups'=2,'depth'=16] {'depth'}, dimensions={0} | all-to-all | bytes 524288 | tf_op jit(solution)/shard_map/all_to_all | solution.py:977
  47.9 0.1 chain.3
  48.0 0.1 collective-permute-start.3
  48.1 0.7 %scale.1.refs_7_ = f32[2,4,68,8,128]{4,3,2,1,0:T(8,128)S(1)} custom-call(s32[4]{0:T(128)} %refs_0_.7, f32[2,4,64,8,128]{4,3,2,1,0:T(8,128)S(1)} %get-tuple-element.46.refs_1_, f32[2,4,64,8,128]{4,3,2,1,0:T(8,128)S(1)} %get-tuple-element.47.refs_2_.refs_8_, f32[2,2,4,3,8,128]{5,4,3,2,1,0:T(8,128)S(1)} %get-tuple-element.48.refs_3_, ...), custom_call_target="tpu_custom_call" | custom-call | flops 4000000 | bytes 4194304 | tf_op jit(solution)/shard_map/scale/pallas_call | solution.py:101
  48.9 0.5 collective-permute-done.3.refs_1_
  49.4 4.4 %final.1 = f32[2,4,64,8,128]{4,3,2,1,0:T(8,128)} custom-call(f32[4,2,2,8,128]{4,3,2,1,0:T(8,128)S(1)} %get-tuple-element.44.refs_0_, f32[4,2,2,8,128]{4,3,2,1,0:T(8,128)S(1)} %collective-permute-done.3.refs_1_, f32[2,2,4,8,128]{4,3,2,1,0:T(8,128)S(1)} %get-tuple-element.43.refs_2_, f32[30,8,128]{2,1,0:T(8,128)S(1)} %get-tuple-element.30.refs_2_.refs_5_.refs_4_.refs_3_, ...), custom_call_target="tpu_custom_call" | custom-call | flops 60000000 | bytes 4194304 | tf_op jit(solution)/shard_map/final/pallas_call | solution.py:101
Async XLA Ops:
  0.0 1.9 %copy-start = (f32[2,4,64,8,128]{4,3,2,1,0:T(8,128)S(1)}, f32[2,4,64,8,128]{4,3,2,1,0:T(8,128)}, u32[]{:S(2)}) copy-start(f32[2,4,64,8,128]{4,3,2,1,0:T(8,128)} %refs_12_.1) | copy-start | bytes 6291460
  1.2 26.9 %copy-start.1 = (f32[2,4,8,128]{3,2,1,0:T(8,128)S(1)}, f32[2,4,8,128]{3,2,1,0:T(8,128)}, u32[]{:S(2)}) copy-start(f32[2,4,8,128]{3,2,1,0:T(8,128)} %refs_6_.1) | copy-start | bytes 98308
  1.2 7.3 %collective-permute-start.1 = (f32[50,8,128]{2,1,0:T(8,128)S(1)}, f32[50,8,128]{2,1,0:T(8,128)S(1)}, u32[]{:S(2)}, u32[]{:S(2)}) collective-permute-start(f32[50,8,128]{2,1,0:T(8,128)S(1)} %get-tuple-element.29), channel_id=1, source_target_pairs={{1,2},{3,4},{5,6},{7,8},{9,10},{11,12},{13,14},{2,1},{4,3},{6,5},{... | collective-permute-start | bytes 614408 | tf_op jit(solution)/shard_map/ppermute | solution.py:903
  4.1 5.5 %collective-permute-start = (f32[50,8,128]{2,1,0:T(8,128)S(1)}, f32[50,8,128]{2,1,0:T(8,128)S(1)}, u32[]{:S(2)}, u32[]{:S(2)}) collective-permute-start(f32[50,8,128]{2,1,0:T(8,128)S(1)} %get-tuple-element.28), channel_id=1, source_target_pairs={{0,1},{1,0},{2,3},{3,2},{4,5},{5,4},{6,7},{7,6},{8,9},{9,8},{10,11... | collective-permute-start | bytes 614408 | tf_op jit(solution)/shard_map/ppermute | solution.py:919
  27.9 1.3 %collective-permute-start.2 = (f32[4,2,2,8,128]{4,3,2,1,0:T(8,128)S(1)}, f32[4,2,2,8,128]{4,3,2,1,0:T(8,128)S(1)}, u32[]{:S(2)}, u32[]{:S(2)}) collective-permute-start(f32[4,2,2,8,128]{4,3,2,1,0:T(8,128)S(1)} %get-tuple-element.34), channel_id=1, source_target_pairs={{0,1},{1,0},{2,3},{3,2},{4,5},{5,4},{6,7},{7,6},{8,9},{9,8},{10,11... | collective-permute-start | bytes 196616 | tf_op jit(solution)/shard_map/ppermute | solution.py:952
  48.0 1.3 %collective-permute-start.3 = (f32[4,2,2,8,128]{4,3,2,1,0:T(8,128)S(1)}, f32[4,2,2,8,128]{4,3,2,1,0:T(8,128)S(1)}, u32[]{:S(2)}, u32[]{:S(2)}) collective-permute-start(f32[4,2,2,8,128]{4,3,2,1,0:T(8,128)S(1)} %get-tuple-element.45), channel_id=1, source_target_pairs={{0,1},{1,0},{2,3},{3,2},{4,5},{5,4},{6,7},{7,6},{8,9},{9,8},{10,11... | collective-permute-start | bytes 196616 | tf_op jit(solution)/shard_map/ppermute | solution.py:952
